TPU v7x, 128 devices: a whole 4x4x4 slice. The times are simulated.
128 devices in a mesh: gx: 8 (over z, core), gy: 16 (over y, x).
Axes of the slice: x: 4, y: 4, z: 4, core: 2. Of those that a mesh axis runs over, the one named last changes fastest.
Arguments:
- points: bfloat16 [1, 131072, 256], P(None, ('gx', 'gy')), may hold values from -16 to 16
- send_rows: int32 [1, 128, 768], P(None, ('gx', 'gy')), may hold values from 0 to 1023, as said below
- recv_slot: int32 [1, 131072], P(None, ('gx', 'gy')), may hold values from 0 to 1791, as said below
- norm1_gain: float32 [256], replicated, may hold values from 0.1 to 1.9
- qkv_weight: bfloat16 [256, 768], replicated, may hold values from -0.375 to 0.375
- proj_weight: bfloat16 [256, 256], replicated, may hold values from -0.375 to 0.375
- norm2_gain: float32 [256], replicated, may hold values from 0.1 to 1.9
- fc1_weight: bfloat16 [256, 1024], replicated, may hold values from -0.375 to 0.375
- fc2_weight: bfloat16 [1024, 256], replicated, may hold values from -0.1875 to 0.1875
- cotangent: bfloat16 [1, 131072, 256], P(None, ('gx', 'gy')), may hold values from -6 to 6
Outputs:
- block_out: bfloat16 [1, 131072, 256], P(None, ('gx', 'gy'))
- grad_points: bfloat16 [1, 131072, 256], P(None, ('gx', 'gy'))
Inputs may be any that keep to these rules, and one draw needn't show every extreme that they name: `send_rows`: for every event and source device a, the first L(a) of the slots toward a - 1 and the first R(a) of the slots toward a + 1 (devices mod 128) are used; the rows they name are distinct and, with the rows that recv_slot of device a lists as its own, cover all 1024 rows of a. Unused slots name arbitrary rows. L(a) and R(a) are at most 384, and in every event some device sends exactly 384 points to its next device. `recv_slot`: for every event and destination device d, the 1024 entries of d's block are distinct: a value s < 1024 names d's own z-order row s, 1024 + c the c-th slot of device d - 1 toward d, 1408 + c the c-th slot of device d + 1 toward d (mod 128); exactly the used slots appear, so that the Hilbert order is a permutation of the z-order in which every point moves at most one device along the curve.
All inputs are finite; a program needn't handle non-finite values.
Results may differ from a plain program's by a relative error of at most 0.0054.
Values may be sent and summed in bfloat16 or wider, within the bound.
No kernel may reach another device: no remote copies, remote signals or barrier semaphores. Data moves between devices by JAX's collectives and lax.ppermute only.
A program may use at most 128 MiB of HBM per device.

v0:
```python
import math

import jax
import jax.numpy as jnp
from jax import lax
from jax.sharding import PartitionSpec as P

H = 16
K = 1024
SHIFT = 512


epsilon = 1e-05


def with_halo(cells, sides, width):
    for axis, dim in sides:
        count = lax.axis_size(axis)
        head = lax.slice_in_dim(cells, 0, width, axis=dim)
        tail = lax.slice_in_dim(cells, cells.shape[dim] - width, cells.shape[dim], axis=dim)
        cells = jnp.concatenate(
            [
                lax.ppermute(tail, axis, [(i, (i + 1) % count) for i in range(count)]),
                cells,
                lax.ppermute(head, axis, [((i + 1) % count, i) for i in range(count)]),
            ],
            axis=dim,
        )
    return cells


def norm_rows(row_block, gain):
    row_mean = jnp.mean(row_block, axis=-1, keepdims=True)
    centered = row_block - row_mean
    spread = jnp.mean(centered * centered, axis=-1, keepdims=True)
    return centered * lax.rsqrt(spread + epsilon) * gain


def gelu_exact(values):
    return jax.nn.gelu(values, approximate=False)


def front(ordered, norm1_gain, qkv_weight):
    normed = norm_rows(ordered.astype(jnp.float32), norm1_gain).astype(jnp.bfloat16)
    return jnp.dot(normed, qkv_weight, preferred_element_type=jnp.float32).astype(jnp.bfloat16)


def rest_pass(ordered, attention, norm2_gain, proj_weight, fc1_weight, fc2_weight, cotangent):
    mixed_rows = ordered.astype(jnp.float32) + jnp.dot(
        attention, proj_weight, preferred_element_type=jnp.float32
    )
    normed_two, norm_back = jax.vjp(lambda row_block: norm_rows(row_block, norm2_gain), mixed_rows)
    hidden_pre = jnp.dot(
        normed_two.astype(jnp.bfloat16), fc1_weight, preferred_element_type=jnp.float32
    )
    activated, gelu_back = jax.vjp(gelu_exact, hidden_pre)
    activated_b = activated.astype(jnp.bfloat16)
    block_out = (
        mixed_rows + jnp.dot(activated_b, fc2_weight, preferred_element_type=jnp.float32)
    ).astype(jnp.bfloat16)
    grad_act = jnp.dot(cotangent, fc2_weight.T, preferred_element_type=jnp.float32)
    grad_pre = gelu_back(grad_act)[0].astype(jnp.bfloat16)
    grad_normed = jnp.dot(grad_pre, fc1_weight.T, preferred_element_type=jnp.float32)
    grad_mixed = cotangent.astype(jnp.float32) + norm_back(grad_normed)[0]
    grad_attention = jnp.dot(
        grad_mixed.astype(jnp.bfloat16), proj_weight.T, preferred_element_type=jnp.float32
    ).astype(jnp.bfloat16)
    return (block_out, grad_attention, grad_mixed)


def front_backward(ordered, grad_qkv, grad_mixed, norm1_gain, qkv_weight):
    unused, norm_back = jax.vjp(
        lambda row_block: norm_rows(row_block, norm1_gain), ordered.astype(jnp.float32)
    )
    grad_normed = jnp.dot(
        grad_qkv.astype(jnp.bfloat16), qkv_weight.T, preferred_element_type=jnp.float32
    )
    return (grad_mixed + norm_back(grad_normed)[0]).astype(jnp.bfloat16)


def split_heads(matrix, head_count):
    return matrix.reshape(matrix.shape[0], head_count, matrix.shape[1] // head_count)


def attend(queries, key_rows, value_rows, head_count):
    row_count = queries.shape[0]
    head_size = queries.shape[1] // head_count
    score_scale = 1.0 / math.sqrt(head_size)
    query_heads = split_heads(queries, head_count)
    key_heads = split_heads(key_rows, head_count)
    value_heads = split_heads(value_rows, head_count)
    scores = (
        jnp.einsum("qhd,khd->hqk", query_heads, key_heads, preferred_element_type=jnp.float32)
        * score_scale
    )
    weights = jnp.exp(scores)
    probs_b = (weights / jnp.sum(weights, axis=-1, keepdims=True)).astype(jnp.bfloat16)
    result = jnp.einsum("hqk,khd->qhd", probs_b, value_heads, preferred_element_type=jnp.float32)
    return result.reshape(row_count, -1).astype(jnp.bfloat16)


def attend_backward(queries, key_rows, value_rows, grad_out, head_count):
    row_count = queries.shape[0]
    window = key_rows.shape[0]
    head_size = queries.shape[1] // head_count
    score_scale = 1.0 / math.sqrt(head_size)
    query_heads = split_heads(queries, head_count)
    key_heads = split_heads(key_rows, head_count)
    value_heads = split_heads(value_rows, head_count)
    grad_heads = split_heads(grad_out, head_count)
    scores = (
        jnp.einsum("qhd,khd->hqk", query_heads, key_heads, preferred_element_type=jnp.float32)
        * score_scale
    )
    weights = jnp.exp(scores)
    probs_full = weights / jnp.sum(weights, axis=-1, keepdims=True)
    probs_b = probs_full.astype(jnp.bfloat16)
    grad_probs = jnp.einsum(
        "qhd,khd->hqk", grad_heads, value_heads, preferred_element_type=jnp.float32
    )
    grad_values = jnp.einsum(
        "hqk,qhd->khd", probs_b, grad_heads, preferred_element_type=jnp.float32
    )
    inner_sum = jnp.sum(probs_full * grad_probs, axis=-1, keepdims=True)
    grad_scores = (probs_full * (grad_probs - inner_sum) * score_scale).astype(jnp.bfloat16)
    grad_queries = jnp.einsum(
        "hqk,khd->qhd", grad_scores, key_heads, preferred_element_type=jnp.float32
    )
    grad_keys = jnp.einsum(
        "hqk,qhd->khd", grad_scores, query_heads, preferred_element_type=jnp.float32
    )
    return (
        grad_queries.reshape(row_count, -1),
        grad_keys.reshape(window, -1),
        grad_values.reshape(window, -1),
    )


def shards(
    points,
    send_rows,
    recv_slot,
    norm1_gain,
    qkv_weight,
    proj_weight,
    norm2_gain,
    fc1_weight,
    fc2_weight,
    cotangent,
):
    event_count, row_count, width = points.shape
    slot_count = send_rows.shape[2] // 2
    head_width = proj_weight.shape[0]
    block_count = 2 * row_count // K
    group_heads = math.gcd(H, 4)
    group_count = H // group_heads
    group_width = group_heads * (head_width // H)
    local_points = points[0]
    sender = send_rows[0, 0]
    outgoing = local_points[sender]
    arrived = with_halo(outgoing, ((("gx", "gy"), 0),), slot_count)
    pool = jnp.concatenate([local_points, arrived[:slot_count], arrived[-slot_count:]], axis=0)
    slot_index = recv_slot[0]
    ordered = pool[slot_index]
    qkv = front(ordered, norm1_gain, qkv_weight)
    queries = qkv[:, :head_width]
    key_values = qkv[:, head_width:]
    extended = with_halo(key_values, ((("gx", "gy"), 0),), SHIFT)

    def forward_block(block_index):
        query_rows = lax.dynamic_slice_in_dim(queries, block_index * SHIFT, SHIFT, 0)
        window_rows = lax.dynamic_slice_in_dim(extended, (block_index + 1) // 2 * K, K, 0)
        return attend(query_rows, window_rows[:, :head_width], window_rows[:, head_width:], H)

    block_ids = jnp.arange(block_count, dtype=jnp.int32)
    attention = lax.map(forward_block, block_ids).reshape(row_count, head_width)
    block_out, grad_attention, grad_mixed = rest_pass(
        ordered, attention, norm2_gain, proj_weight, fc1_weight, fc2_weight, cotangent[0]
    )

    def backward_block(block_index):
        query_rows = lax.dynamic_slice_in_dim(queries, block_index * SHIFT, SHIFT, 0)
        grad_rows = lax.dynamic_slice_in_dim(grad_attention, block_index * SHIFT, SHIFT, 0)
        window_rows = lax.dynamic_slice_in_dim(extended, (block_index + 1) // 2 * K, K, 0)
        key_rows = window_rows[:, :head_width]
        value_rows = window_rows[:, head_width:]

        def one_group(group_index):
            start = group_index * group_width

            def columns(matrix):
                return lax.dynamic_slice_in_dim(matrix, start, group_width, 1)

            return attend_backward(
                columns(query_rows),
                columns(key_rows),
                columns(value_rows),
                columns(grad_rows),
                group_heads,
            )

        group_q, group_k, group_v = lax.map(one_group, jnp.arange(group_count, dtype=jnp.int32))
        grad_q = jnp.transpose(group_q, (1, 0, 2)).reshape(SHIFT, head_width)
        grad_k = jnp.transpose(group_k, (1, 0, 2)).reshape(K, head_width)
        grad_v = jnp.transpose(group_v, (1, 0, 2)).reshape(K, head_width)
        return (grad_q, jnp.concatenate([grad_k, grad_v], axis=1))

    grad_q_blocks, grad_windows = lax.map(backward_block, block_ids)
    grad_queries = grad_q_blocks.reshape(row_count, head_width)
    zero_block = jnp.zeros((1, K, 2 * head_width), jnp.float32)
    paired = jnp.concatenate([zero_block, grad_windows, zero_block], axis=0)
    paired = paired.reshape(block_count // 2 + 1, 2, K, 2 * head_width).sum(axis=1)
    paired = paired.reshape((block_count // 2 + 1) * K, 2 * head_width)
    outgoing_grads = jnp.concatenate([paired[:SHIFT], paired[-SHIFT:]], axis=0)
    returned = with_halo(outgoing_grads.astype(jnp.bfloat16), ((("gx", "gy"), 0),), SHIFT).astype(
        outgoing_grads.dtype
    )
    grad_kv = paired[SHIFT : SHIFT + row_count]
    grad_kv = grad_kv.at[:SHIFT].add(returned[:SHIFT])
    grad_kv = grad_kv.at[row_count - SHIFT :].add(returned[-SHIFT:])
    grad_qkv = jnp.concatenate([grad_queries, grad_kv], axis=1)
    grad_ordered = front_backward(ordered, grad_qkv, grad_mixed, norm1_gain, qkv_weight)
    back_pool = (
        jnp.zeros((row_count + 2 * slot_count, width), jnp.bfloat16)
        .at[slot_index]
        .set(grad_ordered)
    )
    back_out = back_pool[row_count:]
    came_back = with_halo(back_out, ((("gx", "gy"), 0),), slot_count)
    returned_rows = jnp.concatenate([came_back[:slot_count], came_back[-slot_count:]], axis=0)
    grad_event = back_pool[:row_count].at[sender].add(returned_rows)
    outputs_list = [block_out]
    grads_list = [grad_event]
    return (jnp.stack(outputs_list), jnp.stack(grads_list))


def solution(mesh):
    in_specs = (
        P(None, ("gx", "gy"), None),
        P(None, ("gx", "gy"), None),
        P(None, ("gx", "gy")),
        P(),
        P(),
        P(),
        P(),
        P(),
        P(),
        P(None, ("gx", "gy"), None),
    )
    out_specs = (P(None, ("gx", "gy"), None), P(None, ("gx", "gy"), None))
    return jax.shard_map(shards, mesh=mesh, in_specs=in_specs, out_specs=out_specs, check_vma=False)
```

profile of v0, /device:TPU:0, one launch (start us, length us, event | category | flops | bytes accessed | tf_op | source)
XLA Modules:
  0.0 678.0 jit_solution(633502237953443395)
XLA Ops:
  5.3 8.3 %collective-permute-start.1 = (bf16[384,256]{1,0:T(8,128)(2,1)S(1)}, bf16[384,256]{1,0:T(8,128)(2,1)S(1)}, u32[]{:S(2)}, u32[]{:S(2)}) collective-permute-start(bf16[384,256]{1,0:T(8,128)(2,1)S(1)} %get-tuple-element.352), channel_id=1, source_target_pairs={{1,0},{2,1},{3,2},{4,3},{5,4},{6,5},{7,6},{8,7},{9,8},{10,9},{11,1... | collective-permute-start | bytes 589832 | tf_op jit(solution)/shard_map/ppermute | solution.py:25
  16.8 8.2 %collective-permute-done = bf16[384,256]{1,0:T(8,128)(2,1)S(1)} collective-permute-done((bf16[384,256]{1,0:T(8,128)(2,1)S(1)}, bf16[384,256]{1,0:T(8,128)(2,1)S(1)}, u32[]{:S(2)}, u32[]{:S(2)}) %collective-permute-start) | collective-permute-done | bytes 196640 | tf_op jit(solution)/shard_map/ppermute | solution.py:23
  42.4 7.7 %collective-permute-done.2 = bf16[512,512]{1,0:T(8,128)(2,1)} collective-permute-done((bf16[512,512]{1,0:T(8,128)(2,1)}, bf16[512,512]{1,0:T(8,128)(2,1)}, u32[]{:S(2)}, u32[]{:S(2)}) %collective-permute-start.2) | collective-permute-done | bytes 524320 | tf_op jit(solution)/shard_map/ppermute | solution.py:23
  56.0 63.4 %while.57 = (s32[]{:T(128)}, bf16[2,512,256]{2,1,0:T(8,128)(2,1)}, s32[2]{0:T(128)S(1)}, bf16[2048,512]{0,1:T(8,128)(2,1)S(1)}, bf16[1024,256]{0,1:T(8,128)(2,1)...) while((s32[]{:T(128)}, bf16[2,512,256]{2,1,0:T(8,128)(2,1)}, ...), condition=%wide.region_4.5_spmd, body=%wide.region_2.4_spmd.sunk | while | flops 578936832 | bytes 72417712 | solution.py:176
  59.8 13.6 %fusion.141 = (f32[16,512]{1,0:T(8,128)S(1)}, f32[16,512,1024]{2,1,0:T(8,128)}) fusion(bf16[512,16,16]{0,2,1:T(8,128)(2,1)S(1)} %bitcast.153, bf16[1024,16,16]{0,2,1:T(8,128)(2,1)S(1)} %bitcast.152), kind=kOutput, calls=%fused_computation.6.clone.1 | convolution fusion | flops 285204480 | bytes 34373632 | tf_op jit(solution)/shard_map/while/body/eval_jaxpr/qhd,khd->hqk/dot_general | solution.py:93
  73.5 13.4 %fusion.142 = bf16[16,16,512]{2,1,0:T(8,128)(2,1)S(1)} fusion(bf16[1024,16,16]{0,2,1:T(8,128)(2,1)} %bitcast.161, f32[16,512,1024]{2,1,0:T(8,128)} %get-tuple-element.507, f32[16,512]{1,0:T(8,128)S(1)} %get-tuple-element.508), kind=kOutput, calls=%fused_computation.8.clone.1 | convolution fusion | flops 293732352 | bytes 34373632 | tf_op jit(solution)/shard_map/while/body/eval_jaxpr/hqk,khd->qhd/dot_general | solution.py:98
  91.5 13.6 %fusion.141 = (f32[16,512]{1,0:T(8,128)S(1)}, f32[16,512,1024]{2,1,0:T(8,128)}) fusion(bf16[512,16,16]{0,2,1:T(8,128)(2,1)S(1)} %bitcast.153, bf16[1024,16,16]{0,2,1:T(8,128)(2,1)S(1)} %bitcast.152), kind=kOutput, calls=%fused_computation.6.clone.1 | convolution fusion | flops 285204480 | bytes 34373632 | tf_op jit(solution)/shard_map/while/body/eval_jaxpr/qhd,khd->hqk/dot_general | solution.py:93
  105.2 13.4 %fusion.142 = bf16[16,16,512]{2,1,0:T(8,128)(2,1)S(1)} fusion(bf16[1024,16,16]{0,2,1:T(8,128)(2,1)} %bitcast.161, f32[16,512,1024]{2,1,0:T(8,128)} %get-tuple-element.507, f32[16,512]{1,0:T(8,128)S(1)} %get-tuple-element.508), kind=kOutput, calls=%fused_computation.8.clone.1 | convolution fusion | flops 293732352 | bytes 34373632 | tf_op jit(solution)/shard_map/while/body/eval_jaxpr/hqk,khd->qhd/dot_general | solution.py:98
  121.2 11.1 %fusion.28 = (f32[1024,1024]{1,0:T(8,128)}, f32[1024,1024]{1,0:T(8,128)}) fusion(bf16[256,1024]{1,0:T(8,128)(2,1)S(1)} %copy-done, f32[1024,256]{0,1:T(8,128)S(1)} %get-tuple-element.354, f32[256]{0:T(256)S(1)} %copy-done.32, f32[1024]{0:T(1024)S(1)} %fusion.80, f32[1024]{0:T(1024)S(1)} %broadcast_multiply_fusion), kind=kOutput, calls=%fused_computation.44 | convolution fusion | flops 602931200 | bytes 9970688 | tf_op jit(solution)/shard_map/dot_general | solution.py:53
  132.3 7.5 %multiply_reduce_fusion.1 = (f32[1024]{0:T(1024)S(1)}, f32[1024,256]{0,1:T(8,128)}) fusion(f32[1024,256]{0,1:T(8,128)} %copy-done.8, f32[1024]{0:T(1024)S(1)} %broadcast_multiply_fusion, f32[256]{0:T(256)S(1)} %copy-done.32, bf16[256,1024]{1,0:T(8,128)(2,1)S(1)} %copy-done, f32[1024,1024]{1,0:T(8,128)} %get-tuple-element.355, ...), kind=kOutput, calls=%fused_computation.94 | convolution fusion | flops 1089469440 | bytes 12067840 | tf_op jit(solution)/shard_map/dot_general | solution.py:63
  143.8 476.7 %while.59 = (s32[]{:T(128)}, bf16[2,512,256]{2,1,0:T(8,128)(2,1)}, f32[2,1024,512]{1,2,0:T(8,128)}, s32[2]{0:T(128)S(1)}, bf16[1024,256]{0,1:T(8,128)(2,1)}, /*i...) while((s32[]{:T(128)}, bf16[2,512,256]{2,1,0:T(8,128)(2,1)}, ...), condition=%wide.region_14.15_spmd, body=%wide.region_9.0_spmd.sunk | while | flops 384307232 | bytes 87655400 | solution.py:208
  149.2 228.9 %while.60 = (s32[]{:T(128)}, bf16[4,512,64]{1,2,0:T(8,128)(2,1)S(1)}, f32[4,1024,64]{1,2,0:T(8,128)}, f32[4,1024,64]{1,2,0:T(8,128)}, s32[4]{0:T(128)S(1)}, /*in...) while((s32[]{:T(128)}, ...), condition=%wide.region_13.13_spmd, body=%wide.region_10.12_spmd.sunk | while | flops 383782912 | bytes 61964504 | solution.py:202
  161.6 21.2 %fusion.157 = bf16[4,16,512]{2,1,0:T(8,128)(2,1)S(1)} fusion(bf16[1024,4,16]{0,2,1:T(8,128)(2,1)S(1)} %bitcast.144, f32[4,512,1024]{2,1,0:T(8,128)} %fusion.155, f32[4,512,1024]{2,1,0:T(8,128)} %get-tuple-element.531, f32[4,512]{1,0:T(4,128)S(1)} %get-tuple-element.532), kind=kOutput, calls=%fused_computation.23.clone.1 | convolution fusion | flops 85986304 | bytes 16982016 | tf_op jit(solution)/shard_map/while/body/eval_jaxpr/while/body/eval_jaxpr/hqk,khd->qhd/dot_general | solution.py:126
  187.0 18.5 %fusion.159 = f32[4,16,1024]{2,1,0:T(8,128)S(1)} fusion(bf16[512,4,16]{0,2,1:T(8,128)(2,1)S(1)} %bitcast.149, f32[4,512,1024]{2,1,0:T(8,128)} %fusion.155, f32[4,512,1024]{2,1,0:T(8,128)} %get-tuple-element.531, f32[4,512]{1,0:T(4,128)S(1)} %get-tuple-element.532), kind=kOutput, calls=%fused_computation.22.clone.1 | convolution fusion | flops 85986304 | bytes 17113088 | tf_op jit(solution)/shard_map/while/body/eval_jaxpr/while/body/eval_jaxpr/hqk,qhd->khd/dot_general | solution.py:129
  218.8 21.2 %fusion.157 = bf16[4,16,512]{2,1,0:T(8,128)(2,1)S(1)} fusion(bf16[1024,4,16]{0,2,1:T(8,128)(2,1)S(1)} %bitcast.144, f32[4,512,1024]{2,1,0:T(8,128)} %fusion.155, f32[4,512,1024]{2,1,0:T(8,128)} %get-tuple-element.531, f32[4,512]{1,0:T(4,128)S(1)} %get-tuple-element.532), kind=kOutput, calls=%fused_computation.23.clone.1 | convolution fusion | flops 85986304 | bytes 16982016 | tf_op jit(solution)/shard_map/while/body/eval_jaxpr/while/body/eval_jaxpr/hqk,khd->qhd/dot_general | solution.py:126
  244.3 18.5 %fusion.159 = f32[4,16,1024]{2,1,0:T(8,128)S(1)} fusion(bf16[512,4,16]{0,2,1:T(8,128)(2,1)S(1)} %bitcast.149, f32[4,512,1024]{2,1,0:T(8,128)} %fusion.155, f32[4,512,1024]{2,1,0:T(8,128)} %get-tuple-element.531, f32[4,512]{1,0:T(4,128)S(1)} %get-tuple-element.532), kind=kOutput, calls=%fused_computation.22.clone.1 | convolution fusion | flops 85986304 | bytes 17113088 | tf_op jit(solution)/shard_map/while/body/eval_jaxpr/while/body/eval_jaxpr/hqk,qhd->khd/dot_general | solution.py:129
  276.0 21.2 %fusion.157 = bf16[4,16,512]{2,1,0:T(8,128)(2,1)S(1)} fusion(bf16[1024,4,16]{0,2,1:T(8,128)(2,1)S(1)} %bitcast.144, f32[4,512,1024]{2,1,0:T(8,128)} %fusion.155, f32[4,512,1024]{2,1,0:T(8,128)} %get-tuple-element.531, f32[4,512]{1,0:T(4,128)S(1)} %get-tuple-element.532), kind=kOutput, calls=%fused_computation.23.clone.1 | convolution fusion | flops 85986304 | bytes 16982016 | tf_op jit(solution)/shard_map/while/body/eval_jaxpr/while/body/eval_jaxpr/hqk,khd->qhd/dot_general | solution.py:126
  301.5 18.5 %fusion.159 = f32[4,16,1024]{2,1,0:T(8,128)S(1)} fusion(bf16[512,4,16]{0,2,1:T(8,128)(2,1)S(1)} %bitcast.149, f32[4,512,1024]{2,1,0:T(8,128)} %fusion.155, f32[4,512,1024]{2,1,0:T(8,128)} %get-tuple-element.531, f32[4,512]{1,0:T(4,128)S(1)} %get-tuple-element.532), kind=kOutput, calls=%fused_computation.22.clone.1 | convolution fusion | flops 85986304 | bytes 17113088 | tf_op jit(solution)/shard_map/while/body/eval_jaxpr/while/body/eval_jaxpr/hqk,qhd->khd/dot_general | solution.py:129
  333.2 21.2 %fusion.157 = bf16[4,16,512]{2,1,0:T(8,128)(2,1)S(1)} fusion(bf16[1024,4,16]{0,2,1:T(8,128)(2,1)S(1)} %bitcast.144, f32[4,512,1024]{2,1,0:T(8,128)} %fusion.155, f32[4,512,1024]{2,1,0:T(8,128)} %get-tuple-element.531, f32[4,512]{1,0:T(4,128)S(1)} %get-tuple-element.532), kind=kOutput, calls=%fused_computation.23.clone.1 | convolution fusion | flops 85986304 | bytes 16982016 | tf_op jit(solution)/shard_map/while/body/eval_jaxpr/while/body/eval_jaxpr/hqk,khd->qhd/dot_general | solution.py:126
  358.7 18.5 %fusion.159 = f32[4,16,1024]{2,1,0:T(8,128)S(1)} fusion(bf16[512,4,16]{0,2,1:T(8,128)(2,1)S(1)} %bitcast.149, f32[4,512,1024]{2,1,0:T(8,128)} %fusion.155, f32[4,512,1024]{2,1,0:T(8,128)} %get-tuple-element.531, f32[4,512]{1,0:T(4,128)S(1)} %get-tuple-element.532), kind=kOutput, calls=%fused_computation.22.clone.1 | convolution fusion | flops 85986304 | bytes 17113088 | tf_op jit(solution)/shard_map/while/body/eval_jaxpr/while/body/eval_jaxpr/hqk,qhd->khd/dot_general | solution.py:129
  387.5 228.9 %while.60 = (s32[]{:T(128)}, bf16[4,512,64]{1,2,0:T(8,128)(2,1)S(1)}, f32[4,1024,64]{1,2,0:T(8,128)}, f32[4,1024,64]{1,2,0:T(8,128)}, s32[4]{0:T(128)S(1)}, /*in...) while((s32[]{:T(128)}, ...), condition=%wide.region_13.13_spmd, body=%wide.region_10.12_spmd.sunk | while | flops 383782912 | bytes 61964504 | solution.py:202
  399.9 21.2 %fusion.157 = bf16[4,16,512]{2,1,0:T(8,128)(2,1)S(1)} fusion(bf16[1024,4,16]{0,2,1:T(8,128)(2,1)S(1)} %bitcast.144, f32[4,512,1024]{2,1,0:T(8,128)} %fusion.155, f32[4,512,1024]{2,1,0:T(8,128)} %get-tuple-element.531, f32[4,512]{1,0:T(4,128)S(1)} %get-tuple-element.532), kind=kOutput, calls=%fused_computation.23.clone.1 | convolution fusion | flops 85986304 | bytes 16982016 | tf_op jit(solution)/shard_map/while/body/eval_jaxpr/while/body/eval_jaxpr/hqk,khd->qhd/dot_general | solution.py:126
  425.4 18.5 %fusion.159 = f32[4,16,1024]{2,1,0:T(8,128)S(1)} fusion(bf16[512,4,16]{0,2,1:T(8,128)(2,1)S(1)} %bitcast.149, f32[4,512,1024]{2,1,0:T(8,128)} %fusion.155, f32[4,512,1024]{2,1,0:T(8,128)} %get-tuple-element.531, f32[4,512]{1,0:T(4,128)S(1)} %get-tuple-element.532), kind=kOutput, calls=%fused_computation.22.clone.1 | convolution fusion | flops 85986304 | bytes 17113088 | tf_op jit(solution)/shard_map/while/body/eval_jaxpr/while/body/eval_jaxpr/hqk,qhd->khd/dot_general | solution.py:129
  457.1 21.2 %fusion.157 = bf16[4,16,512]{2,1,0:T(8,128)(2,1)S(1)} fusion(bf16[1024,4,16]{0,2,1:T(8,128)(2,1)S(1)} %bitcast.144, f32[4,512,1024]{2,1,0:T(8,128)} %fusion.155, f32[4,512,1024]{2,1,0:T(8,128)} %get-tuple-element.531, f32[4,512]{1,0:T(4,128)S(1)} %get-tuple-element.532), kind=kOutput, calls=%fused_computation.23.clone.1 | convolution fusion | flops 85986304 | bytes 16982016 | tf_op jit(solution)/shard_map/while/body/eval_jaxpr/while/body/eval_jaxpr/hqk,khd->qhd/dot_general | solution.py:126
  482.6 18.5 %fusion.159 = f32[4,16,1024]{2,1,0:T(8,128)S(1)} fusion(bf16[512,4,16]{0,2,1:T(8,128)(2,1)S(1)} %bitcast.149, f32[4,512,1024]{2,1,0:T(8,128)} %fusion.155, f32[4,512,1024]{2,1,0:T(8,128)} %get-tuple-element.531, f32[4,512]{1,0:T(4,128)S(1)} %get-tuple-element.532), kind=kOutput, calls=%fused_computation.22.clone.1 | convolution fusion | flops 85986304 | bytes 17113088 | tf_op jit(solution)/shard_map/while/body/eval_jaxpr/while/body/eval_jaxpr/hqk,qhd->khd/dot_general | solution.py:129
  514.4 21.2 %fusion.157 = bf16[4,16,512]{2,1,0:T(8,128)(2,1)S(1)} fusion(bf16[1024,4,16]{0,2,1:T(8,128)(2,1)S(1)} %bitcast.144, f32[4,512,1024]{2,1,0:T(8,128)} %fusion.155, f32[4,512,1024]{2,1,0:T(8,128)} %get-tuple-element.531, f32[4,512]{1,0:T(4,128)S(1)} %get-tuple-element.532), kind=kOutput, calls=%fused_computation.23.clone.1 | convolution fusion | flops 85986304 | bytes 16982016 | tf_op jit(solution)/shard_map/while/body/eval_jaxpr/while/body/eval_jaxpr/hqk,khd->qhd/dot_general | solution.py:126
  539.8 18.5 %fusion.159 = f32[4,16,1024]{2,1,0:T(8,128)S(1)} fusion(bf16[512,4,16]{0,2,1:T(8,128)(2,1)S(1)} %bitcast.149, f32[4,512,1024]{2,1,0:T(8,128)} %fusion.155, f32[4,512,1024]{2,1,0:T(8,128)} %get-tuple-element.531, f32[4,512]{1,0:T(4,128)S(1)} %get-tuple-element.532), kind=kOutput, calls=%fused_computation.22.clone.1 | convolution fusion | flops 85986304 | bytes 17113088 | tf_op jit(solution)/shard_map/while/body/eval_jaxpr/while/body/eval_jaxpr/hqk,qhd->khd/dot_general | solution.py:129
  571.6 21.2 %fusion.157 = bf16[4,16,512]{2,1,0:T(8,128)(2,1)S(1)} fusion(bf16[1024,4,16]{0,2,1:T(8,128)(2,1)S(1)} %bitcast.144, f32[4,512,1024]{2,1,0:T(8,128)} %fusion.155, f32[4,512,1024]{2,1,0:T(8,128)} %get-tuple-element.531, f32[4,512]{1,0:T(4,128)S(1)} %get-tuple-element.532), kind=kOutput, calls=%fused_computation.23.clone.1 | convolution fusion | flops 85986304 | bytes 16982016 | tf_op jit(solution)/shard_map/while/body/eval_jaxpr/while/body/eval_jaxpr/hqk,khd->qhd/dot_general | solution.py:126
  597.0 18.5 %fusion.159 = f32[4,16,1024]{2,1,0:T(8,128)S(1)} fusion(bf16[512,4,16]{0,2,1:T(8,128)(2,1)S(1)} %bitcast.149, f32[4,512,1024]{2,1,0:T(8,128)} %fusion.155, f32[4,512,1024]{2,1,0:T(8,128)} %get-tuple-element.531, f32[4,512]{1,0:T(4,128)S(1)} %get-tuple-element.532), kind=kOutput, calls=%fused_computation.22.clone.1 | convolution fusion | flops 85986304 | bytes 17113088 | tf_op jit(solution)/shard_map/while/body/eval_jaxpr/while/body/eval_jaxpr/hqk,qhd->khd/dot_general | solution.py:129
  636.3 7.4 %collective-permute-done.5 = bf16[512,512]{1,0:T(8,128)(2,1)S(1)} collective-permute-done((bf16[512,512]{1,0:T(8,128)(2,1)S(1)}, bf16[512,512]{1,0:T(8,128)(2,1)S(1)}, u32[]{:S(2)}, u32[]{:S(2)}) %collective-permute-start.5) | collective-permute-done | bytes 524320 | tf_op jit(solution)/shard_map/ppermute | solution.py:25
  643.7 6.6 collective-permute-done.4
  670.4 6.5 scatter_custom_fusion.1
  (261 shorter events, 230.1 us)
Async XLA Ops:
  0.6 120.6 %copy-start = (bf16[256,1024]{1,0:T(8,128)(2,1)S(1)}, bf16[256,1024]{1,0:T(8,128)(2,1)}, u32[]{:S(2)}) copy-start(bf16[256,1024]{1,0:T(8,128)(2,1)} %param.27) | copy-start | bytes 1572868
  0.6 24.3 %copy-start.5 = (bf16[1,1024,256]{2,1,0:T(8,128)(2,1)S(1)}, bf16[1,1024,256]{2,1,0:T(8,128)(2,1)}, u32[]{:S(2)}) copy-start(bf16[1,1024,256]{2,1,0:T(8,128)(2,1)} %param.20) | copy-start | bytes 1572868
  0.7 13.0 %copy-start.28 = (s32[1,1024]{1,0:T(1,128)S(1)}, s32[1,1024]{1,0:T(1,128)}, u32[]{:S(2)}) copy-start(s32[1,1024]{1,0:T(1,128)} %param.22) | copy-start | bytes 12292
  5.3 11.5 %collective-permute-start.1 = (bf16[384,256]{1,0:T(8,128)(2,1)S(1)}, bf16[384,256]{1,0:T(8,128)(2,1)S(1)}, u32[]{:S(2)}, u32[]{:S(2)}) collective-permute-start(bf16[384,256]{1,0:T(8,128)(2,1)S(1)} %get-tuple-element.352), channel_id=1, source_target_pairs={{1,0},{2,1},{3,2},{4,3},{5,4},{6,5},{7,6},{8,7},{9,8},{10,9},{11,1... | collective-permute-start | bytes 589832 | tf_op jit(solution)/shard_map/ppermute | solution.py:25
  13.6 11.4 %collective-permute-start = (bf16[384,256]{1,0:T(8,128)(2,1)S(1)}, bf16[384,256]{1,0:T(8,128)(2,1)S(1)}, u32[]{:S(2)}, u32[]{:S(2)}) collective-permute-start(bf16[384,256]{1,0:T(8,128)(2,1)S(1)} %get-tuple-element.351), channel_id=1, source_target_pairs={{0,1},{1,2},{2,3},{3,4},{4,5},{5,6},{6,7},{7,8},{8,9},{9,10},{10,1... | collective-permute-start | bytes 589832 | tf_op jit(solution)/shard_map/ppermute | solution.py:23
  13.6 3.2 copy-start.27
  13.6 16.5 %copy-start.30 = (bf16[256,768]{1,0:T(8,128)(2,1)S(1)}, bf16[256,768]{1,0:T(8,128)(2,1)}, u32[]{:S(2)}) copy-start(bf16[256,768]{1,0:T(8,128)(2,1)} %param.24) | copy-start | bytes 1179652
  13.7 16.5 %copy-start.33 = (f32[256]{0:T(256)S(1)}, f32[256]{0:T(256)}, u32[]{:S(2)}) copy-start(f32[256]{0:T(256)} %param.23) | copy-start | bytes 3076
  29.0 5.4 copy-start.16
  29.2 7.3 %copy-start.6 = (bf16[1024,256]{0,1:T(8,128)(2,1)}, bf16[1024,256]{0,1:T(8,128)(2,1)S(1)}, u32[]{:S(2)}) copy-start(bf16[1024,256]{0,1:T(8,128)(2,1)S(1)} %copy.45) | copy-start | bytes 1572868
  31.9 10.4 %collective-permute-start.3 = (bf16[512,512]{1,0:T(8,128)(2,1)}, bf16[512,512]{1,0:T(8,128)(2,1)}, u32[]{:S(2)}, u32[]{:S(2)}) collective-permute-start(bf16[512,512]{1,0:T(8,128)(2,1)} %get-tuple-element.348), channel_id=1, source_target_pairs={{1,0},{2,1},{3,2},{4,3},{5,4},{6,5},{7,6},{8,7},{9,8},{10,9},{11,1... | collective-permute-start | bytes 1572872 | tf_op jit(solution)/shard_map/ppermute | solution.py:25
  31.9 18.2 %collective-permute-start.2 = (bf16[512,512]{1,0:T(8,128)(2,1)}, bf16[512,512]{1,0:T(8,128)(2,1)}, u32[]{:S(2)}, u32[]{:S(2)}) collective-permute-start(bf16[512,512]{1,0:T(8,128)(2,1)} %get-tuple-element.347), channel_id=1, source_target_pairs={{0,1},{1,2},{2,3},{3,4},{4,5},{5,6},{6,7},{7,8},{8,9},{9,10},{10,1... | collective-permute-start | bytes 1572872 | tf_op jit(solution)/shard_map/ppermute | solution.py:23
  56.0 63.5 %copy-start.15 = (bf16[256,256]{1,0:T(8,128)(2,1)S(1)}, bf16[256,256]{1,0:T(8,128)(2,1)}, u32[]{:S(2)}) copy-start(bf16[256,256]{1,0:T(8,128)(2,1)} %param.25) | copy-start | bytes 393220
  56.0 65.2 %copy-start.32 = (f32[256]{0:T(256)S(1)}, f32[256]{0:T(256)}, u32[]{:S(2)}) copy-start(f32[256]{0:T(256)} %param.26) | copy-start | bytes 3076
  121.0 11.3 %copy-start.8 = (f32[1024,256]{0,1:T(8,128)}, f32[1024,256]{0,1:T(8,128)S(1)}, u32[]{:S(2)}) copy-start(f32[1024,256]{0,1:T(8,128)S(1)} %get-tuple-element.354) | copy-start | bytes 3145732
  132.3 10.2 %copy-start.12 = (bf16[1,1024,256]{1,2,0:T(8,128)(2,1)S(1)}, bf16[1,1024,256]{1,2,0:T(8,128)(2,1)}, u32[]{:S(2)}) copy-start(bf16[1,1024,256]{1,2,0:T(8,128)(2,1)} %copy.50) | copy-start | bytes 1572868
  143.8 4.3 copy-start.35
  143.8 5.4 copy-start.2
  378.1 4.0 copy-start.3
  378.1 4.0 copy-start.36
  382.1 4.3 copy-start.35
  382.1 5.4 copy-start.2
  616.4 4.0 copy-start.3
  616.4 4.0 copy-start.36
  631.3 4.8 copy-start.4
  634.0 9.7 %collective-permute-start.5 = (bf16[512,512]{1,0:T(8,128)(2,1)S(1)}, bf16[512,512]{1,0:T(8,128)(2,1)S(1)}, u32[]{:S(2)}, u32[]{:S(2)}) collective-permute-start(bf16[512,512]{1,0:T(8,128)(2,1)S(1)} %get-tuple-element.346), channel_id=1, source_target_pairs={{1,0},{2,1},{3,2},{4,3},{5,4},{6,5},{7,6},{8,7},{9,8},{10,9},{11,1... | collective-permute-start | bytes 1572872 | tf_op jit(solution)/shard_map/ppermute | solution.py:25
  634.1 16.2 %collective-permute-start.4 = (bf16[512,512]{1,0:T(8,128)(2,1)S(1)}, bf16[512,512]{1,0:T(8,128)(2,1)S(1)}, u32[]{:S(2)}, u32[]{:S(2)}) collective-permute-start(bf16[512,512]{1,0:T(8,128)(2,1)S(1)} %get-tuple-element.345), channel_id=1, source_target_pairs={{0,1},{1,2},{2,3},{3,4},{4,5},{5,6},{6,7},{7,8},{8,9},{9,10},{10,1... | collective-permute-start | bytes 1572872 | tf_op jit(solution)/shard_map/ppermute | solution.py:23
  652.4 9.2 %copy-start.9 = (f32[1024,256]{0,1:T(8,128)S(1)}, f32[1024,256]{0,1:T(8,128)}, u32[]{:S(2)}) copy-start(f32[1024,256]{0,1:T(8,128)} %copy-done.8) | copy-start | bytes 3145732
  652.4 9.2 %copy-start.14 = (bf16[1024,256]{1,0:T(8,128)(2,1)S(1)}, bf16[1024,256]{1,0:T(8,128)(2,1)}, u32[]{:S(2)}) copy-start(bf16[1024,256]{1,0:T(8,128)(2,1)} %param.28) | copy-start | bytes 1572868
  659.6 7.3 %collective-permute-start.7 = (bf16[384,256]{1,0:T(8,128)(2,1)}, bf16[384,256]{1,0:T(8,128)(2,1)}, u32[]{:S(2)}, u32[]{:S(2)}) collective-permute-start(bf16[384,256]{1,0:T(8,128)(2,1)} %get-tuple-element.350), channel_id=1, source_target_pairs={{1,0},{2,1},{3,2},{4,3},{5,4},{6,5},{7,6},{8,7},{9,8},{10,9},{11,1... | collective-permute-start | bytes 589832 | tf_op jit(solution)/shard_map/ppermute | solution.py:25
  659.6 18.1 %copy-start.1 = (bf16[256,1024]{1,0:T(8,128)(2,1)S(1)}, bf16[256,1024]{1,0:T(8,128)(2,1)}, u32[]{:S(2)}) copy-start(bf16[256,1024]{1,0:T(8,128)(2,1)} %param.27) | copy-start | bytes 1572868
  659.6 10.8 %collective-permute-start.6 = (bf16[384,256]{1,0:T(8,128)(2,1)}, bf16[384,256]{1,0:T(8,128)(2,1)}, u32[]{:S(2)}, u32[]{:S(2)}) collective-permute-start(bf16[384,256]{1,0:T(8,128)(2,1)} %get-tuple-element.349), channel_id=1, source_target_pairs={{0,1},{1,2},{2,3},{3,4},{4,5},{5,6},{6,7},{7,8},{8,9},{9,10},{10,1... | collective-permute-start | bytes 589832 | tf_op jit(solution)/shard_map/ppermute | solution.py:23
  (17 other events, 21.2 us)
where the time goes:
time: 682 us; the launch traced here: 678 us
  matrix products  506 us (74%)
  local copies, waits for them, and re-layouts  75 us (11%)
  waiting for transfers between devices  41.4 us (6%)
  other arithmetic  27.9 us (4%)
  starting transfers between devices  14.9 us (2%)
  loops' own time  11.4 us (2%)
    dot_general x8, matrix products, attend_backward(): jnp.einsum('hqk,khd->qhd', grad_scores, key_heads, preferred_element_type...  169 us
    dot_general x8, matrix products, attend_backward(): jnp.einsum('hqk,qhd->khd', grad_scores, query_heads, preferred_element_ty...  148 us
    dot_general x8, matrix products, attend_backward(): jnp.einsum('qhd,khd->hqk', query_heads, key_heads, preferred_element_type...  37.2 us
    dot_general x8, matrix products, attend_backward(): jnp.einsum('qhd,khd->hqk', grad_heads, value_heads, preferred_element_typ...  36.1 us
    dot_general x8, matrix products, attend_backward(): jnp.einsum('hqk,qhd->khd', probs_b, grad_heads, preferred_element_type=jn...  34 us
    dot_general x2, matrix products, attend(): jnp.einsum('qhd,khd->hqk', query_heads, key_heads, preferred_element_type...  27.2 us
    dot_general x2, matrix products, attend(): jnp.einsum('hqk,khd->qhd', probs_b, value_heads, preferred_element_type=j...  26.8 us
    ppermute x4, waiting for transfers between devices, with_halo(): lax.ppermute(tail, axis, [(i, (i + 1) % count) for i in range(count)])  26 us
  transfers between devices with their start and end apart: 8, of which 7 were waited for; matrix products, arithmetic and copies ran while one was open for 1% of the time, Pallas kernels for 0%

commit v1 on v0

v1 whole, which is shorter than its diff:
```python
import functools
import math

import jax
import jax.numpy as jnp
from jax import lax
from jax.experimental import pallas as pl
from jax.experimental.pallas import tpu as pltpu
from jax.sharding import PartitionSpec as P

H = 16
D = 16
C = 256
N = 1024
HALF = 512
CAP = 384
FF = 1024
ROWS = 256
EPS = 1e-05
LOG2E = 1.4426950408889634
SCORE = LOG2E / 4.0
VSCALE = 2.0**-8

bf16 = jnp.bfloat16
f32 = jnp.float32


def dg(a, b, ca, cb):
    return lax.dot_general(a, b, (((ca,), (cb,)), ((), ())), preferred_element_type=f32)


def column(row, count):
    return jnp.transpose(jnp.broadcast_to(row, (128, count)))


def picks_from_column(col, start, width):
    lanes = lax.broadcasted_iota(jnp.int32, col.shape, 1)
    parts = [
        jnp.where(col == lanes + (start + 128 * b), 1.0, 0.0).astype(bf16)
        for b in range(width // 128)
    ]
    return jnp.concatenate(parts, axis=1)


def picks_from_row(row, start, height):
    ids = lax.broadcasted_iota(jnp.int32, (height, row.shape[1]), 0) + start
    return jnp.where(ids == row, 1.0, 0.0).astype(bf16)


def gather_kernel(points, sender, left, right):
    col = column(sender[...], 2 * CAP)
    rows = dg(picks_from_column(col, 0, N), points[...], 1, 0).astype(bf16)
    left[...] = rows[:CAP]
    right[...] = rows[CAP:]


def order_kernel(points, from_prev, from_next, slot, first, second):
    col = column(slot[...], N)
    rows = dg(picks_from_column(col, 0, N), points[...], 1, 0)
    rows += dg(picks_from_column(col, N, CAP), from_prev[...], 1, 0)
    rows += dg(picks_from_column(col, N + CAP, CAP), from_next[...], 1, 0)
    rows = rows.astype(bf16)
    first[...] = rows[:HALF]
    second[...] = rows[HALF:]


def back_kernel(first, second, slot, to_prev, to_next):
    row = slot[...]
    picks = picks_from_row(row, N, 2 * CAP)
    rows = dg(picks[:, :HALF], first[...], 1, 0) + dg(picks[:, HALF:], second[...], 1, 0)
    rows = rows.astype(bf16)
    to_prev[...] = rows[:CAP]
    to_next[...] = rows[CAP:]


def own_kernel(first, second, slot, out):
    picks = picks_from_row(slot[...], 0, N)
    rows = dg(picks[:, :HALF], first[...], 1, 0) + dg(picks[:, HALF:], second[...], 1, 0)
    out[...] = rows.astype(bf16)


def final_kernel(own, left, right, sender, out):
    picks = picks_from_row(sender[...], 0, N)
    rows = dg(picks[:, :CAP], left[...], 1, 0) + dg(picks[:, CAP:], right[...], 1, 0)
    out[...] = (own[...].astype(f32) + rows).astype(bf16)


def normalize(rows):
    mean = jnp.mean(rows, axis=-1, keepdims=True)
    centered = rows - mean
    spread = jnp.mean(centered * centered, axis=-1, keepdims=True)
    scale = lax.rsqrt(spread + EPS)
    return centered * scale, scale


def normalize_back(grad, unit, scale):
    return scale * (
        grad
        - jnp.mean(grad, axis=-1, keepdims=True)
        - unit * jnp.mean(grad * unit, axis=-1, keepdims=True)
    )


def main_kernel(
    ord_lo, ord_hi, cot_lo, cot_hi, gain1, wqkv, wproj, gain2, wfc1, wfc2,
    out_lo, out_hi, grad_lo, grad_hi,
    e_scr, x_scr, kn, vn, qt, kt, vt, ot, inv_scr, amp_scr, gt, mix_grad, dt,
):
    x_scr[:HALF] = ord_lo[...]
    x_scr[HALF:] = ord_hi[...]

    vt[...] = jnp.full((H, 2 * D, N), VSCALE, bf16)
    for b in range(N // ROWS):
        sl = slice(b * ROWS, (b + 1) * ROWS)
        unit, _ = normalize(x_scr[sl].astype(f32))
        normed = (unit * gain1[...]).astype(bf16)
        qkv = dg(normed, wqkv[...], 1, 0).astype(bf16)
        kn[0, sl] = qkv[:, 256:384]
        kn[1, sl] = qkv[:, 384:512]
        vn[0, sl] = qkv[:, 512:640]
        vn[1, sl] = qkv[:, 640:768]
        flipped = jnp.transpose(qkv)
        qt[:, sl] = flipped[:256]
        kt[:, sl] = flipped[256:512]
        vt[:, :D, sl] = flipped[512:].reshape(H, D, ROWS) * bf16(VSCALE)

    lane_head = lax.broadcasted_iota(jnp.int32, (N, 128), 1) // D

    def forward_head(h, carry):
        block = h // 8
        mask = lane_head == h % 8
        keys = jnp.where(mask, kn[block], bf16(0))
        scores = dg(keys, qt[pl.ds(block * 128, 128)], 1, 0)
        weights = jnp.exp2(scores * SCORE).astype(bf16)
        e_scr[h] = weights
        sums = dg(vt[h], weights, 1, 0)
        total = sums[D : D + 1]
        amp = jnp.where(total >= 2.0**40, 2.0**-80, jnp.where(total < 2.0**-40, 2.0**80, 1.0))
        inverse = 1.0 / (total * amp)
        ot[pl.ds(h * D, D)] = (sums[:D] * amp) * inverse
        inv_scr[pl.ds(h * D, D)] = jnp.broadcast_to(inverse * VSCALE, (D, N))
        amp_scr[h] = jnp.broadcast_to(amp, (D, N)).astype(bf16)
        return carry

    lax.fori_loop(0, H, forward_head, 0)

    for b in range(N // ROWS):
        sl = slice(b * ROWS, (b + 1) * ROWS)
        half = b // 2
        hs = slice((b % 2) * ROWS, (b % 2 + 1) * ROWS)
        attention = jnp.transpose(ot[:, sl].astype(bf16))
        mixed = x_scr[sl].astype(f32) + dg(attention, wproj[...], 1, 0)
        unit, scale = normalize(mixed)
        normed = (unit * gain2[...]).astype(bf16)
        pre = dg(normed, wfc1[...], 1, 0)
        cdf = 0.5 * (1.0 + lax.erf(pre * (2.0**-0.5)))
        act = (pre * cdf).astype(bf16)
        (out_lo, out_hi)[half][hs] = (mixed + dg(act, wfc2[...], 1, 0)).astype(bf16)
        cot = (cot_lo, cot_hi)[half][hs]
        grad_act = dg(cot, wfc2[...], 1, 1)
        density = jnp.exp(-0.5 * pre * pre) * (1.0 / math.sqrt(2.0 * math.pi))
        grad_pre = (grad_act * (cdf + pre * density)).astype(bf16)
        grad_normed = dg(grad_pre, wfc1[...], 1, 1)
        grad_mixed = cot.astype(f32) + normalize_back(grad_normed * gain2[...], unit, scale)
        mix_grad[sl] = grad_mixed
        grad_att = dg(grad_mixed.astype(bf16), wproj[...], 1, 1).astype(bf16)
        gt[:, sl] = (jnp.transpose(grad_att).astype(f32) * inv_scr[:, sl]).astype(bf16)

    def backward_head(h, carry):
        block = h // 8
        rows = pl.ds(h * D, D)
        mask = lane_head == h % 8
        values = jnp.where(mask, vn[block], bf16(0))
        grads = gt[rows]
        inner = jnp.sum(grads.astype(f32) * ot[rows], axis=0, keepdims=True)
        probs = e_scr[h] * amp_scr[h, :1]
        dt[pl.ds(512 + h * D, D)] = dg(grads, probs, 1, 1).astype(bf16)
        grad_probs = dg(values, gt[pl.ds(block * 128, 128)], 1, 0) - inner
        grad_scores = probs * grad_probs.astype(bf16)
        dt[rows] = (dg(kt[rows], grad_scores, 1, 0) * 0.25).astype(bf16)
        dt[pl.ds(256 + h * D, D)] = (dg(qt[rows], grad_scores, 1, 1) * 0.25).astype(bf16)
        return carry

    lax.fori_loop(0, H, backward_head, 0)

    for b in range(N // ROWS):
        sl = slice(b * ROWS, (b + 1) * ROWS)
        half = b // 2
        hs = slice((b % 2) * ROWS, (b % 2 + 1) * ROWS)
        grad_qkv = jnp.transpose(dt[:, sl])
        grad_normed = dg(grad_qkv, wqkv[...], 1, 1)
        unit, scale = normalize(x_scr[sl].astype(f32))
        grad = mix_grad[sl] + normalize_back(grad_normed * gain1[...], unit, scale)
        (grad_lo, grad_hi)[half][hs] = grad.astype(bf16)


PARAMS = pltpu.CompilerParams(vmem_limit_bytes=60 * 1024 * 1024)


def call(kernel, outs, scratch=(), name=None):
    return pl.pallas_call(
        kernel,
        out_shape=tuple(jax.ShapeDtypeStruct(s, bf16) for s in outs),
        scratch_shapes=list(scratch),
        compiler_params=PARAMS,
        name=name,
    )


def shift(rows, step):
    axes = ("gx", "gy")
    count = lax.axis_size(axes)
    return lax.ppermute(rows, axes, [(i, (i + step) % count) for i in range(count)])


def shards(
    points, send_rows, recv_slot, norm1_gain, qkv_weight, proj_weight, norm2_gain,
    fc1_weight, fc2_weight, cotangent,
):
    local = points[0]
    sender = send_rows[0]
    slot = recv_slot
    cot = cotangent[0]
    gain1 = norm1_gain.reshape(1, C)
    gain2 = norm2_gain.reshape(1, C)

    left, right = call(gather_kernel, [(CAP, C)] * 2, name="gather")(local, sender)
    from_prev = shift(right, 1)
    from_next = shift(left, -1)
    cot_lo = shift(cot[HALF:], 1)
    first, second = call(order_kernel, [(HALF, C)] * 2, name="order")(
        local, from_prev, from_next, slot
    )
    ord_lo = shift(second, 1)
    vm = pltpu.VMEM
    out_lo, out_hi, grad_lo, grad_hi = call(
        main_kernel,
        [(HALF, C)] * 4,
        [
            vm((H, N, N), bf16),
            vm((N, C), bf16),
            vm((2, N, 128), bf16),
            vm((2, N, 128), bf16),
            vm((C, N), bf16),
            vm((C, N), bf16),
            vm((H, 2 * D, N), bf16),
            vm((C, N), f32),
            vm((C, N), f32),
            vm((H, D, N), bf16),
            vm((C, N), bf16),
            vm((N, C), f32),
            vm((3 * C, N), bf16),
        ],
        name="block",
    )(
        ord_lo, first, cot_lo, cot[:HALF], gain1, qkv_weight, proj_weight, gain2,
        fc1_weight, fc2_weight,
    )
    grad_second = shift(grad_lo, -1)
    out_second = shift(out_lo, -1)
    to_prev, to_next = call(back_kernel, [(CAP, C)] * 2, name="back")(grad_hi, grad_second, slot)
    back_left = shift(to_prev, -1)
    back_right = shift(to_next, 1)
    (own,) = call(own_kernel, [(N, C)], name="own")(grad_hi, grad_second, slot)
    (grad_points,) = call(final_kernel, [(N, C)], name="final")(own, back_right, back_left, sender)
    block_out = jnp.concatenate([out_hi, out_second], axis=0)
    return (block_out[None], grad_points[None])


def solution(mesh):
    rows = P(None, ("gx", "gy"), None)
    in_specs = (rows, rows, P(None, ("gx", "gy")), P(), P(), P(), P(), P(), P(), rows)
    return jax.shard_map(
        shards, mesh=mesh, in_specs=in_specs, out_specs=(rows, rows), check_vma=False
    )
```

time: 682 us -> 120 us (0.18)
  matrix products: 506 us -> 0 us
  Pallas kernels: 0 us -> 72.7 us
  local copies, waits for them, and re-layouts: 75 us -> 4.84 us
  other arithmetic: 27.9 us -> 0.83 us
  waiting for transfers between devices: 41.4 us -> 24.9 us
  loops' own time: 11.4 us -> 0 us
    dot_general x51 -> x0, matrix products: 506 us -> none  [the longest x8 169 us: attend_backward(): jnp.einsum('hqk,khd->qhd', grad_scores, key_heads, preferred_element_type...]
    pallas_call x0 -> x6, Pallas kernels: none -> 72.7 us  [the longest x1 59.5 us: shards(): call(main_kernel, [(HALF, C)] * 4, [vm((H, N, N), bf16), vm((N, C), bf16)...]
    dynamic_slice x52 -> x0, local copies, waits for them, and re-layouts: 29.1 us -> none  [the longest x32 14.9 us: columns(): return lax.dynamic_slice_in_dim(matrix, start, group_width, 1)]
    ppermute x8, waiting for transfers between devices: 41.4 us -> 24.9 us  [shift(): lax.ppermute(rows, axes, [(i, (i + step) % count) for i in range(count)])]
    another operation x4 -> x0, loops' own time: 11.4 us -> none  [the longest x2 5.82 us: backward_block(): lax.map(one_group, jnp.arange(group_count, dtype=jnp.int32))]
    dynamic_update_slice x24 -> x0, local copies, waits for them, and re-layouts: 10.4 us -> none  [the longest x16 6.93 us: backward_block(): lax.map(one_group, jnp.arange(group_count, dtype=jnp.int32))]
    reduce_sum x6 -> x0, other arithmetic: 7.62 us -> none  [the longest x1 5.17 us: shards(): paired.reshape(block_count // 2 + 1, 2, K, 2 * head_width).sum(axis=1)]
    gather x3 -> x0, local copies, waits for them, and re-layouts: 7.35 us -> none  [the longest x2 4.15 us: shards(): ordered = pool[slot_index]]
  transfers between devices with their start and end apart: 8 -> 8, of which waited for: 7 -> 5; matrix products, arithmetic and copies ran while one was open for 1% -> 1% of each run, Pallas kernels for 0% -> 7%
where the time goes in v1:
time: 120 us; the launch traced here: 119 us
  Pallas kernels  72.7 us (61%)
  waiting for transfers between devices  24.9 us (21%)
  starting transfers between devices  15.6 us (13%)
  local copies, waits for them, and re-layouts  4.84 us (4%)
    pallas_call x1, Pallas kernels, shards(): call(main_kernel, [(HALF, C)] * 4, [vm((H, N, N), bf16), vm((N, C), bf16)...  59.5 us
    ppermute x8, waiting for transfers between devices, shift(): lax.ppermute(rows, axes, [(i, (i + step) % count) for i in range(count)])  24.9 us
    ppermute x8, starting transfers between devices, shift(): lax.ppermute(rows, axes, [(i, (i + step) % count) for i in range(count)])  15.6 us
    unnamed x18, local copies, waits for them, and re-layouts  4.11 us
    pallas_call x1, Pallas kernels, shards(): call(order_kernel, [(HALF, C)] * 2, name='order')  3.28 us
    pallas_call x1, Pallas kernels, shards(): call(final_kernel, [(N, C)], name='final')  2.68 us
    pallas_call x1, Pallas kernels, shards(): own, = call(own_kernel, [(N, C)], name='own')(grad_hi, grad_second, slot)  2.54 us
    pallas_call x1, Pallas kernels, shards(): call(gather_kernel, [(CAP, C)] * 2, name='gather')(local, sender)  2.4 us
  transfers between devices with their start and end apart: 8, of which 5 were waited for; matrix products, arithmetic and copies ran while one was open for 1% of the time, Pallas kernels for 7%

profile of v1, /device:TPU:0, one launch (start us, length us, event | category | flops | bytes accessed | tf_op | source)
XLA Modules:
  0.0 119.5 jit_solution(12658590726772660876)
XLA Ops:
  0.6 0.0 copy-start.1
  0.6 2.4 %gather.1 = (bf16[384,256]{1,0:T(8,128)(2,1)}, bf16[384,256]{1,0:T(8,128)(2,1)}) custom-call(bf16[1024,256]{1,0:T(8,128)(2,1)} %bitcast.11, s32[1,768]{1,0:T(1,128)} %bitcast.14), custom_call_target="tpu_custom_call" | custom-call | tf_op jit(solution)/shard_map/gather/pallas_call | solution.py:227
  3.0 1.6 %collective-permute-start = (bf16[384,256]{1,0:T(8,128)(2,1)}, bf16[384,256]{1,0:T(8,128)(2,1)S(1)}, u32[]{:S(2)}, u32[]{:S(2)}) collective-permute-start(bf16[384,256]{1,0:T(8,128)(2,1)} %get-tuple-element.12), channel_id=1, source_target_pairs={{0,1},{1,2},{2,3},{3,4},{4,5},{5,6},{6,7},{7,8},{8,9},{9,10},{10,1... | collective-permute-start | bytes 589832 | tf_op jit(solution)/shard_map/ppermute | solution.py:213
  4.6 6.6 %collective-permute-start.1 = (bf16[384,256]{1,0:T(8,128)(2,1)}, bf16[384,256]{1,0:T(8,128)(2,1)S(1)}, u32[]{:S(2)}, u32[]{:S(2)}) collective-permute-start(bf16[384,256]{1,0:T(8,128)(2,1)} %get-tuple-element.13), channel_id=1, source_target_pairs={{0,127},{1,0},{2,1},{3,2},{4,3},{5,4},{6,5},{7,6},{8,7},{9,8},{10,... | collective-permute-start | bytes 589832 | tf_op jit(solution)/shard_map/ppermute | solution.py:213
  11.3 0.0 copy-done.1
  11.3 0.7 slice_bitcast_fusion
  12.0 0.0 collective-permute-start.3
  12.0 4.1 %collective-permute-done.from_prev = bf16[384,256]{1,0:T(8,128)(2,1)S(1)} collective-permute-done((bf16[384,256]{1,0:T(8,128)(2,1)}, bf16[384,256]{1,0:T(8,128)(2,1)S(1)}, u32[]{:S(2)}, u32[]{:S(2)}) %collective-permute-start) | collective-permute-done | bytes 196640 | tf_op jit(solution)/shard_map/ppermute | solution.py:213
  16.1 0.0 collective-permute-done.1.from_next
  16.1 0.7 copy-done.6
  16.8 0.7 copy-done.8
  17.4 3.3 %order.1 = (bf16[512,256]{1,0:T(8,128)(2,1)}, bf16[512,256]{1,0:T(8,128)(2,1)}) custom-call(bf16[1024,256]{1,0:T(8,128)(2,1)} %bitcast.12, bf16[384,256]{1,0:T(8,128)(2,1)} %copy-done.6, bf16[384,256]{1,0:T(8,128)(2,1)} %copy-done.8, s32[1,1024]{1,0:T(1,128)} %slot.5), custom_call_target="tpu_custom_call" | custom-call | tf_op jit(solution)/shard_map/order/pallas_call | solution.py:231
  20.7 0.0 collective-permute-start.2
  20.7 4.1 %collective-permute-done.3.cot_lo = bf16[512,256]{1,0:T(8,128)(2,1)S(1)} collective-permute-done((bf16[512,256]{1,0:T(8,128)(2,1)S(1)}, bf16[512,256]{1,0:T(8,128)(2,1)S(1)}, u32[]{:S(2)}, u32[]{:S(2)}) %collective-permute-start.3) | collective-permute-done | bytes 262176 | tf_op jit(solution)/shard_map/ppermute | solution.py:213
  24.8 9.2 %collective-permute-done.2.ord_lo = bf16[512,256]{1,0:T(8,128)(2,1)S(1)} collective-permute-done((bf16[512,256]{1,0:T(8,128)(2,1)}, bf16[512,256]{1,0:T(8,128)(2,1)S(1)}, u32[]{:S(2)}, u32[]{:S(2)}) %collective-permute-start.2) | collective-permute-done | bytes 262176 | tf_op jit(solution)/shard_map/ppermute | solution.py:213
  34.0 0.7 copy-done.3
  34.7 59.5 %block.1 = (bf16[512,256]{1,0:T(8,128)(2,1)}, bf16[512,256]{1,0:T(8,128)(2,1)}, bf16[512,256]{1,0:T(8,128)(2,1)}, bf16[512,256]{1,0:T(8,128)(2,1)}) custom-call(bf16[512,256]{1,0:T(8,128)(2,1)} %copy-done.3, bf16[512,256]{1,0:T(8,128)(2,1)} %get-tuple-element.15.ord_hi, bf16[512,256]{1,0:T(8,128)(2,1)} %copy-done.2, ...), custom_call_target="tpu_custom_call" | custom-call | tf_op jit(solution)/shard_map/block/pallas_call | solution.py:236
  94.2 0.1 collective-permute-start.5
  94.3 0.0 collective-permute-start.4
  94.4 7.0 %collective-permute-done.5.second = bf16[512,256]{1,0:T(8,128)(2,1)S(1)} collective-permute-done((bf16[512,256]{1,0:T(8,128)(2,1)}, bf16[512,256]{1,0:T(8,128)(2,1)S(1)}, u32[]{:S(2)}, u32[]{:S(2)}) %collective-permute-start.5) | collective-permute-done | bytes 262176 | tf_op jit(solution)/shard_map/ppermute | solution.py:213
  101.4 0.7 copy-done
  102.1 2.3 %back.1 = (bf16[384,256]{1,0:T(8,128)(2,1)}, bf16[384,256]{1,0:T(8,128)(2,1)}) custom-call(bf16[512,256]{1,0:T(8,128)(2,1)} %get-tuple-element.18.first, bf16[512,256]{1,0:T(8,128)(2,1)} %copy-done, s32[1,1024]{1,0:T(1,128)} %slot.5), custom_call_target="tpu_custom_call" | custom-call | tf_op jit(solution)/shard_map/back/pallas_call | solution.py:261
  104.3 0.0 collective-permute-start.6
  104.4 7.2 %collective-permute-start.7 = (bf16[384,256]{1,0:T(8,128)(2,1)}, bf16[384,256]{1,0:T(8,128)(2,1)S(1)}, u32[]{:S(2)}, u32[]{:S(2)}) collective-permute-start(bf16[384,256]{1,0:T(8,128)(2,1)} %get-tuple-element.21), channel_id=1, source_target_pairs={{0,127},{1,0},{2,1},{3,2},{4,3},{5,4},{6,5},{7,6},{8,7},{9,8},{10,... | collective-permute-start | bytes 589832 | tf_op jit(solution)/shard_map/ppermute | solution.py:213
  111.5 2.5 %own.1 = bf16[1024,256]{1,0:T(8,128)(2,1)} custom-call(bf16[512,256]{1,0:T(8,128)(2,1)} %get-tuple-element.18.first, bf16[512,256]{1,0:T(8,128)(2,1)} %copy-done, s32[1,1024]{1,0:T(1,128)} %slot.5), custom_call_target="tpu_custom_call" | custom-call | tf_op jit(solution)/shard_map/own/pallas_call | solution.py:264
  114.1 0.0 collective-permute-done.4
  114.1 0.8 maximum_bitcast_fusion
  114.9 0.5 collective-permute-done.6.left
  115.4 0.0 collective-permute-done.7.right
  115.4 0.7 copy-done.5
  116.1 0.7 copy-done.7
  116.8 2.7 %final.1 = bf16[1024,256]{1,0:T(8,128)(2,1)} custom-call(bf16[1024,256]{1,0:T(8,128)(2,1)} %own.1, bf16[384,256]{1,0:T(8,128)(2,1)} %copy-done.5, bf16[384,256]{1,0:T(8,128)(2,1)} %copy-done.7, s32[1,768]{1,0:T(1,128)} %bitcast.15), custom_call_target="tpu_custom_call" | custom-call | tf_op jit(solution)/shard_map/final/pallas_call | solution.py:265
  (10 shorter events, 0.0 us)
Async XLA Ops:
  0.6 10.7 %copy-start.1 = (bf16[1,1024,256]{2,1,0:T(8,128)(2,1)S(1)}, bf16[1,1024,256]{2,1,0:T(8,128)(2,1)}, u32[]{:S(2)}) copy-start(bf16[1,1024,256]{2,1,0:T(8,128)(2,1)} %param.19) | copy-start | bytes 1572868
  3.0 13.0 %collective-permute-start = (bf16[384,256]{1,0:T(8,128)(2,1)}, bf16[384,256]{1,0:T(8,128)(2,1)S(1)}, u32[]{:S(2)}, u32[]{:S(2)}) collective-permute-start(bf16[384,256]{1,0:T(8,128)(2,1)} %get-tuple-element.12), channel_id=1, source_target_pairs={{0,1},{1,2},{2,3},{3,4},{4,5},{5,6},{6,7},{7,8},{8,9},{9,10},{10,1... | collective-permute-start | bytes 589832 | tf_op jit(solution)/shard_map/ppermute | solution.py:213
  4.6 11.4 %collective-permute-start.1 = (bf16[384,256]{1,0:T(8,128)(2,1)}, bf16[384,256]{1,0:T(8,128)(2,1)S(1)}, u32[]{:S(2)}, u32[]{:S(2)}) collective-permute-start(bf16[384,256]{1,0:T(8,128)(2,1)} %get-tuple-element.13), channel_id=1, source_target_pairs={{0,127},{1,0},{2,1},{3,2},{4,3},{5,4},{6,5},{7,6},{8,7},{9,8},{10,... | collective-permute-start | bytes 589832 | tf_op jit(solution)/shard_map/ppermute | solution.py:213
  12.0 12.8 %collective-permute-start.3 = (bf16[512,256]{1,0:T(8,128)(2,1)S(1)}, bf16[512,256]{1,0:T(8,128)(2,1)S(1)}, u32[]{:S(2)}, u32[]{:S(2)}) collective-permute-start(bf16[512,256]{1,0:T(8,128)(2,1)S(1)} %get-tuple-element.23), channel_id=1, source_target_pairs={{0,1},{1,2},{2,3},{3,4},{4,5},{5,6},{6,7},{7,8},{8,9},{9,10},{10,1... | collective-permute-start | bytes 786440 | tf_op jit(solution)/shard_map/ppermute | solution.py:213
  16.1 0.7 copy-start.6
  16.8 0.7 copy-start.8
  20.7 13.3 %collective-permute-start.2 = (bf16[512,256]{1,0:T(8,128)(2,1)}, bf16[512,256]{1,0:T(8,128)(2,1)S(1)}, u32[]{:S(2)}, u32[]{:S(2)}) collective-permute-start(bf16[512,256]{1,0:T(8,128)(2,1)} %get-tuple-element.14), channel_id=1, source_target_pairs={{0,1},{1,2},{2,3},{3,4},{4,5},{5,6},{6,7},{7,8},{8,9},{9,10},{10,1... | collective-permute-start | bytes 786440 | tf_op jit(solution)/shard_map/ppermute | solution.py:213
  24.8 9.2 %copy-start.2 = (bf16[512,256]{1,0:T(8,128)(2,1)}, bf16[512,256]{1,0:T(8,128)(2,1)S(1)}, u32[]{:S(2)}) copy-start(bf16[512,256]{1,0:T(8,128)(2,1)S(1)} %collective-permute-done.3.cot_lo) | copy-start | bytes 786436
  34.0 0.7 copy-start.3
  94.2 7.1 %collective-permute-start.5 = (bf16[512,256]{1,0:T(8,128)(2,1)}, bf16[512,256]{1,0:T(8,128)(2,1)S(1)}, u32[]{:S(2)}, u32[]{:S(2)}) collective-permute-start(bf16[512,256]{1,0:T(8,128)(2,1)} %get-tuple-element.19), channel_id=1, source_target_pairs={{0,127},{1,0},{2,1},{3,2},{4,3},{5,4},{6,5},{7,6},{8,7},{9,8},{10,... | collective-permute-start | bytes 786440 | tf_op jit(solution)/shard_map/ppermute | solution.py:213
  94.3 19.8 %collective-permute-start.4 = (bf16[512,256]{1,0:T(8,128)(2,1)}, bf16[512,256]{1,0:T(8,128)(2,1)S(1)}, u32[]{:S(2)}, u32[]{:S(2)}) collective-permute-start(bf16[512,256]{1,0:T(8,128)(2,1)} %get-tuple-element.17), channel_id=1, source_target_pairs={{0,127},{1,0},{2,1},{3,2},{4,3},{5,4},{6,5},{7,6},{8,7},{9,8},{10,... | collective-permute-start | bytes 786440 | tf_op jit(solution)/shard_map/ppermute | solution.py:213
  101.4 0.7 copy-start
  104.3 11.1 %collective-permute-start.6 = (bf16[384,256]{1,0:T(8,128)(2,1)}, bf16[384,256]{1,0:T(8,128)(2,1)S(1)}, u32[]{:S(2)}, u32[]{:S(2)}) collective-permute-start(bf16[384,256]{1,0:T(8,128)(2,1)} %get-tuple-element.20), channel_id=1, source_target_pairs={{0,1},{1,2},{2,3},{3,4},{4,5},{5,6},{6,7},{7,8},{8,9},{9,10},{10,1... | collective-permute-start | bytes 589832 | tf_op jit(solution)/shard_map/ppermute | solution.py:213
  104.3 9.7 %copy-start.4 = (bf16[512,256]{1,0:T(8,128)(2,1)S(1)}, bf16[512,256]{1,0:T(8,128)(2,1)}, u32[]{:S(2)}) copy-start(bf16[512,256]{1,0:T(8,128)(2,1)} %get-tuple-element.16) | copy-start | bytes 786436
  104.4 11.1 %collective-permute-start.7 = (bf16[384,256]{1,0:T(8,128)(2,1)}, bf16[384,256]{1,0:T(8,128)(2,1)S(1)}, u32[]{:S(2)}, u32[]{:S(2)}) collective-permute-start(bf16[384,256]{1,0:T(8,128)(2,1)} %get-tuple-element.21), channel_id=1, source_target_pairs={{0,127},{1,0},{2,1},{3,2},{4,3},{5,4},{6,5},{7,6},{8,7},{9,8},{10,... | collective-permute-start | bytes 589832 | tf_op jit(solution)/shard_map/ppermute | solution.py:213
  115.4 0.7 copy-start.5
  116.1 0.7 copy-start.7

commit v2 on v1

--- a/solution.py
+++ b/solution.py
@@ -47,42 +47,91 @@
     return jnp.where(ids == row, 1.0, 0.0).astype(bf16)
 
 
-def gather_kernel(points, sender, left, right):
-    col = column(sender[...], 2 * CAP)
-    rows = dg(picks_from_column(col, 0, N), points[...], 1, 0).astype(bf16)
-    left[...] = rows[:CAP]
-    right[...] = rows[CAP:]
-
-
-def order_kernel(points, from_prev, from_next, slot, first, second):
-    col = column(slot[...], N)
-    rows = dg(picks_from_column(col, 0, N), points[...], 1, 0)
-    rows += dg(picks_from_column(col, N, CAP), from_prev[...], 1, 0)
-    rows += dg(picks_from_column(col, N + CAP, CAP), from_next[...], 1, 0)
-    rows = rows.astype(bf16)
-    first[...] = rows[:HALF]
-    second[...] = rows[HALF:]
-
-
-def back_kernel(first, second, slot, to_prev, to_next):
-    row = slot[...]
-    picks = picks_from_row(row, N, 2 * CAP)
-    rows = dg(picks[:, :HALF], first[...], 1, 0) + dg(picks[:, HALF:], second[...], 1, 0)
-    rows = rows.astype(bf16)
-    to_prev[...] = rows[:CAP]
-    to_next[...] = rows[CAP:]
-
-
-def own_kernel(first, second, slot, out):
+class Fetch:
+    def __init__(self, pairs, sems):
+        self.copies = [
+            pltpu.make_async_copy(src, dst, sems.at[i]) for i, (src, dst) in enumerate(pairs)
+        ]
+        for copy in self.copies:
+            copy.start()
+
+    def wait(self, *which):
+        for i in which:
+            self.copies[i].wait()
+
+
+def gather_kernel(points, sender, left, right, points_v, rows_v, sems):
+    fetch = Fetch([(points, points_v)], sems)
+    picks = picks_from_column(column(sender[...], 2 * CAP), 0, N)
+    fetch.wait(0)
+    rows_v[:CAP] = dg(picks[:CAP], points_v[...], 1, 0).astype(bf16)
+    store = pltpu.make_async_copy(rows_v.at[:CAP], left, sems.at[1])
+    store.start()
+    rows_v[CAP:] = dg(picks[CAP:], points_v[...], 1, 0).astype(bf16)
+    last = pltpu.make_async_copy(rows_v.at[CAP:], right, sems.at[2])
+    last.start()
+    store.wait()
+    last.wait()
+
+
+def order_kernel(points, from_prev, from_next, slot, first, second, pool, rows_v, sems):
+    fetch = Fetch(
+        [
+            (points, pool.at[:N]),
+            (from_prev, pool.at[N : N + CAP]),
+            (from_next, pool.at[N + CAP :]),
+        ],
+        sems,
+    )
+    picks = picks_from_column(column(slot[...], N), 0, N + 2 * CAP)
+    fetch.wait(0, 1, 2)
+    rows_v[HALF:] = dg(picks[HALF:], pool[...], 1, 0).astype(bf16)
+    store = pltpu.make_async_copy(rows_v.at[HALF:], second, sems.at[3])
+    store.start()
+    rows_v[:HALF] = dg(picks[:HALF], pool[...], 1, 0).astype(bf16)
+    last = pltpu.make_async_copy(rows_v.at[:HALF], first, sems.at[4])
+    last.start()
+    store.wait()
+    last.wait()
+
+
+def back_kernel(first, second, slot, to_prev, to_next, grads, rows_v, sems):
+    fetch = Fetch([(first, grads.at[:HALF]), (second, grads.at[HALF:])], sems)
+    picks = picks_from_row(slot[...], N, 2 * CAP)
+    fetch.wait(0, 1)
+    rows_v[:CAP] = dg(picks[:CAP], grads[...], 1, 0).astype(bf16)
+    store = pltpu.make_async_copy(rows_v.at[:CAP], to_prev, sems.at[2])
+    store.start()
+    rows_v[CAP:] = dg(picks[CAP:], grads[...], 1, 0).astype(bf16)
+    last = pltpu.make_async_copy(rows_v.at[CAP:], to_next, sems.at[3])
+    last.start()
+    store.wait()
+    last.wait()
+
+
+def own_kernel(first, second, slot, out, grads, rows_v, sems):
+    fetch = Fetch([(first, grads.at[:HALF]), (second, grads.at[HALF:])], sems)
     picks = picks_from_row(slot[...], 0, N)
-    rows = dg(picks[:, :HALF], first[...], 1, 0) + dg(picks[:, HALF:], second[...], 1, 0)
-    out[...] = rows.astype(bf16)
-
-
-def final_kernel(own, left, right, sender, out):
+    fetch.wait(0, 1)
+    rows_v[...] = dg(picks, grads[...], 1, 0).astype(bf16)
+    pltpu.sync_copy(rows_v, out)
+
+
+def final_kernel(own, left, right, sender, out, own_v, returned, rows_v, sems):
+    fetch = Fetch(
+        [(left, returned.at[:CAP]), (right, returned.at[CAP:]), (own, own_v)], sems
+    )
     picks = picks_from_row(sender[...], 0, N)
-    rows = dg(picks[:, :CAP], left[...], 1, 0) + dg(picks[:, CAP:], right[...], 1, 0)
-    out[...] = (own[...].astype(f32) + rows).astype(bf16)
+    fetch.wait(0, 1, 2)
+    stores = []
+    for b in range(2):
+        sl = slice(b * HALF, (b + 1) * HALF)
+        rows = dg(picks[sl], returned[...], 1, 0)
+        rows_v[sl] = (own_v[sl].astype(f32) + rows).astype(bf16)
+        stores.append(pltpu.make_async_copy(rows_v.at[sl], out.at[sl], sems.at[3 + b]))
+        stores[-1].start()
+    for store in stores:
+        store.wait()
 
 
 def normalize(rows):
@@ -102,14 +151,26 @@
 
 
 def main_kernel(
-    ord_lo, ord_hi, cot_lo, cot_hi, gain1, wqkv, wproj, gain2, wfc1, wfc2,
+    ord_lo, ord_hi, cot_lo, cot_hi, wqkv_h, wproj_h, wfc1_h, wfc2_h, gain1, gain2,
     out_lo, out_hi, grad_lo, grad_hi,
+    wqkv, wproj, wfc1, wfc2, cot_v, out_v, probs_t, scores_t, sems,
     e_scr, x_scr, kn, vn, qt, kt, vt, ot, inv_scr, amp_scr, gt, mix_grad, dt,
 ):
-    x_scr[:HALF] = ord_lo[...]
-    x_scr[HALF:] = ord_hi[...]
-
+    fetch = Fetch(
+        [
+            (ord_hi, x_scr.at[HALF:]),
+            (wqkv_h, wqkv),
+            (ord_lo, x_scr.at[:HALF]),
+            (wproj_h, wproj),
+            (wfc1_h, wfc1),
+            (wfc2_h, wfc2),
+            (cot_lo, cot_v.at[:HALF]),
+            (cot_hi, cot_v.at[HALF:]),
+        ],
+        sems,
+    )
     vt[...] = jnp.full((H, 2 * D, N), VSCALE, bf16)
+    fetch.wait(0, 1, 2)
     for b in range(N // ROWS):
         sl = slice(b * ROWS, (b + 1) * ROWS)
         unit, _ = normalize(x_scr[sl].astype(f32))
@@ -143,11 +204,10 @@
         return carry
 
     lax.fori_loop(0, H, forward_head, 0)
+    fetch.wait(3, 4, 5, 6, 7)
 
     for b in range(N // ROWS):
         sl = slice(b * ROWS, (b + 1) * ROWS)
-        half = b // 2
-        hs = slice((b % 2) * ROWS, (b % 2 + 1) * ROWS)
         attention = jnp.transpose(ot[:, sl].astype(bf16))
         mixed = x_scr[sl].astype(f32) + dg(attention, wproj[...], 1, 0)
         unit, scale = normalize(mixed)
@@ -155,8 +215,8 @@
         pre = dg(normed, wfc1[...], 1, 0)
         cdf = 0.5 * (1.0 + lax.erf(pre * (2.0**-0.5)))
         act = (pre * cdf).astype(bf16)
-        (out_lo, out_hi)[half][hs] = (mixed + dg(act, wfc2[...], 1, 0)).astype(bf16)
-        cot = (cot_lo, cot_hi)[half][hs]
+        out_v[sl] = (mixed + dg(act, wfc2[...], 1, 0)).astype(bf16)
+        cot = cot_v[sl]
         grad_act = dg(cot, wfc2[...], 1, 1)
         density = jnp.exp(-0.5 * pre * pre) * (1.0 / math.sqrt(2.0 * math.pi))
         grad_pre = (grad_act * (cdf + pre * density)).astype(bf16)
@@ -166,6 +226,13 @@
         grad_att = dg(grad_mixed.astype(bf16), wproj[...], 1, 1).astype(bf16)
         gt[:, sl] = (jnp.transpose(grad_att).astype(f32) * inv_scr[:, sl]).astype(bf16)
 
+    stores = [
+        pltpu.make_async_copy(out_v.at[:HALF], out_lo, sems.at[8]),
+        pltpu.make_async_copy(out_v.at[HALF:], out_hi, sems.at[9]),
+    ]
+    for store in stores:
+        store.start()
+
     def backward_head(h, carry):
         block = h // 8
         rows = pl.ds(h * D, D)
@@ -174,37 +241,51 @@
         grads = gt[rows]
         inner = jnp.sum(grads.astype(f32) * ot[rows], axis=0, keepdims=True)
         probs = e_scr[h] * amp_scr[h, :1]
-        dt[pl.ds(512 + h * D, D)] = dg(grads, probs, 1, 1).astype(bf16)
+        probs_t[...] = jnp.transpose(probs)
         grad_probs = dg(values, gt[pl.ds(block * 128, 128)], 1, 0) - inner
         grad_scores = probs * grad_probs.astype(bf16)
         dt[rows] = (dg(kt[rows], grad_scores, 1, 0) * 0.25).astype(bf16)
-        dt[pl.ds(256 + h * D, D)] = (dg(qt[rows], grad_scores, 1, 1) * 0.25).astype(bf16)
+        dt[pl.ds(512 + h * D, D)] = dg(grads, probs_t[...], 1, 0).astype(bf16)
+        scores_t[...] = jnp.transpose(grad_scores)
+        dt[pl.ds(256 + h * D, D)] = (dg(qt[rows], scores_t[...], 1, 0) * 0.25).astype(bf16)
         return carry
 
     lax.fori_loop(0, H, backward_head, 0)
+    for store in stores:
+        store.wait()
 
     for b in range(N // ROWS):
         sl = slice(b * ROWS, (b + 1) * ROWS)
-        half = b // 2
-        hs = slice((b % 2) * ROWS, (b % 2 + 1) * ROWS)
         grad_qkv = jnp.transpose(dt[:, sl])
         grad_normed = dg(grad_qkv, wqkv[...], 1, 1)
         unit, scale = normalize(x_scr[sl].astype(f32))
         grad = mix_grad[sl] + normalize_back(grad_normed * gain1[...], unit, scale)
-        (grad_lo, grad_hi)[half][hs] = grad.astype(bf16)
+        out_v[sl] = grad.astype(bf16)
+        if b % 2:
+            hs = slice((b // 2) * HALF, (b // 2 + 1) * HALF)
+            out = (grad_lo, grad_hi)[b // 2]
+            stores[b // 2] = pltpu.make_async_copy(out_v.at[hs], out, sems.at[10 + b // 2])
+            stores[b // 2].start()
+    for store in stores:
+        store.wait()
 
 
 PARAMS = pltpu.CompilerParams(vmem_limit_bytes=60 * 1024 * 1024)
-
-
-def call(kernel, outs, scratch=(), name=None):
+vm = pltpu.VMEM
+
+
+def call(kernel, anys, others, outs, scratch, sems, name):
+    anyspace = pl.BlockSpec(memory_space=pl.ANY)
+    vmspace = pl.BlockSpec(memory_space=pltpu.VMEM)
     return pl.pallas_call(
         kernel,
+        in_specs=[anyspace] * len(anys) + [vmspace] * len(others),
+        out_specs=tuple([anyspace] * len(outs)),
         out_shape=tuple(jax.ShapeDtypeStruct(s, bf16) for s in outs),
-        scratch_shapes=list(scratch),
+        scratch_shapes=list(scratch) + ([pltpu.SemaphoreType.DMA((sems,))] if sems else []),
         compiler_params=PARAMS,
         name=name,
-    )
+    )(*anys, *others)
 
 
 def shift(rows, step):
@@ -224,21 +305,41 @@
     gain1 = norm1_gain.reshape(1, C)
     gain2 = norm2_gain.reshape(1, C)
 
-    left, right = call(gather_kernel, [(CAP, C)] * 2, name="gather")(local, sender)
+    block = vm((N, C), bf16)
+    slots = vm((2 * CAP, C), bf16)
+    left, right = call(
+        gather_kernel, [local], [sender], [(CAP, C)] * 2, [block, slots], 3, "gather"
+    )
     from_prev = shift(right, 1)
     from_next = shift(left, -1)
     cot_lo = shift(cot[HALF:], 1)
-    first, second = call(order_kernel, [(HALF, C)] * 2, name="order")(
-        local, from_prev, from_next, slot
+    first, second = call(
+        order_kernel,
+        [local, from_prev, from_next],
+        [slot],
+        [(HALF, C)] * 2,
+        [vm((N + 2 * CAP, C), bf16), block],
+        5,
+        "order",
     )
     ord_lo = shift(second, 1)
-    vm = pltpu.VMEM
     out_lo, out_hi, grad_lo, grad_hi = call(
         main_kernel,
+        [ord_lo, first, cot_lo, cot[:HALF], qkv_weight, proj_weight, fc1_weight, fc2_weight],
+        [gain1, gain2],
         [(HALF, C)] * 4,
         [
+            vm((C, 3 * C), bf16),
+            vm((C, C), bf16),
+            vm((C, FF), bf16),
+            vm((FF, C), bf16),
+            block,
+            block,
+            vm((N, N), bf16),
+            vm((N, N), bf16),
+            pltpu.SemaphoreType.DMA((12,)),
             vm((H, N, N), bf16),
-            vm((N, C), bf16),
+            block,
             vm((2, N, 128), bf16),
             vm((2, N, 128), bf16),
             vm((C, N), bf16),
@@ -251,18 +352,26 @@
             vm((N, C), f32),
             vm((3 * C, N), bf16),
         ],
-        name="block",
-    )(
-        ord_lo, first, cot_lo, cot[:HALF], gain1, qkv_weight, proj_weight, gain2,
-        fc1_weight, fc2_weight,
+        0,
+        "block",
     )
     grad_second = shift(grad_lo, -1)
     out_second = shift(out_lo, -1)
-    to_prev, to_next = call(back_kernel, [(CAP, C)] * 2, name="back")(grad_hi, grad_second, slot)
+    to_prev, to_next = call(
+        back_kernel, [grad_hi, grad_second], [slot], [(CAP, C)] * 2, [block, slots], 4, "back"
+    )
     back_left = shift(to_prev, -1)
     back_right = shift(to_next, 1)
-    (own,) = call(own_kernel, [(N, C)], name="own")(grad_hi, grad_second, slot)
-    (grad_points,) = call(final_kernel, [(N, C)], name="final")(own, back_right, back_left, sender)
+    (own,) = call(own_kernel, [grad_hi, grad_second], [slot], [(N, C)], [block, block], 2, "own")
+    (grad_points,) = call(
+        final_kernel,
+        [own, back_right, back_left],
+        [sender],
+        [(N, C)],
+        [block, slots, block],
+        5,
+        "final",
+    )
     block_out = jnp.concatenate([out_hi, out_second], axis=0)
     return (block_out[None], grad_points[None])
 

time: 120 us -> 116 us (0.967)
  Pallas kernels: 72.7 us -> 68.9 us
    pallas_call x6, Pallas kernels: 72.7 us -> 68.9 us  [call(): pl.pallas_call(kernel, in_specs=[anyspace] * len(anys) + [vmspace] * len(...]
  transfers between devices with their start and end apart: 8 -> 8, of which waited for: 5 -> 5; matrix products, arithmetic and copies ran while one was open for 1% -> 1% of each run, Pallas kernels for 7% -> 9%
where the time goes in v2:
time: 116 us
  Pallas kernels  68.9 us (59%)
  waiting for transfers between devices  24.2 us (21%)
  starting transfers between devices  16.4 us (14%)
  local copies, waits for them, and re-layouts  4.84 us (4%)
    pallas_call x6, Pallas kernels, call(): pl.pallas_call(kernel, in_specs=[anyspace] * len(anys) + [vmspace] * len(...  68.9 us
    ppermute x8, waiting for transfers between devices, shift(): lax.ppermute(rows, axes, [(i, (i + step) % count) for i in range(count)])  24.2 us
    ppermute x8, starting transfers between devices, shift(): lax.ppermute(rows, axes, [(i, (i + step) % count) for i in range(count)])  16.4 us
    unnamed x18, local copies, waits for them, and re-layouts  4.11 us
  transfers between devices with their start and end apart: 8, of which 5 were waited for; matrix products, arithmetic and copies ran while one was open for 1% of the time, Pallas kernels for 9%

profile of v2, /device:TPU:0, one launch (start us, length us, event | category | flops | bytes accessed | tf_op | source)
XLA Modules:
  0.0 116.1 jit_solution(11750999461108100355)
XLA Ops:
  0.6 0.0 copy-start.1
  0.6 3.1 %gather.1 = (bf16[384,256]{1,0:T(8,128)(2,1)}, bf16[384,256]{1,0:T(8,128)(2,1)}) custom-call(bf16[1024,256]{1,0:T(8,128)(2,1)} %bitcast.11, s32[1,768]{1,0:T(1,128)} %bitcast.14), custom_call_target="tpu_custom_call" | custom-call | tf_op jit(solution)/shard_map/gather/pallas_call | solution.py:280
  3.8 1.7 %collective-permute-start = (bf16[384,256]{1,0:T(8,128)(2,1)}, bf16[384,256]{1,0:T(8,128)(2,1)S(1)}, u32[]{:S(2)}, u32[]{:S(2)}) collective-permute-start(bf16[384,256]{1,0:T(8,128)(2,1)} %get-tuple-element.12), channel_id=1, source_target_pairs={{0,1},{1,2},{2,3},{3,4},{4,5},{5,6},{6,7},{7,8},{8,9},{9,10},{10,1... | collective-permute-start | bytes 589832 | tf_op jit(solution)/shard_map/ppermute | solution.py:294
  5.4 6.7 %collective-permute-start.1 = (bf16[384,256]{1,0:T(8,128)(2,1)}, bf16[384,256]{1,0:T(8,128)(2,1)S(1)}, u32[]{:S(2)}, u32[]{:S(2)}) collective-permute-start(bf16[384,256]{1,0:T(8,128)(2,1)} %get-tuple-element.13), channel_id=1, source_target_pairs={{0,127},{1,0},{2,1},{3,2},{4,3},{5,4},{6,5},{7,6},{8,7},{9,8},{10,... | collective-permute-start | bytes 589832 | tf_op jit(solution)/shard_map/ppermute | solution.py:294
  12.2 0.0 copy-done.1
  12.2 0.7 slice_bitcast_fusion
  12.9 0.0 collective-permute-start.3
  12.9 4.0 %collective-permute-done.from_prev = bf16[384,256]{1,0:T(8,128)(2,1)S(1)} collective-permute-done((bf16[384,256]{1,0:T(8,128)(2,1)}, bf16[384,256]{1,0:T(8,128)(2,1)S(1)}, u32[]{:S(2)}, u32[]{:S(2)}) %collective-permute-start) | collective-permute-done | bytes 196640 | tf_op jit(solution)/shard_map/ppermute | solution.py:294
  16.9 0.0 collective-permute-done.1.from_next
  16.9 0.7 copy-done.6
  17.6 0.7 copy-done.8
  18.2 3.8 %order.1 = (bf16[512,256]{1,0:T(8,128)(2,1)}, bf16[512,256]{1,0:T(8,128)(2,1)}) custom-call(bf16[1024,256]{1,0:T(8,128)(2,1)} %bitcast.12, bf16[384,256]{1,0:T(8,128)(2,1)} %copy-done.6, bf16[384,256]{1,0:T(8,128)(2,1)} %copy-done.8, s32[1,1024]{1,0:T(1,128)} %slot.5), custom_call_target="tpu_custom_call" | custom-call | tf_op jit(solution)/shard_map/order/pallas_call | solution.py:280
  22.0 0.3 collective-permute-start.2
  22.3 3.4 %collective-permute-done.3.cot_lo = bf16[512,256]{1,0:T(8,128)(2,1)S(1)} collective-permute-done((bf16[512,256]{1,0:T(8,128)(2,1)S(1)}, bf16[512,256]{1,0:T(8,128)(2,1)S(1)}, u32[]{:S(2)}, u32[]{:S(2)}) %collective-permute-start.3) | collective-permute-done | bytes 262176 | tf_op jit(solution)/shard_map/ppermute | solution.py:294
  25.7 9.9 %collective-permute-done.2.ord_lo = bf16[512,256]{1,0:T(8,128)(2,1)S(1)} collective-permute-done((bf16[512,256]{1,0:T(8,128)(2,1)}, bf16[512,256]{1,0:T(8,128)(2,1)S(1)}, u32[]{:S(2)}, u32[]{:S(2)}) %collective-permute-start.2) | collective-permute-done | bytes 262176 | tf_op jit(solution)/shard_map/ppermute | solution.py:294
  35.6 0.7 copy-done.3
  36.3 52.3 %block.1 = (bf16[512,256]{1,0:T(8,128)(2,1)}, bf16[512,256]{1,0:T(8,128)(2,1)}, bf16[512,256]{1,0:T(8,128)(2,1)}, bf16[512,256]{1,0:T(8,128)(2,1)}) custom-call(bf16[512,256]{1,0:T(8,128)(2,1)} %copy-done.3, bf16[512,256]{1,0:T(8,128)(2,1)} %get-tuple-element.15.ord_hi, bf16[512,256]{1,0:T(8,128)(2,1)} %copy-done.2, ...), custom_call_target="tpu_custom_call" | custom-call | tf_op jit(solution)/shard_map/block/pallas_call | solution.py:280
  88.6 0.4 collective-permute-start.5
  89.0 0.1 collective-permute-start.4
  89.1 6.1 %collective-permute-done.5.second = bf16[512,256]{1,0:T(8,128)(2,1)S(1)} collective-permute-done((bf16[512,256]{1,0:T(8,128)(2,1)}, bf16[512,256]{1,0:T(8,128)(2,1)S(1)}, u32[]{:S(2)}, u32[]{:S(2)}) %collective-permute-start.5) | collective-permute-done | bytes 262176 | tf_op jit(solution)/shard_map/ppermute | solution.py:294
  95.2 0.7 copy-done
  95.9 3.1 %back.1 = (bf16[384,256]{1,0:T(8,128)(2,1)}, bf16[384,256]{1,0:T(8,128)(2,1)}) custom-call(bf16[512,256]{1,0:T(8,128)(2,1)} %get-tuple-element.18.first, bf16[512,256]{1,0:T(8,128)(2,1)} %copy-done, s32[1,1024]{1,0:T(1,128)} %slot.5), custom_call_target="tpu_custom_call" | custom-call | tf_op jit(solution)/shard_map/back/pallas_call | solution.py:280
  99.0 0.1 collective-permute-start.6
  99.1 7.2 %collective-permute-start.7 = (bf16[384,256]{1,0:T(8,128)(2,1)}, bf16[384,256]{1,0:T(8,128)(2,1)S(1)}, u32[]{:S(2)}, u32[]{:S(2)}) collective-permute-start(bf16[384,256]{1,0:T(8,128)(2,1)} %get-tuple-element.21), channel_id=1, source_target_pairs={{0,127},{1,0},{2,1},{3,2},{4,3},{5,4},{6,5},{7,6},{8,7},{9,8},{10,... | collective-permute-start | bytes 589832 | tf_op jit(solution)/shard_map/ppermute | solution.py:294
  106.3 3.2 %own.1 = bf16[1024,256]{1,0:T(8,128)(2,1)} custom-call(bf16[512,256]{1,0:T(8,128)(2,1)} %get-tuple-element.18.first, bf16[512,256]{1,0:T(8,128)(2,1)} %copy-done, s32[1,1024]{1,0:T(1,128)} %slot.5), custom_call_target="tpu_custom_call" | custom-call | tf_op jit(solution)/shard_map/own/pallas_call | solution.py:280
  109.5 0.0 collective-permute-done.4
  109.5 0.8 maximum_bitcast_fusion
  110.4 0.8 collective-permute-done.6.left
  111.2 0.0 collective-permute-done.7.right
  111.2 0.7 copy-done.5
  111.9 0.7 copy-done.7
  112.6 3.3 %final.1 = bf16[1024,256]{1,0:T(8,128)(2,1)} custom-call(bf16[1024,256]{1,0:T(8,128)(2,1)} %own.1, bf16[384,256]{1,0:T(8,128)(2,1)} %copy-done.5, bf16[384,256]{1,0:T(8,128)(2,1)} %copy-done.7, s32[1,768]{1,0:T(1,128)} %bitcast.15), custom_call_target="tpu_custom_call" | custom-call | tf_op jit(solution)/shard_map/final/pallas_call | solution.py:280
  (10 shorter events, 0.0 us)
Async XLA Ops:
  0.6 11.5 %copy-start.1 = (bf16[1,1024,256]{2,1,0:T(8,128)(2,1)S(1)}, bf16[1,1024,256]{2,1,0:T(8,128)(2,1)}, u32[]{:S(2)}) copy-start(bf16[1,1024,256]{2,1,0:T(8,128)(2,1)} %param.19) | copy-start | bytes 1572868
  3.8 13.1 %collective-permute-start = (bf16[384,256]{1,0:T(8,128)(2,1)}, bf16[384,256]{1,0:T(8,128)(2,1)S(1)}, u32[]{:S(2)}, u32[]{:S(2)}) collective-permute-start(bf16[384,256]{1,0:T(8,128)(2,1)} %get-tuple-element.12), channel_id=1, source_target_pairs={{0,1},{1,2},{2,3},{3,4},{4,5},{5,6},{6,7},{7,8},{8,9},{9,10},{10,1... | collective-permute-start | bytes 589832 | tf_op jit(solution)/shard_map/ppermute | solution.py:294
  5.4 11.4 %collective-permute-start.1 = (bf16[384,256]{1,0:T(8,128)(2,1)}, bf16[384,256]{1,0:T(8,128)(2,1)S(1)}, u32[]{:S(2)}, u32[]{:S(2)}) collective-permute-start(bf16[384,256]{1,0:T(8,128)(2,1)} %get-tuple-element.13), channel_id=1, source_target_pairs={{0,127},{1,0},{2,1},{3,2},{4,3},{5,4},{6,5},{7,6},{8,7},{9,8},{10,... | collective-permute-start | bytes 589832 | tf_op jit(solution)/shard_map/ppermute | solution.py:294
  12.9 12.8 %collective-permute-start.3 = (bf16[512,256]{1,0:T(8,128)(2,1)S(1)}, bf16[512,256]{1,0:T(8,128)(2,1)S(1)}, u32[]{:S(2)}, u32[]{:S(2)}) collective-permute-start(bf16[512,256]{1,0:T(8,128)(2,1)S(1)} %get-tuple-element.23), channel_id=1, source_target_pairs={{0,1},{1,2},{2,3},{3,4},{4,5},{5,6},{6,7},{7,8},{8,9},{9,10},{10,1... | collective-permute-start | bytes 786440 | tf_op jit(solution)/shard_map/ppermute | solution.py:294
  16.9 0.7 copy-start.6
  17.6 0.7 copy-start.8
  22.0 13.5 %collective-permute-start.2 = (bf16[512,256]{1,0:T(8,128)(2,1)}, bf16[512,256]{1,0:T(8,128)(2,1)S(1)}, u32[]{:S(2)}, u32[]{:S(2)}) collective-permute-start(bf16[512,256]{1,0:T(8,128)(2,1)} %get-tuple-element.14), channel_id=1, source_target_pairs={{0,1},{1,2},{2,3},{3,4},{4,5},{5,6},{6,7},{7,8},{8,9},{9,10},{10,1... | collective-permute-start | bytes 786440 | tf_op jit(solution)/shard_map/ppermute | solution.py:294
  25.7 9.9 %copy-start.2 = (bf16[512,256]{1,0:T(8,128)(2,1)}, bf16[512,256]{1,0:T(8,128)(2,1)S(1)}, u32[]{:S(2)}) copy-start(bf16[512,256]{1,0:T(8,128)(2,1)S(1)} %collective-permute-done.3.cot_lo) | copy-start | bytes 786436
  35.6 0.7 copy-start.3
  88.6 6.7 %collective-permute-start.5 = (bf16[512,256]{1,0:T(8,128)(2,1)}, bf16[512,256]{1,0:T(8,128)(2,1)S(1)}, u32[]{:S(2)}, u32[]{:S(2)}) collective-permute-start(bf16[512,256]{1,0:T(8,128)(2,1)} %get-tuple-element.19), channel_id=1, source_target_pairs={{0,127},{1,0},{2,1},{3,2},{4,3},{5,4},{6,5},{7,6},{8,7},{9,8},{10,... | collective-permute-start | bytes 786440 | tf_op jit(solution)/shard_map/ppermute | solution.py:294
  89.0 20.5 %collective-permute-start.4 = (bf16[512,256]{1,0:T(8,128)(2,1)}, bf16[512,256]{1,0:T(8,128)(2,1)S(1)}, u32[]{:S(2)}, u32[]{:S(2)}) collective-permute-start(bf16[512,256]{1,0:T(8,128)(2,1)} %get-tuple-element.17), channel_id=1, source_target_pairs={{0,127},{1,0},{2,1},{3,2},{4,3},{5,4},{6,5},{7,6},{8,7},{9,8},{10,... | collective-permute-start | bytes 786440 | tf_op jit(solution)/shard_map/ppermute | solution.py:294
  95.2 0.7 copy-start
  99.0 12.2 %collective-permute-start.6 = (bf16[384,256]{1,0:T(8,128)(2,1)}, bf16[384,256]{1,0:T(8,128)(2,1)S(1)}, u32[]{:S(2)}, u32[]{:S(2)}) collective-permute-start(bf16[384,256]{1,0:T(8,128)(2,1)} %get-tuple-element.20), channel_id=1, source_target_pairs={{0,1},{1,2},{2,3},{3,4},{4,5},{5,6},{6,7},{7,8},{8,9},{9,10},{10,1... | collective-permute-start | bytes 589832 | tf_op jit(solution)/shard_map/ppermute | solution.py:294
  99.1 10.4 %copy-start.4 = (bf16[512,256]{1,0:T(8,128)(2,1)S(1)}, bf16[512,256]{1,0:T(8,128)(2,1)}, u32[]{:S(2)}) copy-start(bf16[512,256]{1,0:T(8,128)(2,1)} %get-tuple-element.16) | copy-start | bytes 786436
  99.1 12.1 %collective-permute-start.7 = (bf16[384,256]{1,0:T(8,128)(2,1)}, bf16[384,256]{1,0:T(8,128)(2,1)S(1)}, u32[]{:S(2)}, u32[]{:S(2)}) collective-permute-start(bf16[384,256]{1,0:T(8,128)(2,1)} %get-tuple-element.21), channel_id=1, source_target_pairs={{0,127},{1,0},{2,1},{3,2},{4,3},{5,4},{6,5},{7,6},{8,7},{9,8},{10,... | collective-permute-start | bytes 589832 | tf_op jit(solution)/shard_map/ppermute | solution.py:294
  111.2 0.7 copy-start.5
  111.9 0.7 copy-start.7

commit v3 on v1

--- a/solution.py
+++ b/solution.py
@@ -101,20 +101,16 @@
     )
 
 
-def main_kernel(
-    ord_lo, ord_hi, cot_lo, cot_hi, gain1, wqkv, wproj, gain2, wfc1, wfc2,
-    out_lo, out_hi, grad_lo, grad_hi,
-    e_scr, x_scr, kn, vn, qt, kt, vt, ot, inv_scr, amp_scr, gt, mix_grad, dt,
-):
-    x_scr[:HALF] = ord_lo[...]
-    x_scr[HALF:] = ord_hi[...]
-
-    vt[...] = jnp.full((H, 2 * D, N), VSCALE, bf16)
-    for b in range(N // ROWS):
+def front(rows, gain, weight):
+    unit, _ = normalize(rows.astype(f32))
+    return dg((unit * gain).astype(bf16), weight, 1, 0).astype(bf16)
+
+
+def split_qkv(rows_ref, gain, weight, kn, vn, qt, kt, vt):
+    vt[...] = jnp.full(vt.shape, VSCALE, bf16)
+    for b in range(HALF // ROWS):
         sl = slice(b * ROWS, (b + 1) * ROWS)
-        unit, _ = normalize(x_scr[sl].astype(f32))
-        normed = (unit * gain1[...]).astype(bf16)
-        qkv = dg(normed, wqkv[...], 1, 0).astype(bf16)
+        qkv = front(rows_ref[sl], gain[...], weight[...])
         kn[0, sl] = qkv[:, 256:384]
         kn[1, sl] = qkv[:, 384:512]
         vn[0, sl] = qkv[:, 512:640]
@@ -124,16 +120,57 @@
         kt[:, sl] = flipped[256:512]
         vt[:, :D, sl] = flipped[512:].reshape(H, D, ROWS) * bf16(VSCALE)
 
-    lane_head = lax.broadcasted_iota(jnp.int32, (N, 128), 1) // D
+
+def front_back(dt, rows_ref, mix_grad, gain, weight, out):
+    for b in range(HALF // ROWS):
+        sl = slice(b * ROWS, (b + 1) * ROWS)
+        grad_normed = dg(jnp.transpose(dt[:, sl]), weight[...], 1, 1)
+        unit, scale = normalize(rows_ref[sl].astype(f32))
+        grad = mix_grad[sl] + normalize_back(grad_normed * gain[...], unit, scale)
+        out[sl] = grad.astype(bf16)
+
+
+def head_mask(h):
+    return lax.broadcasted_iota(jnp.int32, (HALF, 128), 1) // D == h % 8
+
+
+def weigh(keys, queries):
+    return jnp.exp2(dg(keys, queries, 1, 0) * SCORE).astype(bf16)
+
+
+def before_kernel(ord_hi, wqkv, gain1, kn, vn, qt, kt, vt, e_hh, sums_hh):
+    split_qkv(ord_hi, gain1, wqkv, kn, vn, qt, kt, vt)
+
+    def one_head(h, carry):
+        block = h // 8
+        keys = jnp.where(head_mask(h), kn[block], bf16(0))
+        weights = weigh(keys, qt[pl.ds(block * 128, 128)])
+        e_hh[h] = weights
+        sums_hh[h] = dg(vt[h], weights, 1, 0)
+        return carry
+
+    lax.fori_loop(0, H, one_head, 0)
+
+
+def main_kernel(
+    ord_lo, ord_hi, cot_lo, cot_hi, wqkv, wproj, wfc1, wfc2, gain1, gain2,
+    kn_hi, vn_hi, qt_hi, kt_hi, vt_hi, sums_hh,
+    out_lo, out_hi, grad_lo, gt_hi, inner_hi, amp_hi, part, mix_hi,
+    e_l, e_hl, kn, vn, qt, kt, vt, ot, inv_scr, amp_scr, gt, mix_lo, dt, p_t, s_t, ph_t, sh_t,
+):
+    split_qkv(ord_lo, gain1, wqkv, kn, vn, qt.at[:, :HALF], kt, vt)
+    qt[:, HALF:] = qt_hi[...]
 
     def forward_head(h, carry):
         block = h // 8
-        mask = lane_head == h % 8
-        keys = jnp.where(mask, kn[block], bf16(0))
-        scores = dg(keys, qt[pl.ds(block * 128, 128)], 1, 0)
-        weights = jnp.exp2(scores * SCORE).astype(bf16)
-        e_scr[h] = weights
+        mask = head_mask(h)
+        lanes = pl.ds(block * 128, 128)
+        weights = weigh(jnp.where(mask, kn[block], bf16(0)), qt[lanes])
+        e_l[h] = weights
+        side = weigh(jnp.where(mask, kn_hi[block], bf16(0)), qt[lanes, :HALF])
+        e_hl[h] = side
         sums = dg(vt[h], weights, 1, 0)
+        sums += jnp.concatenate([dg(vt_hi[h], side, 1, 0), sums_hh[h]], axis=1)
         total = sums[D : D + 1]
         amp = jnp.where(total >= 2.0**40, 2.0**-80, jnp.where(total < 2.0**-40, 2.0**80, 1.0))
         inverse = 1.0 / (total * amp)
@@ -149,7 +186,7 @@
         half = b // 2
         hs = slice((b % 2) * ROWS, (b % 2 + 1) * ROWS)
         attention = jnp.transpose(ot[:, sl].astype(bf16))
-        mixed = x_scr[sl].astype(f32) + dg(attention, wproj[...], 1, 0)
+        mixed = (ord_lo, ord_hi)[half][hs].astype(f32) + dg(attention, wproj[...], 1, 0)
         unit, scale = normalize(mixed)
         normed = (unit * gain2[...]).astype(bf16)
         pre = dg(normed, wfc1[...], 1, 0)
@@ -162,49 +199,91 @@
         grad_pre = (grad_act * (cdf + pre * density)).astype(bf16)
         grad_normed = dg(grad_pre, wfc1[...], 1, 1)
         grad_mixed = cot.astype(f32) + normalize_back(grad_normed * gain2[...], unit, scale)
-        mix_grad[sl] = grad_mixed
+        (mix_lo, mix_hi)[half][hs] = grad_mixed
         grad_att = dg(grad_mixed.astype(bf16), wproj[...], 1, 1).astype(bf16)
         gt[:, sl] = (jnp.transpose(grad_att).astype(f32) * inv_scr[:, sl]).astype(bf16)
+
+    gt_hi[...] = gt[:, HALF:]
+    amp_hi[...] = amp_scr[:, :, HALF:]
 
     def backward_head(h, carry):
         block = h // 8
         rows = pl.ds(h * D, D)
-        mask = lane_head == h % 8
-        values = jnp.where(mask, vn[block], bf16(0))
+        rows_k = pl.ds(256 + h * D, D)
+        rows_v = pl.ds(512 + h * D, D)
+        lanes = pl.ds(block * 128, 128)
+        mask = head_mask(h)
         grads = gt[rows]
         inner = jnp.sum(grads.astype(f32) * ot[rows], axis=0, keepdims=True)
-        probs = e_scr[h] * amp_scr[h, :1]
-        dt[pl.ds(512 + h * D, D)] = dg(grads, probs, 1, 1).astype(bf16)
-        grad_probs = dg(values, gt[pl.ds(block * 128, 128)], 1, 0) - inner
-        grad_scores = probs * grad_probs.astype(bf16)
-        dt[rows] = (dg(kt[rows], grad_scores, 1, 0) * 0.25).astype(bf16)
-        dt[pl.ds(256 + h * D, D)] = (dg(qt[rows], grad_scores, 1, 1) * 0.25).astype(bf16)
+        inner_hi[h] = jnp.broadcast_to(inner[:, HALF:], (8, HALF))
+        amp = amp_scr[h, :1]
+        probs = e_l[h] * amp
+        p_t[...] = jnp.transpose(probs)
+        side = e_hl[h] * amp[:, :HALF]
+        ph_t[...] = jnp.transpose(side)
+        values = jnp.where(mask, vn[block], bf16(0))
+        scores = probs * (dg(values, gt[lanes], 1, 0) - inner).astype(bf16)
+        grad_q = dg(kt[rows], scores, 1, 0)
+        values = jnp.where(mask, vn_hi[block], bf16(0))
+        side_scores = side * (dg(values, gt[lanes, :HALF], 1, 0) - inner[:, :HALF]).astype(bf16)
+        s_t[...] = jnp.transpose(scores)
+        sh_t[...] = jnp.transpose(side_scores)
+        dt[rows] = ((grad_q[:, :HALF] + dg(kt_hi[rows], side_scores, 1, 0)) * 0.25).astype(bf16)
+        part[rows] = grad_q[:, HALF:]
+        dt[rows_v] = dg(grads, p_t[...], 1, 0).astype(bf16)
+        part[rows_v] = dg(gt[rows, :HALF], ph_t[...], 1, 0)
+        dt[rows_k] = (dg(qt[rows], s_t[...], 1, 0) * 0.25).astype(bf16)
+        part[rows_k] = dg(qt[rows, :HALF], sh_t[...], 1, 0)
         return carry
 
     lax.fori_loop(0, H, backward_head, 0)
-
-    for b in range(N // ROWS):
-        sl = slice(b * ROWS, (b + 1) * ROWS)
-        half = b // 2
-        hs = slice((b % 2) * ROWS, (b % 2 + 1) * ROWS)
-        grad_qkv = jnp.transpose(dt[:, sl])
-        grad_normed = dg(grad_qkv, wqkv[...], 1, 1)
-        unit, scale = normalize(x_scr[sl].astype(f32))
-        grad = mix_grad[sl] + normalize_back(grad_normed * gain1[...], unit, scale)
-        (grad_lo, grad_hi)[half][hs] = grad.astype(bf16)
-
-
-PARAMS = pltpu.CompilerParams(vmem_limit_bytes=60 * 1024 * 1024)
-
-
-def call(kernel, outs, scratch=(), name=None):
+    front_back(dt, ord_lo, mix_lo, gain1, wqkv, grad_lo)
+
+
+def after_kernel(
+    ord_hi, wqkv, gain1, vn, qt, kt, e_hh, gt, inner_hi, amp_hi, part, mix_hi,
+    grad_hi, dt, p_t, s_t,
+):
+    def backward_head(h, carry):
+        block = h // 8
+        rows = pl.ds(h * D, D)
+        rows_k = pl.ds(256 + h * D, D)
+        rows_v = pl.ds(512 + h * D, D)
+        probs = e_hh[h] * amp_hi[h, :1]
+        p_t[...] = jnp.transpose(probs)
+        values = jnp.where(head_mask(h), vn[block], bf16(0))
+        inner = inner_hi[h][:1]
+        scores = probs * (dg(values, gt[pl.ds(block * 128, 128)], 1, 0) - inner).astype(bf16)
+        s_t[...] = jnp.transpose(scores)
+        dt[rows] = ((part[rows] + dg(kt[rows], scores, 1, 0)) * 0.25).astype(bf16)
+        dt[rows_v] = (part[rows_v] + dg(gt[rows], p_t[...], 1, 0)).astype(bf16)
+        dt[rows_k] = ((part[rows_k] + dg(qt[rows], s_t[...], 1, 0)) * 0.25).astype(bf16)
+        return carry
+
+    lax.fori_loop(0, H, backward_head, 0)
+    front_back(dt, ord_hi, mix_hi, gain1, wqkv, grad_hi)
+
+
+vm = pltpu.VMEM
+
+
+def chip(rows):
+    return pltpu.with_memory_space_constraint(rows, pltpu.VMEM)
+
+
+def call(kernel, operands, outs, scratch, name, limit=16):
+    space = pl.BlockSpec(memory_space=pltpu.VMEM)
     return pl.pallas_call(
         kernel,
-        out_shape=tuple(jax.ShapeDtypeStruct(s, bf16) for s in outs),
+        in_specs=[space] * len(operands),
+        out_specs=tuple([space] * len(outs)),
+        out_shape=tuple(
+            o if not isinstance(o, tuple) else jax.ShapeDtypeStruct(o, bf16) for o in outs
+        ),
         scratch_shapes=list(scratch),
-        compiler_params=PARAMS,
+        compiler_params=pltpu.CompilerParams(vmem_limit_bytes=limit << 20),
         name=name,
-    )
+    )(*operands)
 
 
 def shift(rows, step):
@@ -224,45 +303,70 @@
     gain1 = norm1_gain.reshape(1, C)
     gain2 = norm2_gain.reshape(1, C)
 
-    left, right = call(gather_kernel, [(CAP, C)] * 2, name="gather")(local, sender)
+    left, right = call(gather_kernel, [local, sender], [(CAP, C)] * 2, [], "gather")
     from_prev = shift(right, 1)
     from_next = shift(left, -1)
     cot_lo = shift(cot[HALF:], 1)
-    first, second = call(order_kernel, [(HALF, C)] * 2, name="order")(
-        local, from_prev, from_next, slot
+    ord_hi, second = call(
+        order_kernel,
+        [local, chip(from_prev), chip(from_next), slot],
+        [(HALF, C)] * 2,
+        [],
+        "order",
     )
     ord_lo = shift(second, 1)
-    vm = pltpu.VMEM
-    out_lo, out_hi, grad_lo, grad_hi = call(
+    natural = vm((2, HALF, 128), bf16)
+    flipped = vm((C, HALF), bf16)
+    valued = vm((H, 2 * D, HALF), bf16)
+    square = vm((H, HALF, HALF), bf16)
+    kn, vn, qt, kt, vt, e_hh, sums_hh = call(
+        before_kernel,
+        [ord_hi, qkv_weight, gain1],
+        [natural, natural, flipped, flipped, valued, square, vm((H, 2 * D, HALF), f32)],
+        [],
+        "before",
+        24,
+    )
+    out_lo, out_hi, grad_lo, gt_hi, inner_hi, amp_hi, part, mix_hi = call(
         main_kernel,
-        [(HALF, C)] * 4,
         [
-            vm((H, N, N), bf16),
-            vm((N, C), bf16),
-            vm((2, N, 128), bf16),
-            vm((2, N, 128), bf16),
-            vm((C, N), bf16),
-            vm((C, N), bf16),
-            vm((H, 2 * D, N), bf16),
-            vm((C, N), f32),
-            vm((C, N), f32),
-            vm((H, D, N), bf16),
-            vm((C, N), bf16),
-            vm((N, C), f32),
-            vm((3 * C, N), bf16),
+            chip(ord_lo), ord_hi, chip(cot_lo), cot[:HALF], qkv_weight, proj_weight,
+            fc1_weight, fc2_weight, gain1, gain2, kn, vn, qt, kt, vt, sums_hh,
         ],
-        name="block",
-    )(
-        ord_lo, first, cot_lo, cot[:HALF], gain1, qkv_weight, proj_weight, gain2,
-        fc1_weight, fc2_weight,
+        [
+            (HALF, C), (HALF, C), (HALF, C), flipped, vm((H, 8, HALF), f32),
+            vm((H, D, HALF), bf16), vm((3 * C, HALF), f32), vm((HALF, C), f32),
+        ],
+        [
+            vm((H, HALF, N), bf16), square, natural, natural, vm((C, N), bf16), flipped, valued,
+            vm((C, N), f32), vm((C, N), f32), vm((H, D, N), bf16), vm((C, N), bf16),
+            vm((HALF, C), f32), vm((3 * C, HALF), bf16), vm((N, HALF), bf16),
+            vm((N, HALF), bf16), vm((HALF, HALF), bf16), vm((HALF, HALF), bf16),
+        ],
+        "block",
+        40,
     )
     grad_second = shift(grad_lo, -1)
     out_second = shift(out_lo, -1)
-    to_prev, to_next = call(back_kernel, [(CAP, C)] * 2, name="back")(grad_hi, grad_second, slot)
+    (grad_hi,) = call(
+        after_kernel,
+        [
+            ord_hi, qkv_weight, gain1, vn, qt, kt, e_hh, gt_hi, inner_hi, amp_hi, part, mix_hi,
+        ],
+        [(HALF, C)],
+        [vm((3 * C, HALF), bf16), vm((HALF, HALF), bf16), vm((HALF, HALF), bf16)],
+        "after",
+        24,
+    )
+    to_prev, to_next = call(
+        back_kernel, [grad_hi, chip(grad_second), slot], [(CAP, C)] * 2, [], "back"
+    )
     back_left = shift(to_prev, -1)
     back_right = shift(to_next, 1)
-    (own,) = call(own_kernel, [(N, C)], name="own")(grad_hi, grad_second, slot)
-    (grad_points,) = call(final_kernel, [(N, C)], name="final")(own, back_right, back_left, sender)
+    (own,) = call(own_kernel, [grad_hi, chip(grad_second), slot], [(N, C)], [], "own")
+    (grad_points,) = call(
+        final_kernel, [own, chip(back_right), chip(back_left), sender], [(N, C)], [], "final"
+    )
     block_out = jnp.concatenate([out_hi, out_second], axis=0)
     return (block_out[None], grad_points[None])
 

time: 120 us -> 106 us (0.88)
  waiting for transfers between devices: 24.9 us -> 9.22 us
  Pallas kernels: 72.7 us -> 64.3 us
  local copies, waits for them, and re-layouts: 4.84 us -> 10.5 us
  starting transfers between devices: 15.6 us -> 19.5 us
    ppermute x8, waiting for transfers between devices: 24.9 us -> 9.22 us  [shift(): lax.ppermute(rows, axes, [(i, (i + step) % count) for i in range(count)])]
    pallas_call x6 -> x8, Pallas kernels: 72.7 us -> 64.3 us  [call(): pl.pallas_call(kernel, in_specs=[space] * len(operands), out_specs=tuple(...]
    unnamed x18 -> x28, local copies, waits for them, and re-layouts: 4.11 us -> 9.44 us
    ppermute x8, starting transfers between devices: 15.6 us -> 19.5 us  [shift(): lax.ppermute(rows, axes, [(i, (i + step) % count) for i in range(count)])]
  transfers between devices with their start and end apart: 8 -> 8, of which waited for: 5 -> 3; matrix products, arithmetic and copies ran while one was open for 1% -> 2% of each run, Pallas kernels for 7% -> 19%
where the time goes in v3:
time: 106 us; the launch traced here: 105 us
  Pallas kernels  64.3 us (61%)
  starting transfers between devices  19.5 us (18%)
  local copies, waits for them, and re-layouts  10.5 us (10%)
  waiting for transfers between devices  9.22 us (9%)
    pallas_call x8, Pallas kernels, call(): pl.pallas_call(kernel, in_specs=[space] * len(operands), out_specs=tuple(...  64.3 us
    ppermute x8, starting transfers between devices, shift(): lax.ppermute(rows, axes, [(i, (i + step) % count) for i in range(count)])  19.5 us
    unnamed x28, local copies, waits for them, and re-layouts  9.44 us
    ppermute x8, waiting for transfers between devices, shift(): lax.ppermute(rows, axes, [(i, (i + step) % count) for i in range(count)])  9.22 us
  transfers between devices with their start and end apart: 8, of which 3 were waited for; matrix products, arithmetic and copies ran while one was open for 2% of the time, Pallas kernels for 19%

profile of v3, /device:TPU:0, one launch (start us, length us, event | category | flops | bytes accessed | tf_op | source)
XLA Modules:
  0.0 105.2 jit_solution(4395258059267068113)
XLA Ops:
  0.7 1.0 copy-done.2
  1.7 0.7 copy-done.8
  2.4 0.6 gather.1
  3.0 1.7 %collective-permute-start = (bf16[384,256]{1,0:T(8,128)(2,1)S(1)}, bf16[384,256]{1,0:T(8,128)(2,1)S(1)}, u32[]{:S(2)}, u32[]{:S(2)}) collective-permute-start(bf16[384,256]{1,0:T(8,128)(2,1)S(1)} %get-tuple-element.23), channel_id=1, source_target_pairs={{0,1},{1,2},{2,3},{3,4},{4,5},{5,6},{6,7},{7,8},{8,9},{9,10},{10,1... | collective-permute-start | bytes 589832 | tf_op jit(solution)/shard_map/ppermute | solution.py:292
  4.7 6.7 %collective-permute-start.1 = (bf16[384,256]{1,0:T(8,128)(2,1)S(1)}, bf16[384,256]{1,0:T(8,128)(2,1)S(1)}, u32[]{:S(2)}, u32[]{:S(2)}) collective-permute-start(bf16[384,256]{1,0:T(8,128)(2,1)S(1)} %get-tuple-element.24), channel_id=1, source_target_pairs={{0,127},{1,0},{2,1},{3,2},{4,3},{5,4},{6,5},{7,6},{8,7},{9,8},{10,... | collective-permute-start | bytes 589832 | tf_op jit(solution)/shard_map/ppermute | solution.py:292
  11.4 1.1 %slice_bitcast_fusion = (bf16[512,256]{1,0:T(8,128)(2,1)S(1)}, bf16[512,256]{1,0:T(8,128)(2,1)S(1)}) fusion(bf16[1,1024,256]{2,1,0:T(8,128)(2,1)} %param.19), kind=kLoop, calls=%fused_computation.1 | loop fusion | bytes 1048576 | tf_op jit(solution)/shard_map/slice | solution.py:333
  12.5 0.1 collective-permute-start.3
  12.5 3.4 %collective-permute-done.from_prev = bf16[384,256]{1,0:T(8,128)(2,1)S(1)} collective-permute-done((bf16[384,256]{1,0:T(8,128)(2,1)S(1)}, bf16[384,256]{1,0:T(8,128)(2,1)S(1)}, u32[]{:S(2)}, u32[]{:S(2)}) %collective-permute-start) | collective-permute-done | bytes 196640 | tf_op jit(solution)/shard_map/ppermute | solution.py:292
  15.9 0.7 copy-done.6
  16.6 1.3 %order.1 = (bf16[512,256]{1,0:T(8,128)(2,1)S(1)}, bf16[512,256]{1,0:T(8,128)(2,1)S(1)}) custom-call(bf16[1024,256]{1,0:T(8,128)(2,1)S(1)} %bitcast.12, bf16[384,256]{1,0:T(8,128)(2,1)S(1)} %collective-permute-done.from_prev, bf16[384,256]{1,0:T(8,128)(2,1)S(1)} %collective-permute-done.1.from_next, s32[1,1024]{1,0:T(1,128)S(1)} %copy-done.6), custom_call_target="tpu_custom_call" | custom-call | tf_op jit(solution)/shard_map/order/pallas_call | solution.py:276
  17.9 0.1 collective-permute-start.2
  18.0 1.0 copy-done
  19.0 0.7 copy-done.10
  19.7 7.5 %before.1 = (bf16[2,512,128]{2,1,0:T(8,128)(2,1)S(1)}, bf16[2,512,128]{2,1,0:T(8,128)(2,1)S(1)}, bf16[256,512]{1,0:T(8,128)(2,1)S(1)}, bf16[256,512]{1,0:T(8,128...) custom-call(bf16[512,256]{1,0:T(8,128)(2,1)S(1)} %get-tuple-element.26.o, ...), custom_call_target="tpu_custom_call" | custom-call | tf_op jit(solution)/shard_map/before/pallas_call | solution.py:276
  27.2 3.9 %collective-permute-done.2.ord_lo = bf16[512,256]{1,0:T(8,128)(2,1)S(1)} collective-permute-done((bf16[512,256]{1,0:T(8,128)(2,1)S(1)}, bf16[512,256]{1,0:T(8,128)(2,1)S(1)}, u32[]{:S(2)}, u32[]{:S(2)}) %collective-permute-start.2) | collective-permute-done | bytes 262176 | tf_op jit(solution)/shard_map/ppermute | solution.py:292
  31.1 1.0 copy-done.1
  32.1 1.0 copy-done.3
  33.1 1.0 copy-done.4
  34.1 0.9 copy-done.5
  35.1 0.7 copy-done.11
  35.7 0.7 copy-done.13
  36.4 42.4 %block.1 = (bf16[512,256]{1,0:T(8,128)(2,1)S(1)}, bf16[512,256]{1,0:T(8,128)(2,1)S(1)}, bf16[512,256]{1,0:T(8,128)(2,1)S(1)}, bf16[256,512]{1,0:T(8,128)(2,1)S(1...) custom-call(bf16[512,256]{1,0:T(8,128)(2,1)S(1)} %collective-permute, ...), custom_call_target="tpu_custom_call" | custom-call | tf_op jit(solution)/shard_map/block/pallas_call | solution.py:276
  78.8 3.5 %collective-permute-start.5 = (bf16[512,256]{1,0:T(8,128)(2,1)S(1)}, bf16[512,256]{1,0:T(8,128)(2,1)S(1)}, u32[]{:S(2)}, u32[]{:S(2)}) collective-permute-start(bf16[512,256]{1,0:T(8,128)(2,1)S(1)} %get-tuple-element.41), channel_id=1, source_target_pairs={{0,127},{1,0},{2,1},{3,2},{4,3},{5,4},{6,5},{7,6},{8,7},{9,8},{10,... | collective-permute-start | bytes 786440 | tf_op jit(solution)/shard_map/ppermute | solution.py:292
  82.3 0.3 collective-permute-start.4
  82.5 9.8 %after.1.first = bf16[512,256]{1,0:T(8,128)(2,1)S(1)} custom-call(bf16[512,256]{1,0:T(8,128)(2,1)S(1)} %get-tuple-element.26.ord_hi, bf16[256,768]{1,0:T(8,128)(2,1)S(1)} %copy-done.1, f32[1,256]{1,0:T(1,128)S(1)} %bitcast.17, bf16[2,512,128]{2,1,0:T(8,128)(2,1)S(1)} %get-tuple-element.28.vn_hi.vn, bf16[256,512]{1,0:T(8,128)(2,1)S(1)} %get-tuple-element.29.qt_hi.qt, ...), custom_call_target="tpu_custom_call" | custom-call | tf_op jit(solution)/shard_map/after/pallas_call | solution.py:276
  92.3 0.6 back.1
  92.9 1.8 %collective-permute-start.6 = (bf16[384,256]{1,0:T(8,128)(2,1)S(1)}, bf16[384,256]{1,0:T(8,128)(2,1)S(1)}, u32[]{:S(2)}, u32[]{:S(2)}) collective-permute-start(bf16[384,256]{1,0:T(8,128)(2,1)S(1)} %get-tuple-element.42), channel_id=1, source_target_pairs={{0,1},{1,2},{2,3},{3,4},{4,5},{5,6},{6,7},{7,8},{8,9},{9,10},{10,1... | collective-permute-start | bytes 589832 | tf_op jit(solution)/shard_map/ppermute | solution.py:292
  94.7 5.4 %collective-permute-start.7 = (bf16[384,256]{1,0:T(8,128)(2,1)S(1)}, bf16[384,256]{1,0:T(8,128)(2,1)S(1)}, u32[]{:S(2)}, u32[]{:S(2)}) collective-permute-start(bf16[384,256]{1,0:T(8,128)(2,1)S(1)} %get-tuple-element.43), channel_id=1, source_target_pairs={{0,127},{1,0},{2,1},{3,2},{4,3},{5,4},{6,5},{7,6},{8,7},{9,8},{10,... | collective-permute-start | bytes 589832 | tf_op jit(solution)/shard_map/ppermute | solution.py:292
  100.1 0.7 own.1
  100.9 0.8 maximum_bitcast_fusion
  101.7 2.0 %collective-permute-done.6.left = bf16[384,256]{1,0:T(8,128)(2,1)S(1)} collective-permute-done((bf16[384,256]{1,0:T(8,128)(2,1)S(1)}, bf16[384,256]{1,0:T(8,128)(2,1)S(1)}, u32[]{:S(2)}, u32[]{:S(2)}) %collective-permute-start.6) | collective-permute-done | bytes 196640 | tf_op jit(solution)/shard_map/ppermute | solution.py:292
  103.7 1.5 %final.1 = bf16[1024,256]{1,0:T(8,128)(2,1)} custom-call(bf16[1024,256]{1,0:T(8,128)(2,1)S(1)} %own.1, bf16[384,256]{1,0:T(8,128)(2,1)S(1)} %collective-permute-done.6.left, bf16[384,256]{1,0:T(8,128)(2,1)S(1)} %collective-permute-done.7.right, s32[1,768]{1,0:T(1,128)S(1)} %bitcast.14), custom_call_target="tpu_custom_call" | custom-call | tf_op jit(solution)/shard_map/final/pallas_call | solution.py:276
  (22 shorter events, 0.0 us)
Async XLA Ops:
  0.6 81.9 %copy-start.12 = (f32[256]{0:T(256)S(1)}, f32[256]{0:T(256)}, u32[]{:S(2)}) copy-start(f32[256]{0:T(256)} %param.13) | copy-start | bytes 3076
  0.6 1.0 copy-start.2
  1.7 0.7 copy-start.8
  3.0 12.9 %collective-permute-start = (bf16[384,256]{1,0:T(8,128)(2,1)S(1)}, bf16[384,256]{1,0:T(8,128)(2,1)S(1)}, u32[]{:S(2)}, u32[]{:S(2)}) collective-permute-start(bf16[384,256]{1,0:T(8,128)(2,1)S(1)} %get-tuple-element.23), channel_id=1, source_target_pairs={{0,1},{1,2},{2,3},{3,4},{4,5},{5,6},{6,7},{7,8},{8,9},{9,10},{10,1... | collective-permute-start | bytes 589832 | tf_op jit(solution)/shard_map/ppermute | solution.py:292
  4.7 11.2 %collective-permute-start.1 = (bf16[384,256]{1,0:T(8,128)(2,1)S(1)}, bf16[384,256]{1,0:T(8,128)(2,1)S(1)}, u32[]{:S(2)}, u32[]{:S(2)}) collective-permute-start(bf16[384,256]{1,0:T(8,128)(2,1)S(1)} %get-tuple-element.24), channel_id=1, source_target_pairs={{0,127},{1,0},{2,1},{3,2},{4,3},{5,4},{6,5},{7,6},{8,7},{9,8},{10,... | collective-permute-start | bytes 589832 | tf_op jit(solution)/shard_map/ppermute | solution.py:292
  12.5 14.7 %collective-permute-start.3 = (bf16[512,256]{1,0:T(8,128)(2,1)S(1)}, bf16[512,256]{1,0:T(8,128)(2,1)S(1)}, u32[]{:S(2)}, u32[]{:S(2)}) collective-permute-start(bf16[512,256]{1,0:T(8,128)(2,1)S(1)} %get-tuple-element.45), channel_id=1, source_target_pairs={{0,1},{1,2},{2,3},{3,4},{4,5},{5,6},{6,7},{7,8},{8,9},{9,10},{10,1... | collective-permute-start | bytes 786440 | tf_op jit(solution)/shard_map/ppermute | solution.py:292
  15.9 0.7 copy-start.6
  17.9 13.2 %collective-permute-start.2 = (bf16[512,256]{1,0:T(8,128)(2,1)S(1)}, bf16[512,256]{1,0:T(8,128)(2,1)S(1)}, u32[]{:S(2)}, u32[]{:S(2)}) collective-permute-start(bf16[512,256]{1,0:T(8,128)(2,1)S(1)} %get-tuple-element.25), channel_id=1, source_target_pairs={{0,1},{1,2},{2,3},{3,4},{4,5},{5,6},{6,7},{7,8},{8,9},{9,10},{10,1... | collective-permute-start | bytes 786440 | tf_op jit(solution)/shard_map/ppermute | solution.py:292
  18.0 1.0 copy-start
  19.0 0.7 copy-start.10
  31.1 1.0 copy-start.1
  32.1 1.0 copy-start.3
  33.1 1.0 copy-start.4
  34.1 0.9 copy-start.5
  35.0 0.7 copy-start.11
  35.7 0.7 copy-start.13
  36.4 55.9 %copy-start.7 = (s32[1,1024]{1,0:T(1,128)S(1)}, s32[1,1024]{1,0:T(1,128)}, u32[]{:S(2)}) copy-start(s32[1,1024]{1,0:T(1,128)} %slot.5) | copy-start | bytes 12292
  78.8 24.9 %copy-start.9 = (s32[1,1,768]{2,1,0:T(1,128)S(1)}, s32[1,1,768]{2,1,0:T(1,128)}, u32[]{:S(2)}) copy-start(s32[1,1,768]{2,1,0:T(1,128)} %param.11) | copy-start | bytes 9220
  78.8 13.5 %collective-permute-start.5 = (bf16[512,256]{1,0:T(8,128)(2,1)S(1)}, bf16[512,256]{1,0:T(8,128)(2,1)S(1)}, u32[]{:S(2)}, u32[]{:S(2)}) collective-permute-start(bf16[512,256]{1,0:T(8,128)(2,1)S(1)} %get-tuple-element.41), channel_id=1, source_target_pairs={{0,127},{1,0},{2,1},{3,2},{4,3},{5,4},{6,5},{7,6},{8,7},{9,8},{10,... | collective-permute-start | bytes 786440 | tf_op jit(solution)/shard_map/ppermute | solution.py:292
  82.3 18.6 %collective-permute-start.4 = (bf16[512,256]{1,0:T(8,128)(2,1)S(1)}, bf16[512,256]{1,0:T(8,128)(2,1)S(1)}, u32[]{:S(2)}, u32[]{:S(2)}) collective-permute-start(bf16[512,256]{1,0:T(8,128)(2,1)S(1)} %get-tuple-element.34), channel_id=1, source_target_pairs={{0,127},{1,0},{2,1},{3,2},{4,3},{5,4},{6,5},{7,6},{8,7},{9,8},{10,... | collective-permute-start | bytes 786440 | tf_op jit(solution)/shard_map/ppermute | solution.py:292
  92.9 10.8 %collective-permute-start.6 = (bf16[384,256]{1,0:T(8,128)(2,1)S(1)}, bf16[384,256]{1,0:T(8,128)(2,1)S(1)}, u32[]{:S(2)}, u32[]{:S(2)}) collective-permute-start(bf16[384,256]{1,0:T(8,128)(2,1)S(1)} %get-tuple-element.42), channel_id=1, source_target_pairs={{0,1},{1,2},{2,3},{3,4},{4,5},{5,6},{6,7},{7,8},{8,9},{9,10},{10,1... | collective-permute-start | bytes 589832 | tf_op jit(solution)/shard_map/ppermute | solution.py:292
  94.7 8.9 %collective-permute-start.7 = (bf16[384,256]{1,0:T(8,128)(2,1)S(1)}, bf16[384,256]{1,0:T(8,128)(2,1)S(1)}, u32[]{:S(2)}, u32[]{:S(2)}) collective-permute-start(bf16[384,256]{1,0:T(8,128)(2,1)S(1)} %get-tuple-element.43), channel_id=1, source_target_pairs={{0,127},{1,0},{2,1},{3,2},{4,3},{5,4},{6,5},{7,6},{8,7},{9,8},{10,... | collective-permute-start | bytes 589832 | tf_op jit(solution)/shard_map/ppermute | solution.py:292

commit v4 on v3

--- a/solution.py
+++ b/solution.py
@@ -7,6 +7,7 @@
 from jax.experimental import pallas as pl
 from jax.experimental.pallas import tpu as pltpu
 from jax.sharding import PartitionSpec as P
+
 
 H = 16
 D = 16
@@ -20,6 +21,10 @@
 LOG2E = 1.4426950408889634
 SCORE = LOG2E / 4.0
 VSCALE = 2.0**-8
+UNROLL_BEFORE = 1
+UNROLL_FORWARD = 1
+UNROLL_BACKWARD = 1
+UNROLL_AFTER = 1
 
 bf16 = jnp.bfloat16
 f32 = jnp.float32
@@ -47,11 +52,32 @@
     return jnp.where(ids == row, 1.0, 0.0).astype(bf16)
 
 
-def gather_kernel(points, sender, left, right):
-    col = column(sender[...], 2 * CAP)
-    rows = dg(picks_from_column(col, 0, N), points[...], 1, 0).astype(bf16)
+def start_copies(pairs, sems):
+    copies = [pltpu.make_async_copy(src, dst, sems.at[i]) for i, (src, dst) in enumerate(pairs)]
+    for copy in copies:
+        copy.start()
+    return copies
+
+
+def gather_kernel(
+    points, sender, slot, wqkv, gain1, gain2,
+    left, right, points_v, sender_v, slot_v, wqkv_v, gain1_v, gain2_v, sems,
+):
+    copies = start_copies(
+        [
+            (sender, sender_v), (points, points_v), (slot, slot_v), (wqkv, wqkv_v),
+            (gain1, gain1_v), (gain2, gain2_v),
+        ],
+        sems,
+    )
+    copies[0].wait()
+    picks = picks_from_column(column(sender_v[...], 2 * CAP), 0, N)
+    copies[1].wait()
+    rows = dg(picks, points_v[...], 1, 0).astype(bf16)
     left[...] = rows[:CAP]
     right[...] = rows[CAP:]
+    for copy in copies[2:]:
+        copy.wait()
 
 
 def order_kernel(points, from_prev, from_next, slot, first, second):
@@ -138,7 +164,10 @@
     return jnp.exp2(dg(keys, queries, 1, 0) * SCORE).astype(bf16)
 
 
-def before_kernel(ord_hi, wqkv, gain1, kn, vn, qt, kt, vt, e_hh, sums_hh):
+def before_kernel(
+    ord_hi, wqkv, gain1, cot, kn, vn, qt, kt, vt, e_hh, sums_hh, cot_second, sems
+):
+    copies = start_copies([(cot.at[pl.ds(HALF, HALF)], cot_second)], sems)
     split_qkv(ord_hi, gain1, wqkv, kn, vn, qt, kt, vt)
 
     def one_head(h, carry):
@@ -149,15 +178,19 @@
         sums_hh[h] = dg(vt[h], weights, 1, 0)
         return carry
 
-    lax.fori_loop(0, H, one_head, 0)
-
-
-def main_kernel(
-    ord_lo, ord_hi, cot_lo, cot_hi, wqkv, wproj, wfc1, wfc2, gain1, gain2,
-    kn_hi, vn_hi, qt_hi, kt_hi, vt_hi, sums_hh,
-    out_lo, out_hi, grad_lo, gt_hi, inner_hi, amp_hi, part, mix_hi,
-    e_l, e_hl, kn, vn, qt, kt, vt, ot, inv_scr, amp_scr, gt, mix_lo, dt, p_t, s_t, ph_t, sh_t,
-):
+    lax.fori_loop(0, H, one_head, 0, unroll=UNROLL_BEFORE)
+    copies[0].wait()
+
+
+def forward_kernel(
+    ord_lo, wqkv, gain1, kn_hi, qt_hi, vt_hi, sums_hh, wproj_h, wfc1_h, wfc2_h, cot_h,
+    vn, qt, kt, e_l, e_hl, ot, inv_scr, amp_scr, wproj, wfc1, wfc2, cot_hi,
+    kn, vt, sems,
+):
+    copies = start_copies(
+        [(wproj_h, wproj), (wfc1_h, wfc1), (wfc2_h, wfc2), (cot_h.at[pl.ds(0, HALF)], cot_hi)],
+        sems,
+    )
     split_qkv(ord_lo, gain1, wqkv, kn, vn, qt.at[:, :HALF], kt, vt)
     qt[:, HALF:] = qt_hi[...]
 
@@ -179,8 +212,15 @@
         amp_scr[h] = jnp.broadcast_to(amp, (D, N)).astype(bf16)
         return carry
 
-    lax.fori_loop(0, H, forward_head, 0)
-
+    lax.fori_loop(0, H, forward_head, 0, unroll=UNROLL_FORWARD)
+    for copy in copies:
+        copy.wait()
+
+
+def middle_kernel(
+    ord_lo, ord_hi, cot_lo, cot_hi, wproj, wfc1, wfc2, gain2, ot, inv_scr,
+    out_lo, out_hi, gt, mix_lo, mix_hi,
+):
     for b in range(N // ROWS):
         sl = slice(b * ROWS, (b + 1) * ROWS)
         half = b // 2
@@ -203,9 +243,12 @@
         grad_att = dg(grad_mixed.astype(bf16), wproj[...], 1, 1).astype(bf16)
         gt[:, sl] = (jnp.transpose(grad_att).astype(f32) * inv_scr[:, sl]).astype(bf16)
 
-    gt_hi[...] = gt[:, HALF:]
-    amp_hi[...] = amp_scr[:, :, HALF:]
-
+
+def backward_kernel(
+    ord_lo, wqkv, gain1, vn, vn_hi, qt, kt, kt_hi, e_l, e_hl, ot, amp_scr, gt, mix_lo,
+    grad_lo, inner_hi, part,
+    dt, p_t, s_t, ph_t, sh_t,
+):
     def backward_head(h, carry):
         block = h // 8
         rows = pl.ds(h * D, D)
@@ -236,7 +279,7 @@
         part[rows_k] = dg(qt[rows, :HALF], sh_t[...], 1, 0)
         return carry
 
-    lax.fori_loop(0, H, backward_head, 0)
+    lax.fori_loop(0, H, backward_head, 0, unroll=UNROLL_BACKWARD)
     front_back(dt, ord_lo, mix_lo, gain1, wqkv, grad_lo)
 
 
@@ -249,18 +292,18 @@
         rows = pl.ds(h * D, D)
         rows_k = pl.ds(256 + h * D, D)
         rows_v = pl.ds(512 + h * D, D)
-        probs = e_hh[h] * amp_hi[h, :1]
+        probs = e_hh[h] * amp_hi[h, :1, HALF:]
         p_t[...] = jnp.transpose(probs)
         values = jnp.where(head_mask(h), vn[block], bf16(0))
         inner = inner_hi[h][:1]
-        scores = probs * (dg(values, gt[pl.ds(block * 128, 128)], 1, 0) - inner).astype(bf16)
+        scores = probs * (dg(values, gt[pl.ds(block * 128, 128), HALF:], 1, 0) - inner).astype(bf16)
         s_t[...] = jnp.transpose(scores)
         dt[rows] = ((part[rows] + dg(kt[rows], scores, 1, 0)) * 0.25).astype(bf16)
-        dt[rows_v] = (part[rows_v] + dg(gt[rows], p_t[...], 1, 0)).astype(bf16)
+        dt[rows_v] = (part[rows_v] + dg(gt[rows, HALF:], p_t[...], 1, 0)).astype(bf16)
         dt[rows_k] = ((part[rows_k] + dg(qt[rows], s_t[...], 1, 0)) * 0.25).astype(bf16)
         return carry
 
-    lax.fori_loop(0, H, backward_head, 0)
+    lax.fori_loop(0, H, backward_head, 0, unroll=UNROLL_AFTER)
     front_back(dt, ord_hi, mix_hi, gain1, wqkv, grad_hi)
 
 
@@ -271,19 +314,19 @@
     return pltpu.with_memory_space_constraint(rows, pltpu.VMEM)
 
 
-def call(kernel, operands, outs, scratch, name, limit=16):
-    space = pl.BlockSpec(memory_space=pltpu.VMEM)
+def call(kernel, operands, far, outs, scratch, limit, sems=0):
+    near = pl.BlockSpec(memory_space=pltpu.VMEM)
+    away = pl.BlockSpec(memory_space=pltpu.HBM)
     return pl.pallas_call(
         kernel,
-        in_specs=[space] * len(operands),
-        out_specs=tuple([space] * len(outs)),
+        in_specs=[near] * len(operands) + [away] * len(far),
+        out_specs=tuple([near] * len(outs)),
         out_shape=tuple(
             o if not isinstance(o, tuple) else jax.ShapeDtypeStruct(o, bf16) for o in outs
         ),
-        scratch_shapes=list(scratch),
+        scratch_shapes=list(scratch) + ([pltpu.SemaphoreType.DMA((sems,))] if sems else []),
         compiler_params=pltpu.CompilerParams(vmem_limit_bytes=limit << 20),
-        name=name,
-    )(*operands)
+    )(*operands, *[pltpu.with_memory_space_constraint(f, pltpu.HBM) for f in far])
 
 
 def shift(rows, step):
@@ -303,69 +346,103 @@
     gain1 = norm1_gain.reshape(1, C)
     gain2 = norm2_gain.reshape(1, C)
 
-    left, right = call(gather_kernel, [local, sender], [(CAP, C)] * 2, [], "gather")
+    half = vm((HALF, C), bf16)
+    half_f = vm((HALF, C), f32)
+    gain_v = vm((1, C), f32)
+    left, right, points_v, sender_v, slot_v, wqkv, gain1, gain2 = call(
+        gather_kernel,
+        [],
+        [local, sender, slot, qkv_weight, gain1, gain2],
+        [
+            (CAP, C), (CAP, C), vm((N, C), bf16), vm((1, 2 * CAP), jnp.int32),
+            vm((1, N), jnp.int32), vm((C, 3 * C), bf16), gain_v, gain_v,
+        ],
+        [],
+        6,
+        6,
+    )
     from_prev = shift(right, 1)
     from_next = shift(left, -1)
-    cot_lo = shift(cot[HALF:], 1)
     ord_hi, second = call(
         order_kernel,
-        [local, chip(from_prev), chip(from_next), slot],
-        [(HALF, C)] * 2,
-        [],
-        "order",
+        [points_v, chip(from_prev), chip(from_next), slot_v],
+        [],
+        [half, (HALF, C)],
+        [],
+        8,
     )
     ord_lo = shift(second, 1)
     natural = vm((2, HALF, 128), bf16)
     flipped = vm((C, HALF), bf16)
+    wide = vm((C, N), bf16)
+    wide_f = vm((C, N), f32)
     valued = vm((H, 2 * D, HALF), bf16)
     square = vm((H, HALF, HALF), bf16)
-    kn, vn, qt, kt, vt, e_hh, sums_hh = call(
+    tall = vm((N, HALF), bf16)
+    tile = vm((HALF, HALF), bf16)
+    kn_hi, vn_hi, qt_hi, kt_hi, vt_hi, e_hh, sums_hh, cot_second = call(
         before_kernel,
-        [ord_hi, qkv_weight, gain1],
-        [natural, natural, flipped, flipped, valued, square, vm((H, 2 * D, HALF), f32)],
-        [],
-        "before",
-        24,
-    )
-    out_lo, out_hi, grad_lo, gt_hi, inner_hi, amp_hi, part, mix_hi = call(
-        main_kernel,
+        [ord_hi, wqkv, gain1],
+        [cot],
         [
-            chip(ord_lo), ord_hi, chip(cot_lo), cot[:HALF], qkv_weight, proj_weight,
-            fc1_weight, fc2_weight, gain1, gain2, kn, vn, qt, kt, vt, sums_hh,
+            natural, natural, flipped, flipped, valued, square, vm((H, 2 * D, HALF), f32),
+            (HALF, C),
         ],
+        [],
+        6,
+        1,
+    )
+    cot_lo = shift(cot_second, 1)
+    vn, qt, kt, e_l, e_hl, ot, inv, amp, wproj, wfc1, wfc2, cot_hi = call(
+        forward_kernel,
+        [chip(ord_lo), wqkv, gain1, kn_hi, qt_hi, vt_hi, sums_hh],
+        [proj_weight, fc1_weight, fc2_weight, cot],
         [
-            (HALF, C), (HALF, C), (HALF, C), flipped, vm((H, 8, HALF), f32),
-            vm((H, D, HALF), bf16), vm((3 * C, HALF), f32), vm((HALF, C), f32),
+            natural, wide, flipped, vm((H, HALF, N), bf16), square, wide_f, wide_f,
+            vm((H, D, N), bf16), vm((C, C), bf16), vm((C, FF), bf16), vm((FF, C), bf16), half,
         ],
+        [natural, valued],
+        9,
+        4,
+    )
+    out_lo, out_hi, gt, mix_lo, mix_hi = call(
+        middle_kernel,
+        [chip(ord_lo), ord_hi, chip(cot_lo), cot_hi, wproj, wfc1, wfc2, gain2, ot, inv],
+        [],
+        [(HALF, C), (HALF, C), wide, half_f, half_f],
+        [],
+        12,
+    )
+    out_second = shift(out_lo, -1)
+    back = functools.partial(
+        call,
+        backward_kernel,
         [
-            vm((H, HALF, N), bf16), square, natural, natural, vm((C, N), bf16), flipped, valued,
-            vm((C, N), f32), vm((C, N), f32), vm((H, D, N), bf16), vm((C, N), bf16),
-            vm((HALF, C), f32), vm((3 * C, HALF), bf16), vm((N, HALF), bf16),
-            vm((N, HALF), bf16), vm((HALF, HALF), bf16), vm((HALF, HALF), bf16),
+            chip(ord_lo), wqkv, gain1, vn, vn_hi, qt, kt, kt_hi, chip(e_l), chip(e_hl), ot, amp, gt, mix_lo,
         ],
-        "block",
-        40,
-    )
+        [],
+        [(HALF, C), vm((H, 8, HALF), f32), vm((3 * C, HALF), f32)],
+        [vm((3 * C, HALF), bf16), tall, tall, tile, tile],
+        9,
+    )
+    grad_lo, inner_hi, part = back()
     grad_second = shift(grad_lo, -1)
-    out_second = shift(out_lo, -1)
     (grad_hi,) = call(
         after_kernel,
-        [
-            ord_hi, qkv_weight, gain1, vn, qt, kt, e_hh, gt_hi, inner_hi, amp_hi, part, mix_hi,
-        ],
-        [(HALF, C)],
-        [vm((3 * C, HALF), bf16), vm((HALF, HALF), bf16), vm((HALF, HALF), bf16)],
-        "after",
-        24,
+        [ord_hi, wqkv, gain1, vn_hi, qt_hi, kt_hi, chip(e_hh), gt, inner_hi, amp, part, mix_hi],
+        [],
+        [half],
+        [vm((3 * C, HALF), bf16), tile, tile],
+        6,
     )
     to_prev, to_next = call(
-        back_kernel, [grad_hi, chip(grad_second), slot], [(CAP, C)] * 2, [], "back"
+        back_kernel, [grad_hi, chip(grad_second), slot_v], [], [(CAP, C)] * 2, [], 6
     )
     back_left = shift(to_prev, -1)
     back_right = shift(to_next, 1)
-    (own,) = call(own_kernel, [grad_hi, chip(grad_second), slot], [(N, C)], [], "own")
+    (own,) = call(own_kernel, [grad_hi, chip(grad_second), slot_v], [], [vm((N, C), bf16)], [], 6)
     (grad_points,) = call(
-        final_kernel, [own, chip(back_right), chip(back_left), sender], [(N, C)], [], "final"
+        final_kernel, [own, chip(back_right), chip(back_left), sender_v], [], [(N, C)], [], 6
     )
     block_out = jnp.concatenate([out_hi, out_second], axis=0)
     return (block_out[None], grad_points[None])
@@ -374,6 +451,7 @@
 def solution(mesh):
     rows = P(None, ("gx", "gy"), None)
     in_specs = (rows, rows, P(None, ("gx", "gy")), P(), P(), P(), P(), P(), P(), rows)
+
     return jax.shard_map(
         shards, mesh=mesh, in_specs=in_specs, out_specs=(rows, rows), check_vma=False
     )

time: 106 us -> 98.4 us (0.928)
  local copies, waits for them, and re-layouts: 10.5 us -> 0 us
  waiting for transfers between devices: 9.22 us -> 11.6 us
  Pallas kernels: 64.3 us -> 65.7 us
    unnamed x28 -> x0, local copies, waits for them, and re-layouts: 9.44 us -> none
    ppermute x8, waiting for transfers between devices: 9.22 us -> 11.6 us  [shift(): lax.ppermute(rows, axes, [(i, (i + step) % count) for i in range(count)])]
    pallas_call x8 -> x10, Pallas kernels: 64.3 us -> 65.7 us  [call(): pl.pallas_call(kernel, in_specs=[near] * len(operands) + [away] * len(far...]
    slice x1 -> x0, local copies, waits for them, and re-layouts: 1.06 us -> none  [shards(): cot[:HALF]]
  transfers between devices with their start and end apart: 8 -> 8, of which waited for: 3 -> 3; matrix products, arithmetic and copies ran while one was open for 2% -> 1% of each run, Pallas kernels for 19% -> 34%
where the time goes in v4:
time: 98.4 us; the launch traced here: 98.3 us
  Pallas kernels  65.7 us (67%)
  starting transfers between devices  19.4 us (20%)
  waiting for transfers between devices  11.6 us (12%)
    pallas_call x10, Pallas kernels, call(): pl.pallas_call(kernel, in_specs=[near] * len(operands) + [away] * len(far...  65.7 us
    ppermute x8, starting transfers between devices, shift(): lax.ppermute(rows, axes, [(i, (i + step) % count) for i in range(count)])  19.4 us
    ppermute x8, waiting for transfers between devices, shift(): lax.ppermute(rows, axes, [(i, (i + step) % count) for i in range(count)])  11.6 us
  transfers between devices with their start and end apart: 8, of which 3 were waited for; matrix products, arithmetic and copies ran while one was open for 1% of the time, Pallas kernels for 34%

profile of v4, /device:TPU:0, one launch (start us, length us, event | category | flops | bytes accessed | tf_op | source)
XLA Modules:
  0.0 98.3 jit_solution(13778492124165797941)
XLA Ops:
  0.6 1.7 %shard_map.113 = (bf16[384,256]{1,0:T(8,128)(2,1)S(1)}, bf16[384,256]{1,0:T(8,128)(2,1)S(1)}, bf16[1024,256]{1,0:T(8,128)(2,1)S(1)}, s32[1,768]{1,0:T(1,128)S(1)...) custom-call(bf16[1024,256]{1,0:T(8,128)(2,1)} %bitcast.11, ...), custom_call_target="tpu_custom_call" | custom-call | tf_op jit(solution)/shard_map/pallas_call | solution.py:320
  2.4 1.7 %collective-permute-start = (bf16[384,256]{1,0:T(8,128)(2,1)S(1)}, bf16[384,256]{1,0:T(8,128)(2,1)S(1)}, u32[]{:S(2)}, u32[]{:S(2)}) collective-permute-start(bf16[384,256]{1,0:T(8,128)(2,1)S(1)} %get-tuple-element.43), channel_id=1, source_target_pairs={{0,1},{1,2},{2,3},{3,4},{4,5},{5,6},{6,7},{7,8},{8,9},{9,10},{10,1... | collective-permute-start | bytes 589832 | tf_op jit(solution)/shard_map/ppermute | solution.py:335
  4.1 6.7 %collective-permute-start.1 = (bf16[384,256]{1,0:T(8,128)(2,1)S(1)}, bf16[384,256]{1,0:T(8,128)(2,1)S(1)}, u32[]{:S(2)}, u32[]{:S(2)}) collective-permute-start(bf16[384,256]{1,0:T(8,128)(2,1)S(1)} %get-tuple-element.44), channel_id=1, source_target_pairs={{0,127},{1,0},{2,1},{3,2},{4,3},{5,4},{6,5},{7,6},{8,7},{9,8},{10,... | collective-permute-start | bytes 589832 | tf_op jit(solution)/shard_map/ppermute | solution.py:335
  10.8 4.5 %collective-permute-done.from_prev = bf16[384,256]{1,0:T(8,128)(2,1)S(1)} collective-permute-done((bf16[384,256]{1,0:T(8,128)(2,1)S(1)}, bf16[384,256]{1,0:T(8,128)(2,1)S(1)}, u32[]{:S(2)}, u32[]{:S(2)}) %collective-permute-start) | collective-permute-done | bytes 196640 | tf_op jit(solution)/shard_map/ppermute | solution.py:335
  15.3 0.0 collective-permute-done.1.from_next
  15.3 1.3 %shard_map.114 = (bf16[512,256]{1,0:T(8,128)(2,1)S(1)}, bf16[512,256]{1,0:T(8,128)(2,1)S(1)}) custom-call(bf16[1024,256]{1,0:T(8,128)(2,1)S(1)} %get-tuple-element.42.points, bf16[384,256]{1,0:T(8,128)(2,1)S(1)} %collective-permute-done.from_prev, bf16[384,256]{1,0:T(8,128)(2,1)S(1)} %collective-permute-done.1.from_next, s32[1,1024]{1,0:T(1,128)S(1)} %get-tuple-element.45.slot), custom_call_target="tpu_custom_call" | custom-call | tf_op jit(solution)/shard_map/pallas_call | solution.py:320
  16.6 0.1 collective-permute-start.2
  16.7 7.5 %shard_map.115 = (bf16[2,512,128]{2,1,0:T(8,128)(2,1)S(1)}, bf16[2,512,128]{2,1,0:T(8,128)(2,1)S(1)}, bf16[256,512]{1,0:T(8,128)(2,1)S(1)}, bf16[256,512]{1,0:T(...) custom-call(bf16[512,256]{1,0:T(8,128)(2,1)S(1)} %get-tuple-element., ...), custom_call_target="tpu_custom_call" | custom-call | tf_op jit(solution)/shard_map/pallas_call | solution.py:320
  24.2 0.3 collective-permute-start.3
  24.5 5.2 %collective-permute-done.2.ord_lo = bf16[512,256]{1,0:T(8,128)(2,1)S(1)} collective-permute-done((bf16[512,256]{1,0:T(8,128)(2,1)S(1)}, bf16[512,256]{1,0:T(8,128)(2,1)S(1)}, u32[]{:S(2)}, u32[]{:S(2)}) %collective-permute-start.2) | collective-permute-done | bytes 262176 | tf_op jit(solution)/shard_map/ppermute | solution.py:335
  29.8 15.1 %shard_map.116 = (bf16[2,512,128]{2,1,0:T(8,128)(2,1)S(1)}, bf16[256,1024]{1,0:T(8,128)(2,1)S(1)}, bf16[256,512]{1,0:T(8,128)(2,1)S(1)}, bf16[16,512,1024]{2,1,0...) custom-call(bf16[512,256]{1,0:T(8,128)(2,1)S(1)} %collective-permute, ...), custom_call_target="tpu_custom_call" | custom-call | tf_op jit(solution)/shard_map/pallas_call | solution.py:320
  44.9 0.0 collective-permute-done.3.cot_lo
  44.9 5.6 %shard_map.117 = (bf16[512,256]{1,0:T(8,128)(2,1)S(1)}, bf16[512,256]{1,0:T(8,128)(2,1)S(1)}, bf16[256,1024]{1,0:T(8,128)(2,1)S(1)}, f32[512,256]{1,0:T(8,128)S(1)}, f32[512,256]{1,0:T(8,128)S(1)}) custom-call(bf16[512,256]{1,0:T(8,128)(2,1)S(1)} %collective-permute-done.2.ord_lo, bf16[512,256]{1,0:T(8,128)(2,1)S(1)} %get-tuple-element.47.ord_hi, ...), custom_call_target="tpu_custom_call" | custom-call | tf_op jit(solution)/shard_map/pallas_call | solution.py:320
  50.5 21.9 %shard_map.118 = (bf16[512,256]{1,0:T(8,128)(2,1)S(1)}, f32[16,8,512]{2,1,0:T(8,128)S(1)}, f32[768,512]{1,0:T(8,128)S(1)}) custom-call(bf16[512,256]{1,0:T(8,128)(2,1)S(1)} %collective-permute-done.2.ord_lo, bf16[256,768]{1,0:T(8,128)(2,1)S(1)} %get-tuple-element.48.wqkv, f32[1,256]{1,0:T(1,128)S(1)} %get-tuple-element.49.gain1, ...), custom_call_target="tpu_custom_call" | custom-call | tf_op jit(solution)/shard_map/pallas_call | solution.py:320
  72.4 2.0 %collective-permute-start.5 = (bf16[512,256]{1,0:T(8,128)(2,1)S(1)}, bf16[512,256]{1,0:T(8,128)(2,1)S(1)}, u32[]{:S(2)}, u32[]{:S(2)}) collective-permute-start(bf16[512,256]{1,0:T(8,128)(2,1)S(1)} %get-tuple-element.78), channel_id=1, source_target_pairs={{0,127},{1,0},{2,1},{3,2},{4,3},{5,4},{6,5},{7,6},{8,7},{9,8},{10,... | collective-permute-start | bytes 786440 | tf_op jit(solution)/shard_map/ppermute | solution.py:335
  74.4 1.4 %collective-permute-start.4 = (bf16[512,256]{1,0:T(8,128)(2,1)S(1)}, bf16[512,256]{1,0:T(8,128)(2,1)S(1)}, u32[]{:S(2)}, u32[]{:S(2)}) collective-permute-start(bf16[512,256]{1,0:T(8,128)(2,1)S(1)} %get-tuple-element.63), channel_id=1, source_target_pairs={{0,127},{1,0},{2,1},{3,2},{4,3},{5,4},{6,5},{7,6},{8,7},{9,8},{10,... | collective-permute-start | bytes 786440 | tf_op jit(solution)/shard_map/ppermute | solution.py:335
  75.8 9.7 %shard_map.119.first = bf16[512,256]{1,0:T(8,128)(2,1)S(1)} custom-call(bf16[512,256]{1,0:T(8,128)(2,1)S(1)} %get-tuple-element.47.ord_hi, bf16[256,768]{1,0:T(8,128)(2,1)S(1)} %get-tuple-element.48.wqkv, f32[1,256]{1,0:T(1,128)S(1)} %get-tuple-element.49.gain1, bf16[2,512,128]{2,1,0:T(8,128)(2,1)S(1)} %get-tuple-element.64.vn_hi.vn, ...), custom_call_target="tpu_custom_call" | custom-call | tf_op jit(solution)/shard_map/pallas_call | solution.py:320
  85.6 0.0 collective-permute-done.5.second
  85.6 0.6 shard_map.121
  86.2 0.7 collective-permute-start.6
  86.8 6.6 %collective-permute-start.7 = (bf16[384,256]{1,0:T(8,128)(2,1)S(1)}, bf16[384,256]{1,0:T(8,128)(2,1)S(1)}, u32[]{:S(2)}, u32[]{:S(2)}) collective-permute-start(bf16[384,256]{1,0:T(8,128)(2,1)S(1)} %get-tuple-element.80), channel_id=1, source_target_pairs={{0,127},{1,0},{2,1},{3,2},{4,3},{5,4},{6,5},{7,6},{8,7},{9,8},{10,... | collective-permute-start | bytes 589832 | tf_op jit(solution)/shard_map/ppermute | solution.py:335
  93.4 0.7 shard_map.120.own
  94.1 0.0 collective-permute-done.4
  94.1 0.8 maximum_bitcast_fusion
  95.0 1.8 %collective-permute-done.6.left = bf16[384,256]{1,0:T(8,128)(2,1)S(1)} collective-permute-done((bf16[384,256]{1,0:T(8,128)(2,1)S(1)}, bf16[384,256]{1,0:T(8,128)(2,1)S(1)}, u32[]{:S(2)}, u32[]{:S(2)}) %collective-permute-start.6) | collective-permute-done | bytes 196640 | tf_op jit(solution)/shard_map/ppermute | solution.py:335
  96.8 0.0 collective-permute-done.7.right
  96.8 1.5 %shard_map.122 = bf16[1024,256]{1,0:T(8,128)(2,1)} custom-call(bf16[1024,256]{1,0:T(8,128)(2,1)S(1)} %shard_map.120.own, bf16[384,256]{1,0:T(8,128)(2,1)S(1)} %collective-permute-done.6.left, bf16[384,256]{1,0:T(8,128)(2,1)S(1)} %collective-permute-done.7.right, s32[1,768]{1,0:T(1,128)S(1)} %get-tuple-element.81.sender), custom_call_target="tpu_custom_call" | custom-call | tf_op jit(solution)/shard_map/pallas_call | solution.py:320
Async XLA Ops:
  2.4 12.9 %collective-permute-start = (bf16[384,256]{1,0:T(8,128)(2,1)S(1)}, bf16[384,256]{1,0:T(8,128)(2,1)S(1)}, u32[]{:S(2)}, u32[]{:S(2)}) collective-permute-start(bf16[384,256]{1,0:T(8,128)(2,1)S(1)} %get-tuple-element.43), channel_id=1, source_target_pairs={{0,1},{1,2},{2,3},{3,4},{4,5},{5,6},{6,7},{7,8},{8,9},{9,10},{10,1... | collective-permute-start | bytes 589832 | tf_op jit(solution)/shard_map/ppermute | solution.py:335
  4.1 11.2 %collective-permute-start.1 = (bf16[384,256]{1,0:T(8,128)(2,1)S(1)}, bf16[384,256]{1,0:T(8,128)(2,1)S(1)}, u32[]{:S(2)}, u32[]{:S(2)}) collective-permute-start(bf16[384,256]{1,0:T(8,128)(2,1)S(1)} %get-tuple-element.44), channel_id=1, source_target_pairs={{0,127},{1,0},{2,1},{3,2},{4,3},{5,4},{6,5},{7,6},{8,7},{9,8},{10,... | collective-permute-start | bytes 589832 | tf_op jit(solution)/shard_map/ppermute | solution.py:335
  16.6 13.1 %collective-permute-start.2 = (bf16[512,256]{1,0:T(8,128)(2,1)S(1)}, bf16[512,256]{1,0:T(8,128)(2,1)S(1)}, u32[]{:S(2)}, u32[]{:S(2)}) collective-permute-start(bf16[512,256]{1,0:T(8,128)(2,1)S(1)} %get-tuple-element.46), channel_id=1, source_target_pairs={{0,1},{1,2},{2,3},{3,4},{4,5},{5,6},{6,7},{7,8},{8,9},{9,10},{10,1... | collective-permute-start | bytes 786440 | tf_op jit(solution)/shard_map/ppermute | solution.py:335
  24.2 20.6 %collective-permute-start.3 = (bf16[512,256]{1,0:T(8,128)(2,1)S(1)}, bf16[512,256]{1,0:T(8,128)(2,1)S(1)}, u32[]{:S(2)}, u32[]{:S(2)}) collective-permute-start(bf16[512,256]{1,0:T(8,128)(2,1)S(1)} %get-tuple-element.50), channel_id=1, source_target_pairs={{0,1},{1,2},{2,3},{3,4},{4,5},{5,6},{6,7},{7,8},{8,9},{9,10},{10,1... | collective-permute-start | bytes 786440 | tf_op jit(solution)/shard_map/ppermute | solution.py:335
  72.4 13.2 %collective-permute-start.5 = (bf16[512,256]{1,0:T(8,128)(2,1)S(1)}, bf16[512,256]{1,0:T(8,128)(2,1)S(1)}, u32[]{:S(2)}, u32[]{:S(2)}) collective-permute-start(bf16[512,256]{1,0:T(8,128)(2,1)S(1)} %get-tuple-element.78), channel_id=1, source_target_pairs={{0,127},{1,0},{2,1},{3,2},{4,3},{5,4},{6,5},{7,6},{8,7},{9,8},{10,... | collective-permute-start | bytes 786440 | tf_op jit(solution)/shard_map/ppermute | solution.py:335
  74.4 19.7 %collective-permute-start.4 = (bf16[512,256]{1,0:T(8,128)(2,1)S(1)}, bf16[512,256]{1,0:T(8,128)(2,1)S(1)}, u32[]{:S(2)}, u32[]{:S(2)}) collective-permute-start(bf16[512,256]{1,0:T(8,128)(2,1)S(1)} %get-tuple-element.63), channel_id=1, source_target_pairs={{0,127},{1,0},{2,1},{3,2},{4,3},{5,4},{6,5},{7,6},{8,7},{9,8},{10,... | collective-permute-start | bytes 786440 | tf_op jit(solution)/shard_map/ppermute | solution.py:335
  86.2 10.6 %collective-permute-start.6 = (bf16[384,256]{1,0:T(8,128)(2,1)S(1)}, bf16[384,256]{1,0:T(8,128)(2,1)S(1)}, u32[]{:S(2)}, u32[]{:S(2)}) collective-permute-start(bf16[384,256]{1,0:T(8,128)(2,1)S(1)} %get-tuple-element.79), channel_id=1, source_target_pairs={{0,1},{1,2},{2,3},{3,4},{4,5},{5,6},{6,7},{7,8},{8,9},{9,10},{10,1... | collective-permute-start | bytes 589832 | tf_op jit(solution)/shard_map/ppermute | solution.py:335
  86.8 9.9 %collective-permute-start.7 = (bf16[384,256]{1,0:T(8,128)(2,1)S(1)}, bf16[384,256]{1,0:T(8,128)(2,1)S(1)}, u32[]{:S(2)}, u32[]{:S(2)}) collective-permute-start(bf16[384,256]{1,0:T(8,128)(2,1)S(1)} %get-tuple-element.80), channel_id=1, source_target_pairs={{0,127},{1,0},{2,1},{3,2},{4,3},{5,4},{6,5},{7,6},{8,7},{9,8},{10,... | collective-permute-start | bytes 589832 | tf_op jit(solution)/shard_map/ppermute | solution.py:335

commit v5 on v4

--- a/solution.py
+++ b/solution.py
@@ -21,10 +21,10 @@
 LOG2E = 1.4426950408889634
 SCORE = LOG2E / 4.0
 VSCALE = 2.0**-8
-UNROLL_BEFORE = 1
-UNROLL_FORWARD = 1
-UNROLL_BACKWARD = 1
-UNROLL_AFTER = 1
+UNROLL_BEFORE = 4
+UNROLL_FORWARD = 2
+UNROLL_BACKWARD = 2
+UNROLL_AFTER = 4
 
 bf16 = jnp.bfloat16
 f32 = jnp.float32
@@ -156,8 +156,18 @@
         out[sl] = grad.astype(bf16)
 
 
-def head_mask(h):
-    return lax.broadcasted_iota(jnp.int32, (HALF, 128), 1) // D == h % 8
+def head_lanes(h):
+    lanes = lax.broadcasted_iota(jnp.int32, (1, 128), 1)
+    return jnp.where(lanes // D == h % 8, 1.0, 0.0).astype(bf16)
+
+
+def each_head(unroll, body):
+    def step(i, carry):
+        for j in range(unroll):
+            body(i * unroll + j, j)
+        return carry
+
+    lax.fori_loop(0, H // unroll, step, 0)
 
 
 def weigh(keys, queries):
@@ -170,15 +180,14 @@
     copies = start_copies([(cot.at[pl.ds(HALF, HALF)], cot_second)], sems)
     split_qkv(ord_hi, gain1, wqkv, kn, vn, qt, kt, vt)
 
-    def one_head(h, carry):
+    def one_head(h, j):
         block = h // 8
-        keys = jnp.where(head_mask(h), kn[block], bf16(0))
+        keys = kn[block] * head_lanes(h)
         weights = weigh(keys, qt[pl.ds(block * 128, 128)])
         e_hh[h] = weights
         sums_hh[h] = dg(vt[h], weights, 1, 0)
-        return carry
-
-    lax.fori_loop(0, H, one_head, 0, unroll=UNROLL_BEFORE)
+
+    each_head(UNROLL_BEFORE, one_head)
     copies[0].wait()
 
 
@@ -194,13 +203,13 @@
     split_qkv(ord_lo, gain1, wqkv, kn, vn, qt.at[:, :HALF], kt, vt)
     qt[:, HALF:] = qt_hi[...]
 
-    def forward_head(h, carry):
+    def forward_head(h, j):
         block = h // 8
-        mask = head_mask(h)
+        mask = head_lanes(h)
         lanes = pl.ds(block * 128, 128)
-        weights = weigh(jnp.where(mask, kn[block], bf16(0)), qt[lanes])
+        weights = weigh(kn[block] * mask, qt[lanes])
         e_l[h] = weights
-        side = weigh(jnp.where(mask, kn_hi[block], bf16(0)), qt[lanes, :HALF])
+        side = weigh(kn_hi[block] * mask, qt[lanes, :HALF])
         e_hl[h] = side
         sums = dg(vt[h], weights, 1, 0)
         sums += jnp.concatenate([dg(vt_hi[h], side, 1, 0), sums_hh[h]], axis=1)
@@ -210,9 +219,8 @@
         ot[pl.ds(h * D, D)] = (sums[:D] * amp) * inverse
         inv_scr[pl.ds(h * D, D)] = jnp.broadcast_to(inverse * VSCALE, (D, N))
         amp_scr[h] = jnp.broadcast_to(amp, (D, N)).astype(bf16)
-        return carry
-
-    lax.fori_loop(0, H, forward_head, 0, unroll=UNROLL_FORWARD)
+
+    each_head(UNROLL_FORWARD, forward_head)
     for copy in copies:
         copy.wait()
 
@@ -249,37 +257,36 @@
     grad_lo, inner_hi, part,
     dt, p_t, s_t, ph_t, sh_t,
 ):
-    def backward_head(h, carry):
+    def backward_head(h, j):
         block = h // 8
         rows = pl.ds(h * D, D)
         rows_k = pl.ds(256 + h * D, D)
         rows_v = pl.ds(512 + h * D, D)
         lanes = pl.ds(block * 128, 128)
-        mask = head_mask(h)
+        mask = head_lanes(h)
         grads = gt[rows]
         inner = jnp.sum(grads.astype(f32) * ot[rows], axis=0, keepdims=True)
         inner_hi[h] = jnp.broadcast_to(inner[:, HALF:], (8, HALF))
         amp = amp_scr[h, :1]
         probs = e_l[h] * amp
-        p_t[...] = jnp.transpose(probs)
+        p_t[j] = jnp.transpose(probs)
         side = e_hl[h] * amp[:, :HALF]
-        ph_t[...] = jnp.transpose(side)
-        values = jnp.where(mask, vn[block], bf16(0))
+        ph_t[j] = jnp.transpose(side)
+        values = vn[block] * mask
         scores = probs * (dg(values, gt[lanes], 1, 0) - inner).astype(bf16)
         grad_q = dg(kt[rows], scores, 1, 0)
-        values = jnp.where(mask, vn_hi[block], bf16(0))
+        values = vn_hi[block] * mask
         side_scores = side * (dg(values, gt[lanes, :HALF], 1, 0) - inner[:, :HALF]).astype(bf16)
-        s_t[...] = jnp.transpose(scores)
-        sh_t[...] = jnp.transpose(side_scores)
+        s_t[j] = jnp.transpose(scores)
+        sh_t[j] = jnp.transpose(side_scores)
         dt[rows] = ((grad_q[:, :HALF] + dg(kt_hi[rows], side_scores, 1, 0)) * 0.25).astype(bf16)
         part[rows] = grad_q[:, HALF:]
-        dt[rows_v] = dg(grads, p_t[...], 1, 0).astype(bf16)
-        part[rows_v] = dg(gt[rows, :HALF], ph_t[...], 1, 0)
-        dt[rows_k] = (dg(qt[rows], s_t[...], 1, 0) * 0.25).astype(bf16)
-        part[rows_k] = dg(qt[rows, :HALF], sh_t[...], 1, 0)
-        return carry
-
-    lax.fori_loop(0, H, backward_head, 0, unroll=UNROLL_BACKWARD)
+        dt[rows_v] = dg(grads, p_t[j], 1, 0).astype(bf16)
+        part[rows_v] = dg(gt[rows, :HALF], ph_t[j], 1, 0)
+        dt[rows_k] = (dg(qt[rows], s_t[j], 1, 0) * 0.25).astype(bf16)
+        part[rows_k] = dg(qt[rows, :HALF], sh_t[j], 1, 0)
+
+    each_head(UNROLL_BACKWARD, backward_head)
     front_back(dt, ord_lo, mix_lo, gain1, wqkv, grad_lo)
 
 
@@ -287,23 +294,22 @@
     ord_hi, wqkv, gain1, vn, qt, kt, e_hh, gt, inner_hi, amp_hi, part, mix_hi,
     grad_hi, dt, p_t, s_t,
 ):
-    def backward_head(h, carry):
+    def backward_head(h, j):
         block = h // 8
         rows = pl.ds(h * D, D)
         rows_k = pl.ds(256 + h * D, D)
         rows_v = pl.ds(512 + h * D, D)
         probs = e_hh[h] * amp_hi[h, :1, HALF:]
-        p_t[...] = jnp.transpose(probs)
-        values = jnp.where(head_mask(h), vn[block], bf16(0))
+        p_t[j] = jnp.transpose(probs)
+        values = vn[block] * head_lanes(h)
         inner = inner_hi[h][:1]
         scores = probs * (dg(values, gt[pl.ds(block * 128, 128), HALF:], 1, 0) - inner).astype(bf16)
-        s_t[...] = jnp.transpose(scores)
+        s_t[j] = jnp.transpose(scores)
         dt[rows] = ((part[rows] + dg(kt[rows], scores, 1, 0)) * 0.25).astype(bf16)
-        dt[rows_v] = (part[rows_v] + dg(gt[rows, HALF:], p_t[...], 1, 0)).astype(bf16)
-        dt[rows_k] = ((part[rows_k] + dg(qt[rows], s_t[...], 1, 0)) * 0.25).astype(bf16)
-        return carry
-
-    lax.fori_loop(0, H, backward_head, 0, unroll=UNROLL_AFTER)
+        dt[rows_v] = (part[rows_v] + dg(gt[rows, HALF:], p_t[j], 1, 0)).astype(bf16)
+        dt[rows_k] = ((part[rows_k] + dg(qt[rows], s_t[j], 1, 0)) * 0.25).astype(bf16)
+
+    each_head(UNROLL_AFTER, backward_head)
     front_back(dt, ord_hi, mix_hi, gain1, wqkv, grad_hi)
 
 
@@ -378,8 +384,8 @@
     wide_f = vm((C, N), f32)
     valued = vm((H, 2 * D, HALF), bf16)
     square = vm((H, HALF, HALF), bf16)
-    tall = vm((N, HALF), bf16)
-    tile = vm((HALF, HALF), bf16)
+    tall_s = (N, HALF)
+    tile_s = (HALF, HALF)
     kn_hi, vn_hi, qt_hi, kt_hi, vt_hi, e_hh, sums_hh, cot_second = call(
         before_kernel,
         [ord_hi, wqkv, gain1],
@@ -389,7 +395,7 @@
             (HALF, C),
         ],
         [],
-        6,
+        8,
         1,
     )
     cot_lo = shift(cot_second, 1)
@@ -402,7 +408,7 @@
             vm((H, D, N), bf16), vm((C, C), bf16), vm((C, FF), bf16), vm((FF, C), bf16), half,
         ],
         [natural, valued],
-        9,
+        13,
         4,
     )
     out_lo, out_hi, gt, mix_lo, mix_hi = call(
@@ -422,8 +428,8 @@
         ],
         [],
         [(HALF, C), vm((H, 8, HALF), f32), vm((3 * C, HALF), f32)],
-        [vm((3 * C, HALF), bf16), tall, tall, tile, tile],
-        9,
+        [vm((3 * C, HALF), bf16)] + [vm((UNROLL_BACKWARD,) + t, bf16) for t in (tall_s, tall_s, tile_s, tile_s)],
+        14,
     )
     grad_lo, inner_hi, part = back()
     grad_second = shift(grad_lo, -1)
@@ -432,8 +438,8 @@
         [ord_hi, wqkv, gain1, vn_hi, qt_hi, kt_hi, chip(e_hh), gt, inner_hi, amp, part, mix_hi],
         [],
         [half],
-        [vm((3 * C, HALF), bf16), tile, tile],
-        6,
+        [vm((3 * C, HALF), bf16)] + [vm((UNROLL_AFTER,) + tile_s, bf16)] * 2,
+        11,
     )
     to_prev, to_next = call(
         back_kernel, [grad_hi, chip(grad_second), slot_v], [], [(CAP, C)] * 2, [], 6

time: 98.4 us -> 93.1 us (0.946)
  Pallas kernels: 65.7 us -> 60.4 us
  waiting for transfers between devices: 11.6 us -> 13 us
  starting transfers between devices: 19.4 us -> 18 us
    pallas_call x10, Pallas kernels: 65.7 us -> 60.4 us  [call(): pl.pallas_call(kernel, in_specs=[near] * len(operands) + [away] * len(far...]
    ppermute x8, waiting for transfers between devices: 11.6 us -> 13 us  [shift(): lax.ppermute(rows, axes, [(i, (i + step) % count) for i in range(count)])]
    ppermute x8, starting transfers between devices: 19.4 us -> 18 us  [shift(): lax.ppermute(rows, axes, [(i, (i + step) % count) for i in range(count)])]
  transfers between devices with their start and end apart: 8 -> 8, of which waited for: 3 -> 3; matrix products, arithmetic and copies ran while one was open for 1% -> 1% of each run, Pallas kernels for 34% -> 32%
where the time goes in v5:
time: 93.1 us; the launch traced here: 92.9 us
  Pallas kernels  60.4 us (65%)
  starting transfers between devices  18 us (19%)
  waiting for transfers between devices  13 us (14%)
    pallas_call x10, Pallas kernels, call(): pl.pallas_call(kernel, in_specs=[near] * len(operands) + [away] * len(far...  60.4 us
    ppermute x8, starting transfers between devices, shift(): lax.ppermute(rows, axes, [(i, (i + step) % count) for i in range(count)])  18 us
    ppermute x8, waiting for transfers between devices, shift(): lax.ppermute(rows, axes, [(i, (i + step) % count) for i in range(count)])  13 us
  transfers between devices with their start and end apart: 8, of which 3 were waited for; matrix products, arithmetic and copies ran while one was open for 1% of the time, Pallas kernels for 32%

profile of v5, /device:TPU:0, one launch (start us, length us, event | category | flops | bytes accessed | tf_op | source)
XLA Modules:
  0.0 92.9 jit_solution(10050996282008765605)
XLA Ops:
  0.6 1.7 %shard_map.113 = (bf16[384,256]{1,0:T(8,128)(2,1)S(1)}, bf16[384,256]{1,0:T(8,128)(2,1)S(1)}, bf16[1024,256]{1,0:T(8,128)(2,1)S(1)}, s32[1,768]{1,0:T(1,128)S(1)...) custom-call(bf16[1024,256]{1,0:T(8,128)(2,1)} %bitcast.11, ...), custom_call_target="tpu_custom_call" | custom-call | tf_op jit(solution)/shard_map/pallas_call | solution.py:326
  2.4 1.7 %collective-permute-start = (bf16[384,256]{1,0:T(8,128)(2,1)S(1)}, bf16[384,256]{1,0:T(8,128)(2,1)S(1)}, u32[]{:S(2)}, u32[]{:S(2)}) collective-permute-start(bf16[384,256]{1,0:T(8,128)(2,1)S(1)} %get-tuple-element.43), channel_id=1, source_target_pairs={{0,1},{1,2},{2,3},{3,4},{4,5},{5,6},{6,7},{7,8},{8,9},{9,10},{10,1... | collective-permute-start | bytes 589832 | tf_op jit(solution)/shard_map/ppermute | solution.py:341
  4.1 6.7 %collective-permute-start.1 = (bf16[384,256]{1,0:T(8,128)(2,1)S(1)}, bf16[384,256]{1,0:T(8,128)(2,1)S(1)}, u32[]{:S(2)}, u32[]{:S(2)}) collective-permute-start(bf16[384,256]{1,0:T(8,128)(2,1)S(1)} %get-tuple-element.44), channel_id=1, source_target_pairs={{0,127},{1,0},{2,1},{3,2},{4,3},{5,4},{6,5},{7,6},{8,7},{9,8},{10,... | collective-permute-start | bytes 589832 | tf_op jit(solution)/shard_map/ppermute | solution.py:341
  10.8 4.5 %collective-permute-done.from_prev = bf16[384,256]{1,0:T(8,128)(2,1)S(1)} collective-permute-done((bf16[384,256]{1,0:T(8,128)(2,1)S(1)}, bf16[384,256]{1,0:T(8,128)(2,1)S(1)}, u32[]{:S(2)}, u32[]{:S(2)}) %collective-permute-start) | collective-permute-done | bytes 196640 | tf_op jit(solution)/shard_map/ppermute | solution.py:341
  15.3 0.0 collective-permute-done.1.from_next
  15.3 1.3 %shard_map.114 = (bf16[512,256]{1,0:T(8,128)(2,1)S(1)}, bf16[512,256]{1,0:T(8,128)(2,1)S(1)}) custom-call(bf16[1024,256]{1,0:T(8,128)(2,1)S(1)} %get-tuple-element.42.points, bf16[384,256]{1,0:T(8,128)(2,1)S(1)} %collective-permute-done.from_prev, bf16[384,256]{1,0:T(8,128)(2,1)S(1)} %collective-permute-done.1.from_next, s32[1,1024]{1,0:T(1,128)S(1)} %get-tuple-element.45.slot), custom_call_target="tpu_custom_call" | custom-call | tf_op jit(solution)/shard_map/pallas_call | solution.py:326
  16.6 0.1 collective-permute-start.2
  16.7 6.1 %shard_map.115 = (bf16[2,512,128]{2,1,0:T(8,128)(2,1)S(1)}, bf16[2,512,128]{2,1,0:T(8,128)(2,1)S(1)}, bf16[256,512]{1,0:T(8,128)(2,1)S(1)}, bf16[256,512]{1,0:T(...) custom-call(bf16[512,256]{1,0:T(8,128)(2,1)S(1)} %get-tuple-element., ...), custom_call_target="tpu_custom_call" | custom-call | tf_op jit(solution)/shard_map/pallas_call | solution.py:326
  22.8 0.3 collective-permute-start.3
  23.1 6.7 %collective-permute-done.2.ord_lo = bf16[512,256]{1,0:T(8,128)(2,1)S(1)} collective-permute-done((bf16[512,256]{1,0:T(8,128)(2,1)S(1)}, bf16[512,256]{1,0:T(8,128)(2,1)S(1)}, u32[]{:S(2)}, u32[]{:S(2)}) %collective-permute-start.2) | collective-permute-done | bytes 262176 | tf_op jit(solution)/shard_map/ppermute | solution.py:341
  29.8 14.0 %shard_map.116 = (bf16[2,512,128]{2,1,0:T(8,128)(2,1)S(1)}, bf16[256,1024]{1,0:T(8,128)(2,1)S(1)}, bf16[256,512]{1,0:T(8,128)(2,1)S(1)}, bf16[16,512,1024]{2,1,0...) custom-call(bf16[512,256]{1,0:T(8,128)(2,1)S(1)} %collective-permute, ...), custom_call_target="tpu_custom_call" | custom-call | tf_op jit(solution)/shard_map/pallas_call | solution.py:326
  43.7 0.0 collective-permute-done.3.cot_lo
  43.7 5.6 %shard_map.117 = (bf16[512,256]{1,0:T(8,128)(2,1)S(1)}, bf16[512,256]{1,0:T(8,128)(2,1)S(1)}, bf16[256,1024]{1,0:T(8,128)(2,1)S(1)}, f32[512,256]{1,0:T(8,128)S(1)}, f32[512,256]{1,0:T(8,128)S(1)}) custom-call(bf16[512,256]{1,0:T(8,128)(2,1)S(1)} %collective-permute-done.2.ord_lo, bf16[512,256]{1,0:T(8,128)(2,1)S(1)} %get-tuple-element.47.ord_hi, ...), custom_call_target="tpu_custom_call" | custom-call | tf_op jit(solution)/shard_map/pallas_call | solution.py:326
  49.4 20.8 %shard_map.118 = (bf16[512,256]{1,0:T(8,128)(2,1)S(1)}, f32[16,8,512]{2,1,0:T(8,128)S(1)}, f32[768,512]{1,0:T(8,128)S(1)}) custom-call(bf16[512,256]{1,0:T(8,128)(2,1)S(1)} %collective-permute-done.2.ord_lo, bf16[256,768]{1,0:T(8,128)(2,1)S(1)} %get-tuple-element.48.wqkv, f32[1,256]{1,0:T(1,128)S(1)} %get-tuple-element.49.gain1, ...), custom_call_target="tpu_custom_call" | custom-call | tf_op jit(solution)/shard_map/pallas_call | solution.py:326
  70.2 1.1 %collective-permute-start.5 = (bf16[512,256]{1,0:T(8,128)(2,1)S(1)}, bf16[512,256]{1,0:T(8,128)(2,1)S(1)}, u32[]{:S(2)}, u32[]{:S(2)}) collective-permute-start(bf16[512,256]{1,0:T(8,128)(2,1)S(1)} %get-tuple-element.78), channel_id=1, source_target_pairs={{0,127},{1,0},{2,1},{3,2},{4,3},{5,4},{6,5},{7,6},{8,7},{9,8},{10,... | collective-permute-start | bytes 786440 | tf_op jit(solution)/shard_map/ppermute | solution.py:341
  71.3 0.9 collective-permute-start.4
  72.2 8.1 %shard_map.119.first = bf16[512,256]{1,0:T(8,128)(2,1)S(1)} custom-call(bf16[512,256]{1,0:T(8,128)(2,1)S(1)} %get-tuple-element.47.ord_hi, bf16[256,768]{1,0:T(8,128)(2,1)S(1)} %get-tuple-element.48.wqkv, f32[1,256]{1,0:T(1,128)S(1)} %get-tuple-element.49.gain1, bf16[2,512,128]{2,1,0:T(8,128)(2,1)S(1)} %get-tuple-element.64.vn_hi.vn, ...), custom_call_target="tpu_custom_call" | custom-call | tf_op jit(solution)/shard_map/pallas_call | solution.py:326
  80.2 0.0 collective-permute-done.5.second
  80.2 0.6 shard_map.121
  80.8 1.2 %collective-permute-start.6 = (bf16[384,256]{1,0:T(8,128)(2,1)S(1)}, bf16[384,256]{1,0:T(8,128)(2,1)S(1)}, u32[]{:S(2)}, u32[]{:S(2)}) collective-permute-start(bf16[384,256]{1,0:T(8,128)(2,1)S(1)} %get-tuple-element.79), channel_id=1, source_target_pairs={{0,1},{1,2},{2,3},{3,4},{4,5},{5,6},{6,7},{7,8},{8,9},{9,10},{10,1... | collective-permute-start | bytes 589832 | tf_op jit(solution)/shard_map/ppermute | solution.py:341
  82.1 6.0 %collective-permute-start.7 = (bf16[384,256]{1,0:T(8,128)(2,1)S(1)}, bf16[384,256]{1,0:T(8,128)(2,1)S(1)}, u32[]{:S(2)}, u32[]{:S(2)}) collective-permute-start(bf16[384,256]{1,0:T(8,128)(2,1)S(1)} %get-tuple-element.80), channel_id=1, source_target_pairs={{0,127},{1,0},{2,1},{3,2},{4,3},{5,4},{6,5},{7,6},{8,7},{9,8},{10,... | collective-permute-start | bytes 589832 | tf_op jit(solution)/shard_map/ppermute | solution.py:341
  88.1 0.7 shard_map.120.own
  88.8 0.0 collective-permute-done.4
  88.8 0.8 maximum_bitcast_fusion
  89.6 1.8 %collective-permute-done.6.left = bf16[384,256]{1,0:T(8,128)(2,1)S(1)} collective-permute-done((bf16[384,256]{1,0:T(8,128)(2,1)S(1)}, bf16[384,256]{1,0:T(8,128)(2,1)S(1)}, u32[]{:S(2)}, u32[]{:S(2)}) %collective-permute-start.6) | collective-permute-done | bytes 196640 | tf_op jit(solution)/shard_map/ppermute | solution.py:341
  91.4 0.0 collective-permute-done.7.right
  91.4 1.5 %shard_map.122 = bf16[1024,256]{1,0:T(8,128)(2,1)} custom-call(bf16[1024,256]{1,0:T(8,128)(2,1)S(1)} %shard_map.120.own, bf16[384,256]{1,0:T(8,128)(2,1)S(1)} %collective-permute-done.6.left, bf16[384,256]{1,0:T(8,128)(2,1)S(1)} %collective-permute-done.7.right, s32[1,768]{1,0:T(1,128)S(1)} %get-tuple-element.81.sender), custom_call_target="tpu_custom_call" | custom-call | tf_op jit(solution)/shard_map/pallas_call | solution.py:326
Async XLA Ops:
  2.4 12.9 %collective-permute-start = (bf16[384,256]{1,0:T(8,128)(2,1)S(1)}, bf16[384,256]{1,0:T(8,128)(2,1)S(1)}, u32[]{:S(2)}, u32[]{:S(2)}) collective-permute-start(bf16[384,256]{1,0:T(8,128)(2,1)S(1)} %get-tuple-element.43), channel_id=1, source_target_pairs={{0,1},{1,2},{2,3},{3,4},{4,5},{5,6},{6,7},{7,8},{8,9},{9,10},{10,1... | collective-permute-start | bytes 589832 | tf_op jit(solution)/shard_map/ppermute | solution.py:341
  4.1 11.2 %collective-permute-start.1 = (bf16[384,256]{1,0:T(8,128)(2,1)S(1)}, bf16[384,256]{1,0:T(8,128)(2,1)S(1)}, u32[]{:S(2)}, u32[]{:S(2)}) collective-permute-start(bf16[384,256]{1,0:T(8,128)(2,1)S(1)} %get-tuple-element.44), channel_id=1, source_target_pairs={{0,127},{1,0},{2,1},{3,2},{4,3},{5,4},{6,5},{7,6},{8,7},{9,8},{10,... | collective-permute-start | bytes 589832 | tf_op jit(solution)/shard_map/ppermute | solution.py:341
  16.6 13.1 %collective-permute-start.2 = (bf16[512,256]{1,0:T(8,128)(2,1)S(1)}, bf16[512,256]{1,0:T(8,128)(2,1)S(1)}, u32[]{:S(2)}, u32[]{:S(2)}) collective-permute-start(bf16[512,256]{1,0:T(8,128)(2,1)S(1)} %get-tuple-element.46), channel_id=1, source_target_pairs={{0,1},{1,2},{2,3},{3,4},{4,5},{5,6},{6,7},{7,8},{8,9},{9,10},{10,1... | collective-permute-start | bytes 786440 | tf_op jit(solution)/shard_map/ppermute | solution.py:341
  22.8 20.9 %collective-permute-start.3 = (bf16[512,256]{1,0:T(8,128)(2,1)S(1)}, bf16[512,256]{1,0:T(8,128)(2,1)S(1)}, u32[]{:S(2)}, u32[]{:S(2)}) collective-permute-start(bf16[512,256]{1,0:T(8,128)(2,1)S(1)} %get-tuple-element.50), channel_id=1, source_target_pairs={{0,1},{1,2},{2,3},{3,4},{4,5},{5,6},{6,7},{7,8},{8,9},{9,10},{10,1... | collective-permute-start | bytes 786440 | tf_op jit(solution)/shard_map/ppermute | solution.py:341
  70.2 10.1 %collective-permute-start.5 = (bf16[512,256]{1,0:T(8,128)(2,1)S(1)}, bf16[512,256]{1,0:T(8,128)(2,1)S(1)}, u32[]{:S(2)}, u32[]{:S(2)}) collective-permute-start(bf16[512,256]{1,0:T(8,128)(2,1)S(1)} %get-tuple-element.78), channel_id=1, source_target_pairs={{0,127},{1,0},{2,1},{3,2},{4,3},{5,4},{6,5},{7,6},{8,7},{9,8},{10,... | collective-permute-start | bytes 786440 | tf_op jit(solution)/shard_map/ppermute | solution.py:341
  71.3 17.5 %collective-permute-start.4 = (bf16[512,256]{1,0:T(8,128)(2,1)S(1)}, bf16[512,256]{1,0:T(8,128)(2,1)S(1)}, u32[]{:S(2)}, u32[]{:S(2)}) collective-permute-start(bf16[512,256]{1,0:T(8,128)(2,1)S(1)} %get-tuple-element.63), channel_id=1, source_target_pairs={{0,127},{1,0},{2,1},{3,2},{4,3},{5,4},{6,5},{7,6},{8,7},{9,8},{10,... | collective-permute-start | bytes 786440 | tf_op jit(solution)/shard_map/ppermute | solution.py:341
  80.8 10.6 %collective-permute-start.6 = (bf16[384,256]{1,0:T(8,128)(2,1)S(1)}, bf16[384,256]{1,0:T(8,128)(2,1)S(1)}, u32[]{:S(2)}, u32[]{:S(2)}) collective-permute-start(bf16[384,256]{1,0:T(8,128)(2,1)S(1)} %get-tuple-element.79), channel_id=1, source_target_pairs={{0,1},{1,2},{2,3},{3,4},{4,5},{5,6},{6,7},{7,8},{8,9},{9,10},{10,1... | collective-permute-start | bytes 589832 | tf_op jit(solution)/shard_map/ppermute | solution.py:341
  82.1 9.4 %collective-permute-start.7 = (bf16[384,256]{1,0:T(8,128)(2,1)S(1)}, bf16[384,256]{1,0:T(8,128)(2,1)S(1)}, u32[]{:S(2)}, u32[]{:S(2)}) collective-permute-start(bf16[384,256]{1,0:T(8,128)(2,1)S(1)} %get-tuple-element.80), channel_id=1, source_target_pairs={{0,127},{1,0},{2,1},{3,2},{4,3},{5,4},{6,5},{7,6},{8,7},{9,8},{10,... | collective-permute-start | bytes 589832 | tf_op jit(solution)/shard_map/ppermute | solution.py:341

commit v6 on v5

--- a/solution.py
+++ b/solution.py
@@ -22,7 +22,7 @@
 SCORE = LOG2E / 4.0
 VSCALE = 2.0**-8
 UNROLL_BEFORE = 4
-UNROLL_FORWARD = 2
+UNROLL_FORWARD = 4
 UNROLL_BACKWARD = 2
 UNROLL_AFTER = 4
 
@@ -80,12 +80,15 @@
         copy.wait()
 
 
-def order_kernel(points, from_prev, from_next, slot, first, second):
+def plan_kernel(points, slot, rows, picks):
     col = column(slot[...], N)
-    rows = dg(picks_from_column(col, 0, N), points[...], 1, 0)
-    rows += dg(picks_from_column(col, N, CAP), from_prev[...], 1, 0)
-    rows += dg(picks_from_column(col, N + CAP, CAP), from_next[...], 1, 0)
-    rows = rows.astype(bf16)
+    rows[...] = dg(picks_from_column(col, 0, N), points[...], 1, 0).astype(bf16)
+    picks[...] = picks_from_column(col, N, 2 * CAP)
+
+
+def order_kernel(own, picks, from_prev, from_next, first, second):
+    rows = dg(picks[:, :CAP], from_prev[...], 1, 0) + dg(picks[:, CAP:], from_next[...], 1, 0)
+    rows = (rows + own[...].astype(f32)).astype(bf16)
     first[...] = rows[:HALF]
     second[...] = rows[HALF:]
 
@@ -99,14 +102,14 @@
     to_next[...] = rows[CAP:]
 
 
-def own_kernel(first, second, slot, out):
+def own_kernel(first, second, slot, sender, out, picks_out):
     picks = picks_from_row(slot[...], 0, N)
     rows = dg(picks[:, :HALF], first[...], 1, 0) + dg(picks[:, HALF:], second[...], 1, 0)
     out[...] = rows.astype(bf16)
-
-
-def final_kernel(own, left, right, sender, out):
-    picks = picks_from_row(sender[...], 0, N)
+    picks_out[...] = picks_from_row(sender[...], 0, N)
+
+
+def final_kernel(own, left, right, picks, out):
     rows = dg(picks[:, :CAP], left[...], 1, 0) + dg(picks[:, CAP:], right[...], 1, 0)
     out[...] = (own[...].astype(f32) + rows).astype(bf16)
 
@@ -369,9 +372,12 @@
     )
     from_prev = shift(right, 1)
     from_next = shift(left, -1)
+    own_rows, arrived = call(
+        plan_kernel, [points_v, slot_v], [], [vm((N, C), bf16), vm((N, 2 * CAP), bf16)], [], 8
+    )
     ord_hi, second = call(
         order_kernel,
-        [points_v, chip(from_prev), chip(from_next), slot_v],
+        [own_rows, arrived, chip(from_prev), chip(from_next)],
         [],
         [half, (HALF, C)],
         [],
@@ -408,7 +414,7 @@
             vm((H, D, N), bf16), vm((C, C), bf16), vm((C, FF), bf16), vm((FF, C), bf16), half,
         ],
         [natural, valued],
-        13,
+        14,
         4,
     )
     out_lo, out_hi, gt, mix_lo, mix_hi = call(
@@ -446,9 +452,16 @@
     )
     back_left = shift(to_prev, -1)
     back_right = shift(to_next, 1)
-    (own,) = call(own_kernel, [grad_hi, chip(grad_second), slot_v], [], [vm((N, C), bf16)], [], 6)
+    own, returning = call(
+        own_kernel,
+        [grad_hi, chip(grad_second), slot_v, sender_v],
+        [],
+        [vm((N, C), bf16), vm((N, 2 * CAP), bf16)],
+        [],
+        8,
+    )
     (grad_points,) = call(
-        final_kernel, [own, chip(back_right), chip(back_left), sender_v], [], [(N, C)], [], 6
+        final_kernel, [own, chip(back_right), chip(back_left), returning], [], [(N, C)], [], 6
     )
     block_out = jnp.concatenate([out_hi, out_second], axis=0)
     return (block_out[None], grad_points[None])

time: 93.1 us -> 91.9 us (0.987)
  waiting for transfers between devices: 13 us -> 12 us
    ppermute x8, waiting for transfers between devices: 13 us -> 12 us  [shift(): lax.ppermute(rows, axes, [(i, (i + step) % count) for i in range(count)])]
    pallas_call x10 -> x11, Pallas kernels: 60.4 us -> 60.3 us  [call(): pl.pallas_call(kernel, in_specs=[near] * len(operands) + [away] * len(far...]
  transfers between devices with their start and end apart: 8 -> 8, of which waited for: 3 -> 3; matrix products, arithmetic and copies ran while one was open for 1% -> 1% of each run, Pallas kernels for 32% -> 33%
where the time goes in v6:
time: 91.9 us; the launch traced here: 91.8 us
  Pallas kernels  60.3 us (66%)
  starting transfers between devices  17.9 us (19%)
  waiting for transfers between devices  12 us (13%)
    pallas_call x11, Pallas kernels, call(): pl.pallas_call(kernel, in_specs=[near] * len(operands) + [away] * len(far...  60.3 us
    ppermute x8, starting transfers between devices, shift(): lax.ppermute(rows, axes, [(i, (i + step) % count) for i in range(count)])  17.9 us
    ppermute x8, waiting for transfers between devices, shift(): lax.ppermute(rows, axes, [(i, (i + step) % count) for i in range(count)])  12 us
  transfers between devices with their start and end apart: 8, of which 3 were waited for; matrix products, arithmetic and copies ran while one was open for 1% of the time, Pallas kernels for 33%

profile of v6, /device:TPU:0, one launch (start us, length us, event | category | flops | bytes accessed | tf_op | source)
XLA Modules:
  0.0 91.8 jit_solution(2416437113627638109)
XLA Ops:
  0.6 1.7 %shard_map.113 = (bf16[384,256]{1,0:T(8,128)(2,1)S(1)}, bf16[384,256]{1,0:T(8,128)(2,1)S(1)}, bf16[1024,256]{1,0:T(8,128)(2,1)S(1)}, s32[1,768]{1,0:T(1,128)S(1)...) custom-call(bf16[1024,256]{1,0:T(8,128)(2,1)} %bitcast.10, ...), custom_call_target="tpu_custom_call" | custom-call | tf_op jit(solution)/shard_map/pallas_call | solution.py:329
  2.4 1.7 %collective-permute-start = (bf16[384,256]{1,0:T(8,128)(2,1)S(1)}, bf16[384,256]{1,0:T(8,128)(2,1)S(1)}, u32[]{:S(2)}, u32[]{:S(2)}) collective-permute-start(bf16[384,256]{1,0:T(8,128)(2,1)S(1)} %get-tuple-element.50), channel_id=1, source_target_pairs={{0,1},{1,2},{2,3},{3,4},{4,5},{5,6},{6,7},{7,8},{8,9},{9,10},{10,1... | collective-permute-start | bytes 589832 | tf_op jit(solution)/shard_map/ppermute | solution.py:344
  4.1 6.7 %collective-permute-start.1 = (bf16[384,256]{1,0:T(8,128)(2,1)S(1)}, bf16[384,256]{1,0:T(8,128)(2,1)S(1)}, u32[]{:S(2)}, u32[]{:S(2)}) collective-permute-start(bf16[384,256]{1,0:T(8,128)(2,1)S(1)} %get-tuple-element.51), channel_id=1, source_target_pairs={{0,127},{1,0},{2,1},{3,2},{4,3},{5,4},{6,5},{7,6},{8,7},{9,8},{10,... | collective-permute-start | bytes 589832 | tf_op jit(solution)/shard_map/ppermute | solution.py:344
  10.8 0.9 shard_map.114
  11.7 3.6 %collective-permute-done.from_prev = bf16[384,256]{1,0:T(8,128)(2,1)S(1)} collective-permute-done((bf16[384,256]{1,0:T(8,128)(2,1)S(1)}, bf16[384,256]{1,0:T(8,128)(2,1)S(1)}, u32[]{:S(2)}, u32[]{:S(2)}) %collective-permute-start) | collective-permute-done | bytes 196640 | tf_op jit(solution)/shard_map/ppermute | solution.py:344
  15.3 0.0 collective-permute-done.1.from_next
  15.3 0.7 shard_map.115
  16.0 0.1 collective-permute-start.2
  16.1 6.1 %shard_map.116 = (bf16[2,512,128]{2,1,0:T(8,128)(2,1)S(1)}, bf16[2,512,128]{2,1,0:T(8,128)(2,1)S(1)}, bf16[256,512]{1,0:T(8,128)(2,1)S(1)}, bf16[256,512]{1,0:T(...) custom-call(bf16[512,256]{1,0:T(8,128)(2,1)S(1)} %get-tuple-element., ...), custom_call_target="tpu_custom_call" | custom-call | tf_op jit(solution)/shard_map/pallas_call | solution.py:329
  22.2 0.3 collective-permute-start.3
  22.5 6.7 %collective-permute-done.2.ord_lo = bf16[512,256]{1,0:T(8,128)(2,1)S(1)} collective-permute-done((bf16[512,256]{1,0:T(8,128)(2,1)S(1)}, bf16[512,256]{1,0:T(8,128)(2,1)S(1)}, u32[]{:S(2)}, u32[]{:S(2)}) %collective-permute-start.2) | collective-permute-done | bytes 262176 | tf_op jit(solution)/shard_map/ppermute | solution.py:344
  29.1 13.5 %shard_map.117 = (bf16[2,512,128]{2,1,0:T(8,128)(2,1)S(1)}, bf16[256,1024]{1,0:T(8,128)(2,1)S(1)}, bf16[256,512]{1,0:T(8,128)(2,1)S(1)}, bf16[16,512,1024]{2,1,0...) custom-call(bf16[512,256]{1,0:T(8,128)(2,1)S(1)} %collective-permute, ...), custom_call_target="tpu_custom_call" | custom-call | tf_op jit(solution)/shard_map/pallas_call | solution.py:329
  42.6 0.0 collective-permute-done.3.cot_lo
  42.6 5.6 %shard_map.118 = (bf16[512,256]{1,0:T(8,128)(2,1)S(1)}, bf16[512,256]{1,0:T(8,128)(2,1)S(1)}, bf16[256,1024]{1,0:T(8,128)(2,1)S(1)}, f32[512,256]{1,0:T(8,128)S(1)}, f32[512,256]{1,0:T(8,128)S(1)}) custom-call(bf16[512,256]{1,0:T(8,128)(2,1)S(1)} %collective-permute-done.2.ord_lo, bf16[512,256]{1,0:T(8,128)(2,1)S(1)} %get-tuple-element.53.ord_hi, ...), custom_call_target="tpu_custom_call" | custom-call | tf_op jit(solution)/shard_map/pallas_call | solution.py:329
  48.3 20.8 %shard_map.119 = (bf16[512,256]{1,0:T(8,128)(2,1)S(1)}, f32[16,8,512]{2,1,0:T(8,128)S(1)}, f32[768,512]{1,0:T(8,128)S(1)}) custom-call(bf16[512,256]{1,0:T(8,128)(2,1)S(1)} %collective-permute-done.2.ord_lo, bf16[256,768]{1,0:T(8,128)(2,1)S(1)} %get-tuple-element.54.wqkv, f32[1,256]{1,0:T(1,128)S(1)} %get-tuple-element.55.gain1, ...), custom_call_target="tpu_custom_call" | custom-call | tf_op jit(solution)/shard_map/pallas_call | solution.py:329
  69.1 1.1 %collective-permute-start.5 = (bf16[512,256]{1,0:T(8,128)(2,1)S(1)}, bf16[512,256]{1,0:T(8,128)(2,1)S(1)}, u32[]{:S(2)}, u32[]{:S(2)}) collective-permute-start(bf16[512,256]{1,0:T(8,128)(2,1)S(1)} %get-tuple-element.84), channel_id=1, source_target_pairs={{0,127},{1,0},{2,1},{3,2},{4,3},{5,4},{6,5},{7,6},{8,7},{9,8},{10,... | collective-permute-start | bytes 786440 | tf_op jit(solution)/shard_map/ppermute | solution.py:344
  70.2 0.9 collective-permute-start.4
  71.1 8.1 %shard_map.120.first = bf16[512,256]{1,0:T(8,128)(2,1)S(1)} custom-call(bf16[512,256]{1,0:T(8,128)(2,1)S(1)} %get-tuple-element.53.ord_hi, bf16[256,768]{1,0:T(8,128)(2,1)S(1)} %get-tuple-element.54.wqkv, f32[1,256]{1,0:T(1,128)S(1)} %get-tuple-element.55.gain1, bf16[2,512,128]{2,1,0:T(8,128)(2,1)S(1)} %get-tuple-element.70.vn_hi.vn, ...), custom_call_target="tpu_custom_call" | custom-call | tf_op jit(solution)/shard_map/pallas_call | solution.py:329
  79.1 0.0 collective-permute-done.5.second
  79.1 0.6 shard_map.122
  79.7 1.2 %collective-permute-start.6 = (bf16[384,256]{1,0:T(8,128)(2,1)S(1)}, bf16[384,256]{1,0:T(8,128)(2,1)S(1)}, u32[]{:S(2)}, u32[]{:S(2)}) collective-permute-start(bf16[384,256]{1,0:T(8,128)(2,1)S(1)} %get-tuple-element.87), channel_id=1, source_target_pairs={{0,1},{1,2},{2,3},{3,4},{4,5},{5,6},{6,7},{7,8},{8,9},{9,10},{10,1... | collective-permute-start | bytes 589832 | tf_op jit(solution)/shard_map/ppermute | solution.py:344
  80.9 6.0 %collective-permute-start.7 = (bf16[384,256]{1,0:T(8,128)(2,1)S(1)}, bf16[384,256]{1,0:T(8,128)(2,1)S(1)}, u32[]{:S(2)}, u32[]{:S(2)}) collective-permute-start(bf16[384,256]{1,0:T(8,128)(2,1)S(1)} %get-tuple-element.88), channel_id=1, source_target_pairs={{0,127},{1,0},{2,1},{3,2},{4,3},{5,4},{6,5},{7,6},{8,7},{9,8},{10,... | collective-permute-start | bytes 589832 | tf_op jit(solution)/shard_map/ppermute | solution.py:344
  87.0 0.8 shard_map.121
  87.8 0.0 collective-permute-done.4
  87.8 0.8 maximum_bitcast_fusion
  88.6 1.7 %collective-permute-done.6.left = bf16[384,256]{1,0:T(8,128)(2,1)S(1)} collective-permute-done((bf16[384,256]{1,0:T(8,128)(2,1)S(1)}, bf16[384,256]{1,0:T(8,128)(2,1)S(1)}, u32[]{:S(2)}, u32[]{:S(2)}) %collective-permute-start.6) | collective-permute-done | bytes 196640 | tf_op jit(solution)/shard_map/ppermute | solution.py:344
  90.3 0.0 collective-permute-done.7.right
  90.3 1.5 %shard_map.123 = bf16[1024,256]{1,0:T(8,128)(2,1)} custom-call(bf16[1024,256]{1,0:T(8,128)(2,1)S(1)} %get-tuple-element.86.own, bf16[384,256]{1,0:T(8,128)(2,1)S(1)} %collective-permute-done.6.left, bf16[384,256]{1,0:T(8,128)(2,1)S(1)} %collective-permute-done.7.right, bf16[1024,768]{1,0:T(8,128)(2,1)S(1)} %get-tuple-element.89.picks), custom_call_target="tpu_custom_call" | custom-call | tf_op jit(solution)/shard_map/pallas_call | solution.py:329
Async XLA Ops:
  2.4 12.9 %collective-permute-start = (bf16[384,256]{1,0:T(8,128)(2,1)S(1)}, bf16[384,256]{1,0:T(8,128)(2,1)S(1)}, u32[]{:S(2)}, u32[]{:S(2)}) collective-permute-start(bf16[384,256]{1,0:T(8,128)(2,1)S(1)} %get-tuple-element.50), channel_id=1, source_target_pairs={{0,1},{1,2},{2,3},{3,4},{4,5},{5,6},{6,7},{7,8},{8,9},{9,10},{10,1... | collective-permute-start | bytes 589832 | tf_op jit(solution)/shard_map/ppermute | solution.py:344
  4.1 11.2 %collective-permute-start.1 = (bf16[384,256]{1,0:T(8,128)(2,1)S(1)}, bf16[384,256]{1,0:T(8,128)(2,1)S(1)}, u32[]{:S(2)}, u32[]{:S(2)}) collective-permute-start(bf16[384,256]{1,0:T(8,128)(2,1)S(1)} %get-tuple-element.51), channel_id=1, source_target_pairs={{0,127},{1,0},{2,1},{3,2},{4,3},{5,4},{6,5},{7,6},{8,7},{9,8},{10,... | collective-permute-start | bytes 589832 | tf_op jit(solution)/shard_map/ppermute | solution.py:344
  16.0 13.1 %collective-permute-start.2 = (bf16[512,256]{1,0:T(8,128)(2,1)S(1)}, bf16[512,256]{1,0:T(8,128)(2,1)S(1)}, u32[]{:S(2)}, u32[]{:S(2)}) collective-permute-start(bf16[512,256]{1,0:T(8,128)(2,1)S(1)} %get-tuple-element.52), channel_id=1, source_target_pairs={{0,1},{1,2},{2,3},{3,4},{4,5},{5,6},{6,7},{7,8},{8,9},{9,10},{10,1... | collective-permute-start | bytes 786440 | tf_op jit(solution)/shard_map/ppermute | solution.py:344
  22.2 20.4 %collective-permute-start.3 = (bf16[512,256]{1,0:T(8,128)(2,1)S(1)}, bf16[512,256]{1,0:T(8,128)(2,1)S(1)}, u32[]{:S(2)}, u32[]{:S(2)}) collective-permute-start(bf16[512,256]{1,0:T(8,128)(2,1)S(1)} %get-tuple-element.56), channel_id=1, source_target_pairs={{0,1},{1,2},{2,3},{3,4},{4,5},{5,6},{6,7},{7,8},{8,9},{9,10},{10,1... | collective-permute-start | bytes 786440 | tf_op jit(solution)/shard_map/ppermute | solution.py:344
  69.1 10.0 %collective-permute-start.5 = (bf16[512,256]{1,0:T(8,128)(2,1)S(1)}, bf16[512,256]{1,0:T(8,128)(2,1)S(1)}, u32[]{:S(2)}, u32[]{:S(2)}) collective-permute-start(bf16[512,256]{1,0:T(8,128)(2,1)S(1)} %get-tuple-element.84), channel_id=1, source_target_pairs={{0,127},{1,0},{2,1},{3,2},{4,3},{5,4},{6,5},{7,6},{8,7},{9,8},{10,... | collective-permute-start | bytes 786440 | tf_op jit(solution)/shard_map/ppermute | solution.py:344
  70.2 17.6 %collective-permute-start.4 = (bf16[512,256]{1,0:T(8,128)(2,1)S(1)}, bf16[512,256]{1,0:T(8,128)(2,1)S(1)}, u32[]{:S(2)}, u32[]{:S(2)}) collective-permute-start(bf16[512,256]{1,0:T(8,128)(2,1)S(1)} %get-tuple-element.69), channel_id=1, source_target_pairs={{0,127},{1,0},{2,1},{3,2},{4,3},{5,4},{6,5},{7,6},{8,7},{9,8},{10,... | collective-permute-start | bytes 786440 | tf_op jit(solution)/shard_map/ppermute | solution.py:344
  79.7 10.6 %collective-permute-start.6 = (bf16[384,256]{1,0:T(8,128)(2,1)S(1)}, bf16[384,256]{1,0:T(8,128)(2,1)S(1)}, u32[]{:S(2)}, u32[]{:S(2)}) collective-permute-start(bf16[384,256]{1,0:T(8,128)(2,1)S(1)} %get-tuple-element.87), channel_id=1, source_target_pairs={{0,1},{1,2},{2,3},{3,4},{4,5},{5,6},{6,7},{7,8},{8,9},{9,10},{10,1... | collective-permute-start | bytes 589832 | tf_op jit(solution)/shard_map/ppermute | solution.py:344
  80.9 9.4 %collective-permute-start.7 = (bf16[384,256]{1,0:T(8,128)(2,1)S(1)}, bf16[384,256]{1,0:T(8,128)(2,1)S(1)}, u32[]{:S(2)}, u32[]{:S(2)}) collective-permute-start(bf16[384,256]{1,0:T(8,128)(2,1)S(1)} %get-tuple-element.88), channel_id=1, source_target_pairs={{0,127},{1,0},{2,1},{3,2},{4,3},{5,4},{6,5},{7,6},{8,7},{9,8},{10,... | collective-permute-start | bytes 589832 | tf_op jit(solution)/shard_map/ppermute | solution.py:344
